TPU v7x, 128 devices: a whole 4x4x4 slice. The times are simulated.
128 devices in a mesh: tile: 16 (over y, z), intra: 8 (over x, core).
Axes of the slice: x: 4, y: 4, z: 4, core: 2. Of those that a mesh axis runs over, the one named last changes fastest.
Arguments:
- leaves: bfloat16 [65536, 256], P(('tile', 'intra')), may hold values from -6 to 6
- window_a: int32 [65536], P(('tile', 'intra')), may hold values from 0 to 127, as said below
- window_b: int32 [65536], P(('tile', 'intra')), may hold values from 0 to 127, as said below
- parent: int32 [65536], P(('tile', 'intra')), may hold values from 0 to 4095
- coarse: bfloat16 [16, 512, 256, 128], P('tile', 'intra'), may hold values from -6 to 6
- w_query: bfloat16 [2, 256, 256], replicated
- w_key: bfloat16 [2, 256, 256], replicated
- w_value: bfloat16 [2, 256, 256], replicated, may hold values from -0.375 to 0.375
- w_out: bfloat16 [2, 256, 256], replicated, may hold values from -0.375 to 0.375
- w_up: bfloat16 [2, 256, 1024], replicated, may hold values from -0.375 to 0.375
- w_down: bfloat16 [2, 1024, 256], replicated, may hold values from -0.1875 to 0.1875
- gain_attn: float32 [2, 256], replicated, may hold values from 0.25 to 1.75
- gain_mlp: float32 [2, 256], replicated, may hold values from 0.25 to 1.75
- w_expand: bfloat16 [256, 256], replicated, may hold values from -0.375 to 0.375
- w_pixels: bfloat16 [256, 512], replicated, may hold values from -0.375 to 0.375
- conv_weight: bfloat16 [3, 3, 128, 128], replicated, may hold values from -0.3125 to 0.3125
Outputs:
- field: bfloat16 [16, 512, 256, 128], P('tile', 'intra')
Inputs may be any that keep to these rules, and one draw needn't show every extreme that they name: `window_a`: the leaves of one device (each aligned block of 512) name each window at most 8 times, and some window exactly 8 times from every device; every window is named by every device. `window_b`: the leaves of one partition A window name each window of partition B at most 8 times.
All inputs are finite; a program needn't handle non-finite values.
Results may differ from a plain program's by a relative error of at most 0.0045.
Values may be sent and summed in bfloat16 or wider, within the bound.
No kernel may reach another device: no remote copies, remote signals or barrier semaphores. Data moves between devices by JAX's collectives and lax.ppermute only.
A program may use at most 256 MiB of HBM per device.

v0:
```python
import functools
import math

import jax
import jax.numpy as jnp
from jax import lax
from jax.experimental import pallas as pl
from jax.experimental.pallas import tpu as pltpu
from jax.sharding import PartitionSpec as P

HEADS = 4
HEAD_DIM = 64
EPSILON = 1e-06
NEGATIVE = -1e30
LOG2E = math.log2(math.e)
D = 256
LANES = 128
WIDE = D + LANES
DEVICES = 128
CAP = 8
SLOTS = DEVICES * CAP
LEAVES = 512
RET = 16
BACK = DEVICES * RET
TILE = 256
FF = 1024
F32 = jnp.float32
BF16 = jnp.bfloat16
I32 = jnp.int32

VMEM = pl.BlockSpec(memory_space=pltpu.VMEM)


def iota(shape, dim):
    return lax.broadcasted_iota(I32, shape, dim)


def fiota(shape, dim):
    return iota(shape, dim).astype(F32)


def dot(a, b):
    return jnp.dot(a, b, preferred_element_type=F32)


def dot_nt(a, b):
    return lax.dot_general(a, b, (((1,), (1,)), ((), ())), preferred_element_type=F32)


def columns(row, count):
    return jnp.broadcast_to(row, (LANES, count)).T


def onehot_rows(first, rows, targets):
    want = iota((rows, targets.shape[1]), 0) + first
    return jnp.where(want == targets, 1.0, 0.0).astype(BF16)


def send_kernel(leaves_ref, wa_ref, wb_ref, out_ref, ret_ref):
    a_row = wa_ref[...].astype(F32)
    b_row = wb_ref[...].astype(F32)
    a_col = columns(a_row, LEAVES)
    b_col = columns(b_row, LEAVES)
    l_col = fiota((LEAVES, LANES), 0)
    key_col = a_col * LEAVES + l_col
    slots = []
    ranks = []
    for part in range(LEAVES // LANES):
        lanes = slice(part * LANES, (part + 1) * LANES)
        ar = a_row[:, lanes]
        br = b_row[:, lanes]
        lr = fiota((1, LANES), 1) + part * LANES
        same_a = jnp.where(a_col == ar, jnp.where(l_col < lr, 1.0, 0.0), 0.0)
        same_b = jnp.where(b_col == br, jnp.where(key_col < ar * LEAVES + lr, 1.0, 0.0), 0.0)
        slots.append(ar * CAP + jnp.sum(same_a, axis=0, keepdims=True))
        ranks.append(jnp.sum(same_b, axis=0, keepdims=True))
    slot = jnp.concatenate(slots, axis=1).astype(I32)
    rank = jnp.concatenate(ranks, axis=1)
    turn = jnp.floor(rank * (1.0 / RET))
    ret = b_row * RET + (rank - turn * RET) + turn * BACK
    ret_ref[...] = jnp.broadcast_to(ret, (8, LEAVES)).astype(I32)
    rounds = jnp.max(turn) + 1.0
    lane = iota((LEAVES, LANES), 1)
    extra = jnp.where(lane == 0, b_col + 1.0, jnp.where(lane == 1, rounds, 0.0)).astype(BF16)
    for first in range(0, SLOTS, TILE):
        hot = onehot_rows(first, TILE, slot)
        out_ref[first : first + TILE, :D] = dot(hot, leaves_ref[...]).astype(BF16)
        out_ref[first : first + TILE, D:] = dot(hot, extra).astype(BF16)


def tags_of(x_ref):
    tags = x_ref[:, D:]
    picks = jnp.where(iota((8, LANES), 0) == iota((8, LANES), 1), 1.0, 0.0).astype(BF16)
    rows = dot_nt(picks, tags)
    spread = jnp.where(iota((LANES, LANES), 0) == 0, 1.0, 0.0).astype(BF16)
    return rows[0:1, :], dot(tags, spread), jnp.max(rows[1:2, :])


def ranks_of(tag_row, tag_col):
    ranks = []
    for part in range(SLOTS // LANES):
        row = tag_row[:, part * LANES : (part + 1) * LANES]
        block = tag_col[part * LANES : (part + 1) * LANES, :]
        before = iota((LANES, LANES), 0) < iota((LANES, LANES), 1)
        hits = jnp.where(before, jnp.where(block == row, 1.0, 0.0), 0.0)
        rank = jnp.sum(hits, axis=0, keepdims=True)
        if part:
            above = jnp.where(tag_col[: part * LANES, :] == row, 1.0, 0.0)
            rank = rank + jnp.sum(above, axis=0, keepdims=True)
        ranks.append(rank)
    return jnp.concatenate(ranks, axis=1)


def rms(values, gain):
    mean_sq = jnp.mean(values * values, axis=-1, keepdims=True)
    return (values * lax.rsqrt(mean_sq + EPSILON) * gain).astype(BF16)


def layer(layer_index, x_ref, tag_row, weights, y_ref, q_ref, k_ref, v_ref):
    wq, wk, wv, wo, wu, wd, gain_one, gain_two = weights
    one = gain_one[layer_index : layer_index + 1, :]
    two = gain_two[layer_index : layer_index + 1, :]
    head_of = iota((TILE, D), 1) // HEAD_DIM

    def project(step, _):
        rows = pl.ds(pl.multiple_of(step * TILE, TILE), TILE)
        normed = rms(x_ref[rows, :D].astype(F32), one)
        q_ref[rows, :] = dot(normed, wq[0]).astype(BF16) * jnp.asarray(HEAD_DIM**-0.5, BF16)
        k_ref[rows, :] = dot(normed, wk[0]).astype(BF16)
        value = dot(normed, wv[0]).astype(BF16)
        for head in range(HEADS):
            v_ref[head, rows, :] = jnp.where(head_of == head, value, jnp.asarray(1, BF16))
        return 0

    lax.fori_loop(0, SLOTS // TILE, project, 0)
    live = tag_row > 0.0

    def attend(step, _):
        rows = pl.ds(pl.multiple_of(step * TILE, TILE), TILE)
        query = q_ref[rows, :]
        top = jnp.zeros((TILE, D), F32)
        total = jnp.zeros((TILE, D), F32)
        for head in range(HEADS):
            own = jnp.where(head_of == head, query, jnp.asarray(0, BF16))
            scores = dot_nt(own, k_ref[...])
            scores = jnp.where(live, scores, NEGATIVE)
            peak = jnp.max(scores, axis=-1, keepdims=True)
            probs = jnp.exp2((scores - peak) * LOG2E).astype(BF16)
            mixed = dot(probs, v_ref[head])
            top = jnp.where(head_of == head, mixed, top)
            total = jnp.where(head_of == (head + 1) % HEADS, mixed, total)
        total = pltpu.roll(total, D - HEAD_DIM, 1)
        att = (top / total).astype(BF16)
        hidden = x_ref[rows, :D].astype(F32) + dot(att, wo[0])
        up = jax.nn.gelu(dot(rms(hidden, two), wu[0])).astype(BF16)
        y_ref[rows, :] = (hidden + dot(up, wd[0])).astype(BF16)
        return 0

    lax.fori_loop(0, SLOTS // TILE, attend, 0)


def layer_a_kernel(x_ref, *refs):
    weights, (out_ref, y_ref, q_ref, k_ref, v_ref) = refs[:8], refs[8:]
    tag_row, tag_col, rounds = tags_of(x_ref)
    layer(0, x_ref, tag_row, weights, y_ref, q_ref, k_ref, v_ref)
    slot = (tag_row - 1.0) * CAP + ranks_of(tag_row, tag_col)
    slot = jnp.where(tag_row > 0.0, slot, -1.0).astype(I32)
    lane = iota((SLOTS, LANES), 1)
    home = iota((SLOTS, LANES), 0) // CAP + 1
    extra = jnp.where(lane == 0, home.astype(F32), 0.0).astype(BF16)
    for first in range(0, SLOTS, TILE):
        hot = onehot_rows(first, TILE, slot)
        out_ref[first : first + TILE, :D] = dot(hot, y_ref[...]).astype(BF16)
        tail = jnp.where(lane[:TILE] == 1, rounds, dot(hot, extra))
        out_ref[first : first + TILE, D:] = tail.astype(BF16)


def layer_b_kernel(x_ref, *refs):
    weights, (out_ref, y_ref, slot_ref, rounds_ref, q_ref, k_ref, v_ref) = refs[:8], refs[8:]
    tag_row, tag_col, rounds = tags_of(x_ref)
    layer(1, x_ref, tag_row, weights, y_ref, q_ref, k_ref, v_ref)
    rank = ranks_of(tag_row, tag_col)
    turn = jnp.floor(rank * (1.0 / RET))
    slot = (tag_row - 1.0) * RET + (rank - turn * RET) + turn * BACK
    slot = jnp.where(tag_row > 0.0, slot, -1.0).astype(I32)
    slot_ref[...] = jnp.broadcast_to(slot, (8, SLOTS))
    rounds_ref[...] = jnp.full((8, LANES), rounds, F32).astype(I32)
    for first in range(0, BACK, TILE):
        hot = onehot_rows(first, TILE, slot)
        out_ref[first : first + TILE, :] = dot(hot, y_ref[...]).astype(BF16)


def call_layer(kernel, layer_index, out_shape, x, weights):
    own = lambda *shape: pl.BlockSpec((1,) + shape, lambda i: (layer_index, 0, 0))
    whole = lambda *shape: pl.BlockSpec(shape, lambda i: (0,) * len(shape))
    specs = [whole(SLOTS, WIDE)] + [own(D, D)] * 4 + [own(D, FF), own(FF, D), whole(2, D), whole(2, D)]
    scratch = [
        pltpu.VMEM((SLOTS, D), BF16),
        pltpu.VMEM((SLOTS, D), BF16),
        pltpu.VMEM((HEADS, SLOTS, D), BF16),
    ]
    if len(out_shape) == 1:
        scratch = [pltpu.VMEM((SLOTS, D), BF16)] + scratch
    return pl.pallas_call(
        kernel,
        grid=(1,),
        out_shape=out_shape,
        in_specs=specs,
        out_specs=[whole(*shape.shape) for shape in out_shape],
        scratch_shapes=scratch,
        compiler_params=pltpu.CompilerParams(vmem_limit_bytes=40 * 2**20),
        cost_estimate=pl.CostEstimate(flops=6 * 10**9, bytes_accessed=4 * 2**20, transcendentals=5 * 2**20),
    )(x, *weights)


def resend_kernel(turn_ref, y_ref, slot_ref, out_ref):
    slot = slot_ref[0:1, :] - turn_ref[0] * BACK
    for first in range(0, BACK, TILE):
        hot = onehot_rows(first, TILE, slot)
        out_ref[first : first + TILE, :] = dot(hot, y_ref[...]).astype(BF16)


def gathered(want, back_ref):
    parts = []
    for first in range(0, LEAVES, LANES):
        block = want[first : first + LANES, :]
        hot = jnp.concatenate(
            [
                jnp.where(block == iota((LANES, LANES), 1) + lanes, 1.0, 0.0).astype(BF16)
                for lanes in range(0, BACK, LANES)
            ],
            axis=1,
        )
        parts.append(dot(hot, back_ref[...]))
    return jnp.concatenate(parts, axis=0)


def regather_kernel(turn_ref, back_ref, want_ref, held_ref, out_ref):
    rows = gathered(want_ref[...] - turn_ref[0] * BACK, back_ref)
    out_ref[...] = (held_ref[...].astype(F32) + rows).astype(BF16)


def order_kernel(ret_ref, parent_ref, want_ref, pixel_ref, start_ref):
    parent = parent_ref[...].astype(F32)
    ret = ret_ref[0:1, :].astype(F32)
    p_col = columns(parent, LEAVES)
    l_col = fiota((LEAVES, LANES), 0)
    parts = []
    for part in range(LEAVES // LANES):
        pr = parent[:, part * LANES : (part + 1) * LANES]
        lr = fiota((1, LANES), 1) + part * LANES
        less = jnp.where(p_col * LEAVES + l_col < pr * LEAVES + lr, 1.0, 0.0)
        parts.append(jnp.sum(less, axis=0, keepdims=True))
    place = jnp.concatenate(parts, axis=1)
    hit = place == fiota((LEAVES, LEAVES), 0)
    want = jnp.sum(jnp.where(hit, ret, 0.0), axis=1, keepdims=True)
    want_ref[...] = jnp.broadcast_to(want, (LEAVES, LANES)).astype(I32)
    place_col = columns(place, LEAVES)
    rows = []
    for part in range(LEAVES // LANES):
        inside = place_col == fiota((1, LANES), 1) + part * LANES
        moved = 2.0 * jnp.sum(jnp.where(inside, p_col, 0.0), axis=0, keepdims=True)
        rows.append(jnp.concatenate([moved, moved + 1.0], axis=1))
    pixel_ref[...] = jnp.concatenate(rows + rows, axis=0).astype(I32)
    below = jnp.where(p_col < fiota((1, LANES), 1) * LANES, 1.0, 0.0)
    start_ref[...] = jnp.broadcast_to(jnp.sum(below, axis=0, keepdims=True), (8, LANES)).astype(I32)


def call_order(ret, parent):
    return pl.pallas_call(
        order_kernel,
        out_shape=[
            jax.ShapeDtypeStruct((LEAVES, LANES), I32),
            jax.ShapeDtypeStruct((8, TILE), I32),
            jax.ShapeDtypeStruct((8, LANES), I32),
        ],
        in_specs=[VMEM, VMEM],
        out_specs=[VMEM, VMEM, VMEM],
        compiler_params=pltpu.CompilerParams(vmem_limit_bytes=24 * 2**20),
        cost_estimate=pl.CostEstimate(flops=10**9, bytes_accessed=2**20, transcendentals=0),
    )(ret, parent)


STRIP = 8


def conv_kernel(count, main_ref, above_ref, below_ref, head_ref, foot_ref, weight_ref, out_ref, w_ref):
    step = pl.program_id(0)

    @pl.when(step == 0)
    def _():
        zero = jnp.zeros((LANES, LANES), BF16)
        for b in range(3):
            for row in range(4):
                for r in range(2):
                    block = weight_ref[row - r, b] if 0 <= row - r < 3 else zero
                    w_ref[b, row * LANES : (row + 1) * LANES, r * LANES : (r + 1) * LANES] = block

    above = jnp.where(step == 0, head_ref[0, 0], above_ref[0, 0])
    below = jnp.where(step == count - 1, foot_ref[0, 0], below_ref[0, 0])
    rows = [above] + [main_ref[0, r] for r in range(STRIP)] + [below]
    column = iota((TILE, TILE), 0)
    for pair in range(STRIP // 2):
        wide = jnp.concatenate(rows[2 * pair : 2 * pair + 4], axis=1)
        left = pltpu.roll(dot(wide, w_ref[0]), 1, 0)
        right = pltpu.roll(dot(wide, w_ref[2]), TILE - 1, 0)
        both = dot(wide, w_ref[1])
        both = both + jnp.where(column == 0, 0.0, left) + jnp.where(column == TILE - 1, 0.0, right)
        out_ref[0, 2 * pair] = both[:, :LANES].astype(BF16)
        out_ref[0, 2 * pair + 1] = both[:, LANES:].astype(BF16)


def call_conv(coarse, head, foot, weight):
    rows, cols, channels = coarse.shape[1:]
    count = rows // STRIP
    single = (1, 1, cols, channels)
    return pl.pallas_call(
        functools.partial(conv_kernel, count),
        grid=(count,),
        out_shape=jax.ShapeDtypeStruct(coarse.shape, BF16),
        in_specs=[
            pl.BlockSpec((1, STRIP, cols, channels), lambda i: (0, i, 0, 0)),
            pl.BlockSpec(single, lambda i: (0, jnp.maximum(i * STRIP - 1, 0), 0, 0)),
            pl.BlockSpec(single, lambda i: (0, jnp.minimum(i * STRIP + STRIP, rows - 1), 0, 0)),
            pl.BlockSpec(single, lambda i: (0, 0, 0, 0)),
            pl.BlockSpec(single, lambda i: (0, 0, 0, 0)),
            pl.BlockSpec(weight.shape, lambda i: (0, 0, 0, 0)),
        ],
        out_specs=pl.BlockSpec((1, STRIP, cols, channels), lambda i: (0, i, 0, 0)),
        scratch_shapes=[pltpu.VMEM((3, 4 * LANES, 2 * LANES), BF16)],
        compiler_params=pltpu.CompilerParams(vmem_limit_bytes=24 * 2**20),
        cost_estimate=pl.CostEstimate(flops=6 * 10**9, bytes_accessed=8 * 2**20, transcendentals=0),
    )(coarse, coarse, coarse, head, foot, weight)


def field_kernel(start_ref, conv_ref, back_ref, held_ref, want_ref, pixel_ref, we_ref, wp_ref, out_ref, pix_ref, acc_ref):
    step = pl.program_id(0)

    @pl.when(step == 0)
    def _():
        leaf = (gathered(want_ref[...], back_ref) + held_ref[...].astype(F32)).astype(BF16)
        expanded = jax.nn.gelu(dot(leaf, we_ref[...])).astype(BF16)
        pixels = dot(expanded, wp_ref[...]).astype(BF16)
        for part in range(LEAVES // LANES):
            leaves = slice(part * LANES, (part + 1) * LANES)
            for c in range(2):
                for r in range(2):
                    block = pixels[leaves, (2 * r + c) * LANES : (2 * r + c + 1) * LANES]
                    pix_ref[part, c * LANES : (c + 1) * LANES, r * LANES : (r + 1) * LANES] = block

    for pair in range(STRIP // 2):
        index = step * (STRIP // 2) + pair
        acc_ref[:, :LANES] = conv_ref[0, 2 * pair].astype(F32)
        acc_ref[:, LANES:] = conv_ref[0, 2 * pair + 1].astype(F32)

        def add(part, _):
            target = pixel_ref[pl.ds(part, 1), :] - index * TILE
            hot = jnp.where(iota((TILE, TILE), 0) == target, 1.0, 0.0).astype(BF16)
            acc_ref[...] += dot(hot, pix_ref[part])
            return 0

        low = start_ref[index] // LANES
        high = (start_ref[index + 1] + LANES - 1) // LANES
        lax.fori_loop(low, high, add, 0)
        out_ref[0, 2 * pair] = acc_ref[:, :LANES].astype(BF16)
        out_ref[0, 2 * pair + 1] = acc_ref[:, LANES:].astype(BF16)


def call_field(starts, conv, back, held, want, pixel, w_expand, w_pixels):
    rows, cols, channels = conv.shape[1:]
    whole = lambda *shape: pl.BlockSpec(shape, lambda i, s: (0,) * len(shape))
    strip = pl.BlockSpec((1, STRIP, cols, channels), lambda i, s: (0, i, 0, 0))
    return pl.pallas_call(
        field_kernel,
        grid_spec=pltpu.PrefetchScalarGridSpec(
            num_scalar_prefetch=1,
            grid=(rows // STRIP,),
            in_specs=[
                strip,
                whole(BACK, D),
                whole(LEAVES, D),
                whole(LEAVES, LANES),
                whole(8, TILE),
                whole(D, D),
                whole(D, 4 * LANES),
            ],
            out_specs=strip,
            scratch_shapes=[pltpu.VMEM((LEAVES // LANES, TILE, TILE), BF16), pltpu.VMEM((TILE, TILE), F32)],
        ),
        out_shape=jax.ShapeDtypeStruct(conv.shape, BF16),
        compiler_params=pltpu.CompilerParams(vmem_limit_bytes=32 * 2**20),
        cost_estimate=pl.CostEstimate(flops=2 * 10**9, bytes_accessed=10 * 2**20, transcendentals=2**17),
    )(starts, conv, back, held, want, pixel, w_expand, w_pixels)


def exchange(rows, capacity):
    width = rows.shape[1]
    blocks = rows.reshape(DEVICES, capacity, width)
    moved = lax.all_to_all(blocks, ("tile", "intra"), split_axis=0, concat_axis=0, tiled=True)
    return moved.reshape(DEVICES * capacity, width)


def shards(
    leaves,
    window_a,
    window_b,
    parent,
    coarse,
    w_query,
    w_key,
    w_value,
    w_out,
    w_up,
    w_down,
    gain_attn,
    gain_mlp,
    w_expand,
    w_pixels,
    conv_weight,
):
    weights = (w_query, w_key, w_value, w_out, w_up, w_down, gain_attn, gain_mlp)
    count = lax.axis_size("intra")
    rows = coarse.shape[1]
    head = lax.ppermute(coarse[:, rows - 1 :], "intra", [(i, i + 1) for i in range(count - 1)])
    foot = lax.ppermute(coarse[:, :1], "intra", [(i + 1, i) for i in range(count - 1)])
    sent, ret = pl.pallas_call(
        send_kernel,
        out_shape=[jax.ShapeDtypeStruct((SLOTS, WIDE), BF16), jax.ShapeDtypeStruct((8, LEAVES), I32)],
        in_specs=[VMEM] * 3,
        out_specs=[VMEM] * 2,
        compiler_params=pltpu.CompilerParams(vmem_limit_bytes=24 * 2**20),
        cost_estimate=pl.CostEstimate(flops=10**9, bytes_accessed=2**20, transcendentals=0),
    )(leaves, window_a.reshape(1, LEAVES), window_b.reshape(1, LEAVES))
    rows_a = exchange(sent, CAP)
    (sent_b,) = call_layer(
        layer_a_kernel, 0, [jax.ShapeDtypeStruct((SLOTS, WIDE), BF16)], rows_a, weights
    )
    rows_b = exchange(sent_b, CAP)
    home, y, slot, rounds = call_layer(
        layer_b_kernel,
        1,
        [
            jax.ShapeDtypeStruct((BACK, D), BF16),
            jax.ShapeDtypeStruct((SLOTS, D), BF16),
            jax.ShapeDtypeStruct((8, SLOTS), I32),
            jax.ShapeDtypeStruct((8, LANES), I32),
        ],
        rows_b,
        weights,
    )
    back = exchange(home, RET)
    conv = call_conv(coarse, head, foot, conv_weight)
    want, pixel, starts = call_order(ret, parent.reshape(1, LEAVES))
    total = rounds[0, 0]

    def more(state):
        return state[0] < total

    def again(state):
        turn, held = state
        index = turn.reshape(1)
        smem = pl.BlockSpec(memory_space=pltpu.SMEM)
        part = pl.pallas_call(
            resend_kernel,
            out_shape=jax.ShapeDtypeStruct((BACK, D), BF16),
            in_specs=[smem, VMEM, VMEM],
            out_specs=VMEM,
        )(index, y, slot)
        held = pl.pallas_call(
            regather_kernel,
            out_shape=jax.ShapeDtypeStruct((LEAVES, D), BF16),
            in_specs=[smem, VMEM, VMEM, VMEM],
            out_specs=VMEM,
        )(index, exchange(part, RET), want, held)
        return turn + 1, held

    _, held = lax.while_loop(more, again, (jnp.asarray(1, I32), jnp.zeros((LEAVES, D), BF16)))
    return call_field(starts[0], conv, back, held, want, pixel, w_expand, w_pixels)


def solution(mesh):
    placed = (
        P(("tile", "intra"), None),
        P(("tile", "intra")),
        P(("tile", "intra")),
        P(("tile", "intra")),
        P("tile", "intra", None, None),
    ) + (P(),) * 11
    return jax.shard_map(
        shards,
        mesh=mesh,
        in_specs=placed,
        out_specs=P("tile", "intra", None, None),
        check_vma=False,
    )
```

profile of v0, /device:TPU:1, one launch (start us, length us, event | category | flops | bytes accessed | tf_op | source)
XLA Modules:
  0.0 131.0 jit_solution(17754094051785843129)
XLA Ops:
  0.0 1.1 copy-done.8
  1.1 0.7 copy-done.15
  1.8 0.7 copy-done.16
  2.5 1.3 %shard_map.154 = (bf16[1024,384]{1,0:T(8,128)(2,1)S(1)}, s32[8,512]{1,0:T(8,128)S(1)}) custom-call(bf16[512,256]{1,0:T(8,128)(2,1)S(1)} %copy-done.8, s32[1,512]{1,0:T(1,128)S(1)} %bitcast.25, s32[1,512]{1,0:T(1,128)S(1)} %bitcast.26), custom_call_target="tpu_custom_call" | custom-call | flops 1000000000 | bytes 1048576 | tf_op jit(solution)/shard_map/pallas_call | solution.py:426
  3.8 27.7 %all_to_all.21 = bf16[128,8,384]{2,1,0:T(8,128)(2,1)S(1)} all-to-all(bf16[128,8,384]{2,1,0:T(8,128)(2,1)S(1)} %bitcast.23), channel_id=1, replica_groups=mesh['tile'=16,'intra'=8] {'tile','intra'}, dimensions={0} | all-to-all | bytes 1572864 | tf_op jit(solution)/shard_map/all_to_all | solution.py:399
  31.6 15.9 %shard_map.157 = bf16[1024,384]{1,0:T(8,128)(2,1)} custom-call(bf16[1024,384]{1,0:T(8,128)(2,1)S(1)} %bitcast.24, bf16[2,256,256]{2,1,0:T(8,128)(2,1)S(1)} %copy-done.9, bf16[2,256,256]{2,1,0:T(8,128)(2,1)S(1)} %copy-done.10, bf16[2,256,256]{2,1,0:T(8,128)(2,1)S(1)} %copy-done.11, bf16[2,256,256]{2,1,0:T(8,128)(2,1)S(1)} %copy-done.13, ...), custom_call_target="tpu_custom_call" | custom-call | flops 6000000000 | bytes 4194304 | tf_op jit(solution)/shard_map/pallas_call | solution.py:204
  47.5 4.5 %all-to-all-start.2 = ((bf16[128,8,384]{2,1,0:T(8,128)(2,1)}), bf16[128,8,384]{2,1,0:T(8,128)(2,1)S(1)}, u32[]{:S(2)}, u32[]{:S(2)}) async-start(bf16[128,8,384]{2,1,0:T(8,128)(2,1)} %bitcast.9), calls=%async_computation.2 | async-start | bytes 1572864 | tf_op jit(solution)/shard_map/all_to_all | solution.py:399
  52.0 1.3 shard_map.155
  53.3 15.1 %all-to-all-done.2 = bf16[128,8,384]{2,1,0:T(8,128)(2,1)S(1)} async-done(((bf16[128,8,384]{2,1,0:T(8,128)(2,1)}), bf16[128,8,384]{2,1,0:T(8,128)(2,1)S(1)}, u32[]{:S(2)}, u32[]{:S(2)}) %all-to-all-start.2) | async-done | bytes 786464 | tf_op jit(solution)/shard_map/all_to_all | solution.py:399
  68.4 0.9 copy-done.12
  69.4 0.9 copy-done.14
  70.3 16.0 %shard_map.158 = (bf16[2048,256]{1,0:T(8,128)(2,1)}, bf16[1024,256]{1,0:T(8,128)(2,1)}, s32[8,1024]{1,0:T(8,128)S(1)}, s32[8,128]{1,0:T(8,128)S(1)}) custom-call(bf16[1024,384]{1,0:T(8,128)(2,1)S(1)} %bitcast.22, bf16[2,256,256]{2,1,0:T(8,128)(2,1)S(1)} %copy-done.9, bf16[2,256,256]{2,1,0:T(8,128)(2,1)S(1)} %copy-done.10, ...), custom_call_target="tpu_custom_call" | custom-call | flops 6000000000 | bytes 4194304 | tf_op jit(solution)/shard_map/pallas_call | solution.py:204
  86.3 0.6 slice.15
  86.9 0.7 while.10
  87.7 4.5 %all-to-all-start.3 = ((bf16[128,16,256]{2,1,0:T(8,128)(2,1)}), bf16[128,16,256]{2,1,0:T(8,128)(2,1)S(1)}, u32[]{:S(2)}, u32[]{:S(2)}) async-start(bf16[128,16,256]{2,1,0:T(8,128)(2,1)} %bitcast.11), calls=%async_computation.3 | async-start | bytes 2097152 | tf_op jit(solution)/shard_map/all_to_all | solution.py:399
  92.2 0.9 fusion
  93.1 3.0 %collective-permute-start.1 = (bf16[1,1,256,128]{3,2,1,0:T(8,128)(2,1)S(1)}, bf16[1,1,256,128]{3,2,1,0:T(8,128)(2,1)S(1)}, u32[]{:S(2)}, u32[]{:S(2)}) collective-permute-start(bf16[1,1,256,128]{3,2,1,0:T(8,128)(2,1)S(1)} %get-tuple-element.69), channel_id=1, source_target_pairs={{1,0},{2,1},{3,2},{4,3},{5,4},{6,5},{7,6},{9,8},{10,9},{11,10},{12... | collective-permute-start | bytes 196616 | tf_op jit(solution)/shard_map/ppermute | solution.py:425
  96.1 2.6 %collective-permute-start = (bf16[1,1,256,128]{3,2,1,0:T(8,128)(2,1)S(1)}, bf16[1,1,256,128]{3,2,1,0:T(8,128)(2,1)S(1)}, u32[]{:S(2)}, u32[]{:S(2)}) collective-permute-start(bf16[1,1,256,128]{3,2,1,0:T(8,128)(2,1)S(1)} %get-tuple-element.70), channel_id=1, source_target_pairs={{0,1},{1,2},{2,3},{3,4},{4,5},{5,6},{6,7},{8,9},{9,10},{10,11},{11... | collective-permute-start | bytes 196616 | tf_op jit(solution)/shard_map/ppermute | solution.py:424
  98.7 7.4 %collective-permute-done.1.foot_ref = bf16[1,1,256,128]{3,2,1,0:T(8,128)(2,1)S(1)} collective-permute-done((bf16[1,1,256,128]{3,2,1,0:T(8,128)(2,1)S(1)}, bf16[1,1,256,128]{3,2,1,0:T(8,128)(2,1)S(1)}, u32[]{:S(2)}, u32[]{:S(2)}) %collective-permute-start.1) | collective-permute-done | bytes 65568 | tf_op jit(solution)/shard_map/ppermute | solution.py:425
  106.1 2.2 %copy-done.4 = bf16[1,64,256,128]{3,2,1,0:T(8,128)(2,1)S(1)} copy-done((bf16[1,64,256,128]{3,2,1,0:T(8,128)(2,1)S(1)}, bf16[1,64,256,128]{3,2,1,0:T(8,128)(2,1)}, u32[]{:S(2)}) %copy-start.4) | copy-done | bytes 4194328
  108.3 8.1 %shard_map.156.conv_ref = bf16[1,64,256,128]{3,2,1,0:T(8,128)(2,1)S(1)} custom-call(bf16[1,64,256,128]{3,2,1,0:T(8,128)(2,1)S(1)} %copy-done.4, bf16[1,64,256,128]{3,2,1,0:T(8,128)(2,1)S(1)} %copy-done.4, bf16[1,64,256,128]{3,2,1,0:T(8,128)(2,1)S(1)} %copy-done.4, bf16[1,1,256,128]{3,2,1,0:T(8,128)(2,1)S(1)} %collective-permute-done.head_ref, ...), custom_call_target="tpu_custom_call" | custom-call | flops 6000000000 | bytes 8388608 | tf_op jit(solution)/shard_map/pallas_call | solution.py:317
  116.4 2.0 %copy-done = bf16[1,64,256,128]{3,2,1,0:T(8,128)(2,1)} copy-done((bf16[1,64,256,128]{3,2,1,0:T(8,128)(2,1)}, bf16[1,64,256,128]{3,2,1,0:T(8,128)(2,1)S(1)}, u32[]{:S(2)}) %copy-start) | copy-done | bytes 4194328
  118.5 2.2 %copy-done.1 = bf16[1,64,256,128]{3,2,1,0:T(8,128)(2,1)S(1)} copy-done((bf16[1,64,256,128]{3,2,1,0:T(8,128)(2,1)S(1)}, bf16[1,64,256,128]{3,2,1,0:T(8,128)(2,1)}, u32[]{:S(2)}) %copy-start.1) | copy-done | bytes 4194328
  120.6 10.3 %shard_map.159 = bf16[1,64,256,128]{3,2,1,0:T(8,128)(2,1)} custom-call(s32[128]{0:T(128)S(1)} %slice_bitcast_fusion.start_ref, bf16[1,64,256,128]{3,2,1,0:T(8,128)(2,1)S(1)} %copy-done.1, bf16[2048,256]{1,0:T(8,128)(2,1)S(1)} %bitcast.21, bf16[512,256]{1,0:T(8,128)(2,1)S(1)} %get-tuple-element.55.held_ref, s32[512,128]{1,0:T(8,128)S(1)} %copy-done.22, ...), custom_call_target="tpu_custom_call" | custom-call | flops 2000000000 | bytes 10485760 | tf_op jit(solution)/shard_map/pallas_call | solution.py:373
  (38 shorter events, 0.1 us)
Async XLA Ops:
  0.0 31.5 %copy-start.6 = (bf16[2,1024,256]{2,1,0:T(8,128)(2,1)S(1)}, bf16[2,1024,256]{2,1,0:T(8,128)(2,1)}, u32[]{:S(2)}) copy-start(bf16[2,1024,256]{2,1,0:T(8,128)(2,1)} %refs_5_.3) | copy-start | bytes 3145732
  0.0 31.5 %copy-start.5 = (bf16[2,256,1024]{2,1,0:T(8,128)(2,1)S(1)}, bf16[2,256,1024]{2,1,0:T(8,128)(2,1)}, u32[]{:S(2)}) copy-start(bf16[2,256,1024]{2,1,0:T(8,128)(2,1)} %refs_4_.3) | copy-start | bytes 3145732
  0.0 1.1 copy-start.8
  1.1 0.7 copy-start.15
  2.5 29.1 %copy-start.9 = (bf16[2,256,256]{2,1,0:T(8,128)(2,1)S(1)}, bf16[2,256,256]{2,1,0:T(8,128)(2,1)}, u32[]{:S(2)}) copy-start(bf16[2,256,256]{2,1,0:T(8,128)(2,1)} %refs_0_.3) | copy-start | bytes 786436
  2.5 29.1 %copy-start.10 = (bf16[2,256,256]{2,1,0:T(8,128)(2,1)S(1)}, bf16[2,256,256]{2,1,0:T(8,128)(2,1)}, u32[]{:S(2)}) copy-start(bf16[2,256,256]{2,1,0:T(8,128)(2,1)} %refs_1_.3) | copy-start | bytes 786436
  2.5 29.1 %copy-start.11 = (bf16[2,256,256]{2,1,0:T(8,128)(2,1)S(1)}, bf16[2,256,256]{2,1,0:T(8,128)(2,1)}, u32[]{:S(2)}) copy-start(bf16[2,256,256]{2,1,0:T(8,128)(2,1)} %refs_2_.3) | copy-start | bytes 786436
  2.5 29.1 %copy-start.13 = (bf16[2,256,256]{2,1,0:T(8,128)(2,1)S(1)}, bf16[2,256,256]{2,1,0:T(8,128)(2,1)}, u32[]{:S(2)}) copy-start(bf16[2,256,256]{2,1,0:T(8,128)(2,1)} %refs_3_.3) | copy-start | bytes 786436
  2.5 29.1 %copy-start.18 = (f32[2,256]{1,0:T(2,128)S(1)}, f32[2,256]{1,0:T(2,128)}, u32[]{:S(2)}) copy-start(f32[2,256]{1,0:T(2,128)} %refs_6_.3) | copy-start | bytes 6148
  2.5 29.1 %copy-start.19 = (f32[2,256]{1,0:T(2,128)S(1)}, f32[2,256]{1,0:T(2,128)}, u32[]{:S(2)}) copy-start(f32[2,256]{1,0:T(2,128)} %refs_7_.3) | copy-start | bytes 6148
  31.6 20.4 %copy-start.17 = (s32[512]{0:T(512)S(1)}, s32[512]{0:T(512)}, u32[]{:S(2)}) copy-start(s32[512]{0:T(512)} %param.21) | copy-start | bytes 6148
  47.5 20.9 %all-to-all-start.2 = ((bf16[128,8,384]{2,1,0:T(8,128)(2,1)}), bf16[128,8,384]{2,1,0:T(8,128)(2,1)S(1)}, u32[]{:S(2)}, u32[]{:S(2)}) async-start(bf16[128,8,384]{2,1,0:T(8,128)(2,1)} %bitcast.9), calls=%async_computation.2 | async-start | bytes 1572864 | tf_op jit(solution)/shard_map/all_to_all | solution.py:399
  68.4 1.0 copy-start.12
  69.4 0.9 copy-start.14
  86.9 19.2 %copy-start.7 = (bf16[3,3,128,128]{3,2,1,0:T(8,128)(2,1)S(1)}, bf16[3,3,128,128]{3,2,1,0:T(8,128)(2,1)}, u32[]{:S(2)}) copy-start(bf16[3,3,128,128]{3,2,1,0:T(8,128)(2,1)} %weight_ref.1) | copy-start | bytes 884740
  87.7 30.8 %all-to-all-start.3 = ((bf16[128,16,256]{2,1,0:T(8,128)(2,1)}), bf16[128,16,256]{2,1,0:T(8,128)(2,1)S(1)}, u32[]{:S(2)}, u32[]{:S(2)}) async-start(bf16[128,16,256]{2,1,0:T(8,128)(2,1)} %bitcast.11), calls=%async_computation.3 | async-start | bytes 2097152 | tf_op jit(solution)/shard_map/all_to_all | solution.py:399
  93.1 13.0 %collective-permute-start.1 = (bf16[1,1,256,128]{3,2,1,0:T(8,128)(2,1)S(1)}, bf16[1,1,256,128]{3,2,1,0:T(8,128)(2,1)S(1)}, u32[]{:S(2)}, u32[]{:S(2)}) collective-permute-start(bf16[1,1,256,128]{3,2,1,0:T(8,128)(2,1)S(1)} %get-tuple-element.69), channel_id=1, source_target_pairs={{1,0},{2,1},{3,2},{4,3},{5,4},{6,5},{7,6},{9,8},{10,9},{11,10},{12... | collective-permute-start | bytes 196616 | tf_op jit(solution)/shard_map/ppermute | solution.py:425
  96.1 10.0 %collective-permute-start = (bf16[1,1,256,128]{3,2,1,0:T(8,128)(2,1)S(1)}, bf16[1,1,256,128]{3,2,1,0:T(8,128)(2,1)S(1)}, u32[]{:S(2)}, u32[]{:S(2)}) collective-permute-start(bf16[1,1,256,128]{3,2,1,0:T(8,128)(2,1)S(1)} %get-tuple-element.70), channel_id=1, source_target_pairs={{0,1},{1,2},{2,3},{3,4},{4,5},{5,6},{6,7},{8,9},{9,10},{10,11},{11... | collective-permute-start | bytes 196616 | tf_op jit(solution)/shard_map/ppermute | solution.py:424
  98.7 19.8 %copy-start.2 = (bf16[256,512]{1,0:T(8,128)(2,1)S(1)}, bf16[256,512]{1,0:T(8,128)(2,1)}, u32[]{:S(2)}) copy-start(bf16[256,512]{1,0:T(8,128)(2,1)} %wp_ref.1) | copy-start | bytes 786436
  98.7 19.8 %copy-start.3 = (bf16[256,256]{1,0:T(8,128)(2,1)S(1)}, bf16[256,256]{1,0:T(8,128)(2,1)}, u32[]{:S(2)}) copy-start(bf16[256,256]{1,0:T(8,128)(2,1)} %we_ref.1) | copy-start | bytes 393220
  106.1 2.2 %copy-start.4 = (bf16[1,64,256,128]{3,2,1,0:T(8,128)(2,1)S(1)}, bf16[1,64,256,128]{3,2,1,0:T(8,128)(2,1)}, u32[]{:S(2)}) copy-start(bf16[1,64,256,128]{3,2,1,0:T(8,128)(2,1)} %below_ref.1) | copy-start | bytes 12582916
  108.3 10.2 %copy-start.22 = (s32[512,128]{1,0:T(8,128)S(1)}, s32[512,128]{1,0:T(8,128)}, u32[]{:S(2)}) copy-start(s32[512,128]{1,0:T(8,128)} %get-tuple-element.137) | copy-start | bytes 786436
  116.4 2.0 %copy-start = (bf16[1,64,256,128]{3,2,1,0:T(8,128)(2,1)}, bf16[1,64,256,128]{3,2,1,0:T(8,128)(2,1)S(1)}, u32[]{:S(2)}) copy-start(bf16[1,64,256,128]{3,2,1,0:T(8,128)(2,1)S(1)} %shard_map.156.conv_ref) | copy-start | bytes 12582916
  118.5 2.2 %copy-start.1 = (bf16[1,64,256,128]{3,2,1,0:T(8,128)(2,1)S(1)}, bf16[1,64,256,128]{3,2,1,0:T(8,128)(2,1)}, u32[]{:S(2)}) copy-start(bf16[1,64,256,128]{3,2,1,0:T(8,128)(2,1)} %copy-done) | copy-start | bytes 12582916
  (1 other events, 0.7 us)
where the time goes:
time: 131 us
  Pallas kernels  52.9 us (40%)
  blocking collectives  27.7 us (21%)
  waiting for transfers between devices  22.5 us (17%)
  starting transfers between devices  14.6 us (11%)
  local copies, waits for them, and re-layouts  12.3 us (9%)
    pallas_call x2, Pallas kernels, call_layer(): pl.pallas_call(kernel, grid=(1,), out_shape=out_shape, in_specs=specs, ou...  31.8 us
    all_to_all x1, blocking collectives, exchange(): lax.all_to_all(blocks, ('tile', 'intra'), split_axis=0, concat_axis=0, ti...  27.7 us
    all_to_all x2, waiting for transfers between devices, exchange(): lax.all_to_all(blocks, ('tile', 'intra'), split_axis=0, concat_axis=0, ti...  15.1 us
    unnamed x42, local copies, waits for them, and re-layouts  10.8 us
    pallas_call x1, Pallas kernels, call_field(): pl.pallas_call(field_kernel, grid_spec=pltpu.PrefetchScalarGridSpec(num_s...  10.3 us
    all_to_all x2, starting transfers between devices, exchange(): lax.all_to_all(blocks, ('tile', 'intra'), split_axis=0, concat_axis=0, ti...  9.06 us
    pallas_call x1, Pallas kernels, call_conv(): pl.pallas_call(functools.partial(conv_kernel, count), grid=(count,), out_...  8.14 us
    ppermute x1, waiting for transfers between devices, shards(): lax.ppermute(coarse[:, :1], 'intra', [(i + 1, i) for i in range(count - 1)])  7.37 us
  transfers between devices with their start and end apart: 4, of which 2 were waited for; matrix products, arithmetic and copies ran while one was open for 1% of the time, Pallas kernels for 7%

commit v1 on v0

--- a/solution.py
+++ b/solution.py
@@ -22,6 +22,9 @@
 LEAVES = 512
 RET = 16
 BACK = DEVICES * RET
+FEW = 640
+GROUP = 64
+ALIGN = 16
 TILE = 256
 FF = 1024
 F32 = jnp.float32
@@ -31,6 +34,10 @@
 VMEM = pl.BlockSpec(memory_space=pltpu.VMEM)
 
 
+def kept(array):
+    return pltpu.with_memory_space_constraint(array, pltpu.HBM)
+
+
 def iota(shape, dim):
     return lax.broadcasted_iota(I32, shape, dim)
 
@@ -56,7 +63,15 @@
     return jnp.where(want == targets, 1.0, 0.0).astype(BF16)
 
 
-def send_kernel(leaves_ref, wa_ref, wb_ref, out_ref, ret_ref):
+def send_kernel(leaves_hbm, wa_hbm, wb_hbm, out_ref, ret_ref, leaves_ref, wa_ref, wb_ref, sems):
+    moves = [
+        pltpu.make_async_copy(source, target, sems.at[index])
+        for index, (source, target) in enumerate(((wa_hbm, wa_ref), (wb_hbm, wb_ref), (leaves_hbm, leaves_ref)))
+    ]
+    for move in moves:
+        move.start()
+    moves[0].wait()
+    moves[1].wait()
     a_row = wa_ref[...].astype(F32)
     b_row = wb_ref[...].astype(F32)
     a_col = columns(a_row, LEAVES)
@@ -82,6 +97,7 @@
     rounds = jnp.max(turn) + 1.0
     lane = iota((LEAVES, LANES), 1)
     extra = jnp.where(lane == 0, b_col + 1.0, jnp.where(lane == 1, rounds, 0.0)).astype(BF16)
+    moves[2].wait()
     for first in range(0, SLOTS, TILE):
         hot = onehot_rows(first, TILE, slot)
         out_ref[first : first + TILE, :D] = dot(hot, leaves_ref[...]).astype(BF16)
@@ -98,7 +114,7 @@
 
 def ranks_of(tag_row, tag_col):
     ranks = []
-    for part in range(SLOTS // LANES):
+    for part in range(tag_row.shape[1] // LANES):
         row = tag_row[:, part * LANES : (part + 1) * LANES]
         block = tag_col[part * LANES : (part + 1) * LANES, :]
         before = iota((LANES, LANES), 0) < iota((LANES, LANES), 1)
@@ -116,58 +132,70 @@
     return (values * lax.rsqrt(mean_sq + EPSILON) * gain).astype(BF16)
 
 
-def layer(layer_index, x_ref, tag_row, weights, y_ref, q_ref, k_ref, v_ref):
+def fetch(layer_index, sources, targets, sems):
+    moves = []
+    for index, (source, target) in enumerate(zip(sources, targets)):
+        part = source if index >= 6 else source.at[layer_index]
+        moves.append(pltpu.make_async_copy(part, target, sems.at[index]))
+        moves[-1].start()
+    return moves
+
+
+def layer(layer_index, count, tile, x_ref, tag_row, weights, y_ref, q_ref, k_ref, v_ref):
     wq, wk, wv, wo, wu, wd, gain_one, gain_two = weights
     one = gain_one[layer_index : layer_index + 1, :]
     two = gain_two[layer_index : layer_index + 1, :]
-    head_of = iota((TILE, D), 1) // HEAD_DIM
+    head_of = iota((tile, D), 1) // HEAD_DIM
 
     def project(step, _):
-        rows = pl.ds(pl.multiple_of(step * TILE, TILE), TILE)
+        rows = pl.ds(pl.multiple_of(step * tile, tile), tile)
         normed = rms(x_ref[rows, :D].astype(F32), one)
-        q_ref[rows, :] = dot(normed, wq[0]).astype(BF16) * jnp.asarray(HEAD_DIM**-0.5, BF16)
-        k_ref[rows, :] = dot(normed, wk[0]).astype(BF16)
-        value = dot(normed, wv[0]).astype(BF16)
+        q_ref[rows, :] = dot(normed, wq[...]).astype(BF16) * jnp.asarray(HEAD_DIM**-0.5, BF16)
+        k_ref[rows, :] = dot(normed, wk[...]).astype(BF16)
+        value = dot(normed, wv[...]).astype(BF16)
         for head in range(HEADS):
             v_ref[head, rows, :] = jnp.where(head_of == head, value, jnp.asarray(1, BF16))
         return 0
 
-    lax.fori_loop(0, SLOTS // TILE, project, 0)
+    lax.fori_loop(0, count // tile, project, 0)
     live = tag_row > 0.0
 
     def attend(step, _):
-        rows = pl.ds(pl.multiple_of(step * TILE, TILE), TILE)
+        rows = pl.ds(pl.multiple_of(step * tile, tile), tile)
         query = q_ref[rows, :]
-        top = jnp.zeros((TILE, D), F32)
-        total = jnp.zeros((TILE, D), F32)
+        top = jnp.zeros((tile, D), F32)
+        total = jnp.zeros((tile, D), F32)
         for head in range(HEADS):
             own = jnp.where(head_of == head, query, jnp.asarray(0, BF16))
-            scores = dot_nt(own, k_ref[...])
+            scores = dot_nt(own, k_ref[:count, :])
             scores = jnp.where(live, scores, NEGATIVE)
             peak = jnp.max(scores, axis=-1, keepdims=True)
             probs = jnp.exp2((scores - peak) * LOG2E).astype(BF16)
-            mixed = dot(probs, v_ref[head])
+            mixed = dot(probs, v_ref[head, :count, :])
             top = jnp.where(head_of == head, mixed, top)
             total = jnp.where(head_of == (head + 1) % HEADS, mixed, total)
         total = pltpu.roll(total, D - HEAD_DIM, 1)
         att = (top / total).astype(BF16)
-        hidden = x_ref[rows, :D].astype(F32) + dot(att, wo[0])
-        up = jax.nn.gelu(dot(rms(hidden, two), wu[0])).astype(BF16)
-        y_ref[rows, :] = (hidden + dot(up, wd[0])).astype(BF16)
+        hidden = x_ref[rows, :D].astype(F32) + dot(att, wo[...])
+        up = jax.nn.gelu(dot(rms(hidden, two), wu[...])).astype(BF16)
+        y_ref[rows, :] = (hidden + dot(up, wd[...])).astype(BF16)
         return 0
 
-    lax.fori_loop(0, SLOTS // TILE, attend, 0)
+    lax.fori_loop(0, count // tile, attend, 0)
 
 
 def layer_a_kernel(x_ref, *refs):
-    weights, (out_ref, y_ref, q_ref, k_ref, v_ref) = refs[:8], refs[8:]
+    sources, out_ref, weights, sems, (y_ref, q_ref, k_ref, v_ref) = refs[:8], refs[8], refs[9:17], refs[17], refs[18:]
+    moves = fetch(0, sources, weights, sems)
     tag_row, tag_col, rounds = tags_of(x_ref)
-    layer(0, x_ref, tag_row, weights, y_ref, q_ref, k_ref, v_ref)
     slot = (tag_row - 1.0) * CAP + ranks_of(tag_row, tag_col)
     slot = jnp.where(tag_row > 0.0, slot, -1.0).astype(I32)
     lane = iota((SLOTS, LANES), 1)
     home = iota((SLOTS, LANES), 0) // CAP + 1
     extra = jnp.where(lane == 0, home.astype(F32), 0.0).astype(BF16)
+    for move in moves:
+        move.wait()
+    layer(0, SLOTS, TILE, x_ref, tag_row, weights, y_ref, q_ref, k_ref, v_ref)
     for first in range(0, SLOTS, TILE):
         hot = onehot_rows(first, TILE, slot)
         out_ref[first : first + TILE, :D] = dot(hot, y_ref[...]).astype(BF16)
@@ -175,25 +203,65 @@
         out_ref[first : first + TILE, D:] = tail.astype(BF16)
 
 
-def layer_b_kernel(x_ref, *refs):
-    weights, (out_ref, y_ref, slot_ref, rounds_ref, q_ref, k_ref, v_ref) = refs[:8], refs[8:]
-    tag_row, tag_col, rounds = tags_of(x_ref)
-    layer(1, x_ref, tag_row, weights, y_ref, q_ref, k_ref, v_ref)
+def finish_b(count, tile, x_ref, tag_row, tag_col, weights, refs):
+    out_ref, y_ref, slot_ref, q_ref, k_ref, v_ref = refs
+    layer(1, count, tile, x_ref, tag_row, weights, y_ref, q_ref, k_ref, v_ref)
     rank = ranks_of(tag_row, tag_col)
     turn = jnp.floor(rank * (1.0 / RET))
     slot = (tag_row - 1.0) * RET + (rank - turn * RET) + turn * BACK
     slot = jnp.where(tag_row > 0.0, slot, -1.0).astype(I32)
-    slot_ref[...] = jnp.broadcast_to(slot, (8, SLOTS))
-    rounds_ref[...] = jnp.full((8, LANES), rounds, F32).astype(I32)
+    slot_ref[:, :count] = jnp.broadcast_to(slot, (8, count))
     for first in range(0, BACK, TILE):
         hot = onehot_rows(first, TILE, slot)
-        out_ref[first : first + TILE, :] = dot(hot, y_ref[...]).astype(BF16)
-
-
-def call_layer(kernel, layer_index, out_shape, x, weights):
-    own = lambda *shape: pl.BlockSpec((1,) + shape, lambda i: (layer_index, 0, 0))
-    whole = lambda *shape: pl.BlockSpec(shape, lambda i: (0,) * len(shape))
-    specs = [whole(SLOTS, WIDE)] + [own(D, D)] * 4 + [own(D, FF), own(FF, D), whole(2, D), whole(2, D)]
+        out_ref[first : first + TILE, :] = dot(hot, y_ref[:count, :]).astype(BF16)
+
+
+def before(flags):
+    parts = flags.shape[1] // LANES
+    square = jnp.concatenate([flags[:, p * LANES : (p + 1) * LANES] for p in range(parts)], axis=0)
+    upper = jnp.where(iota((LANES, LANES), 0) < iota((LANES, LANES), 1), 1.0, 0.0).astype(BF16)
+    inner = dot(square.astype(BF16), upper)
+    held = jnp.zeros((1, 1), F32)
+    rows = []
+    for p in range(parts):
+        rows.append(inner[p : p + 1, :] + held)
+        held = held + jnp.sum(square[p : p + 1, :], axis=1, keepdims=True)
+    return jnp.concatenate(rows, axis=1)
+
+
+def layer_b_kernel(x_ref, *refs):
+    sources, (out_ref, y_ref, slot_ref, rounds_ref) = refs[:8], refs[8:12]
+    weights, sems, (q_ref, k_ref, v_ref, packed_ref) = refs[12:20], refs[20], refs[21:]
+    moves = fetch(1, sources, weights, sems)
+    tag_row, tag_col, rounds = tags_of(x_ref)
+    rounds_ref[0] = rounds.astype(I32)
+    rest = (out_ref, y_ref, slot_ref, q_ref, k_ref, v_ref)
+    live = jnp.where(tag_row > 0.0, 1.0, 0.0)
+    total = jnp.sum(live)
+
+    @pl.when(total <= FEW)
+    def _():
+        place = jnp.where(tag_row > 0.0, before(live), -1.0).astype(I32)
+        for first in range(0, FEW, LANES):
+            hot = onehot_rows(first, LANES, place)
+            packed_ref[first : first + LANES, :] = dot(hot, x_ref[...]).astype(BF16)
+        few_row, few_col, _ = tags_of(packed_ref)
+        slot_ref[:, FEW:] = jnp.full((8, SLOTS - FEW), -1, I32)
+        y_ref[FEW:, :] = jnp.zeros((SLOTS - FEW, D), BF16)
+        for move in moves:
+            move.wait()
+        finish_b(FEW, FEW // 2, packed_ref, few_row, few_col, weights, rest)
+
+    @pl.when(total > FEW)
+    def _():
+        for move in moves:
+            move.wait()
+        finish_b(SLOTS, TILE, x_ref, tag_row, tag_col, weights, rest)
+
+
+def call_layer(kernel, out_shape, x, weights):
+    kernel_weights = [pltpu.VMEM(weight.shape[1:], BF16) for weight in weights[:6]]
+    kernel_weights += [pltpu.VMEM(gain.shape, F32) for gain in weights[6:]]
     scratch = [
         pltpu.VMEM((SLOTS, D), BF16),
         pltpu.VMEM((SLOTS, D), BF16),
@@ -201,16 +269,17 @@
     ]
     if len(out_shape) == 1:
         scratch = [pltpu.VMEM((SLOTS, D), BF16)] + scratch
+    else:
+        scratch = scratch + [pltpu.VMEM((FEW, WIDE), BF16)]
     return pl.pallas_call(
         kernel,
-        grid=(1,),
         out_shape=out_shape,
-        in_specs=specs,
-        out_specs=[whole(*shape.shape) for shape in out_shape],
-        scratch_shapes=scratch,
-        compiler_params=pltpu.CompilerParams(vmem_limit_bytes=40 * 2**20),
+        in_specs=[VMEM] + [pl.BlockSpec(memory_space=pltpu.HBM)] * 8,
+        out_specs=[pl.BlockSpec(memory_space=pltpu.SMEM if shape.shape == (1,) else pltpu.VMEM) for shape in out_shape],
+        scratch_shapes=kernel_weights + [pltpu.SemaphoreType.DMA((8,))] + scratch,
+        compiler_params=pltpu.CompilerParams(vmem_limit_bytes=24 * 2**20),
         cost_estimate=pl.CostEstimate(flops=6 * 10**9, bytes_accessed=4 * 2**20, transcendentals=5 * 2**20),
-    )(x, *weights)
+    )(x, *map(kept, weights))
 
 
 def resend_kernel(turn_ref, y_ref, slot_ref, out_ref):
@@ -240,7 +309,7 @@
     out_ref[...] = (held_ref[...].astype(F32) + rows).astype(BF16)
 
 
-def order_kernel(ret_ref, parent_ref, want_ref, pixel_ref, start_ref):
+def order_kernel(ret_ref, parent_ref, want_ref, block_ref, start_ref):
     parent = parent_ref[...].astype(F32)
     ret = ret_ref[0:1, :].astype(F32)
     p_col = columns(parent, LEAVES)
@@ -252,16 +321,14 @@
         less = jnp.where(p_col * LEAVES + l_col < pr * LEAVES + lr, 1.0, 0.0)
         parts.append(jnp.sum(less, axis=0, keepdims=True))
     place = jnp.concatenate(parts, axis=1)
-    hit = place == fiota((LEAVES, LEAVES), 0)
-    want = jnp.sum(jnp.where(hit, ret, 0.0), axis=1, keepdims=True)
-    want_ref[...] = jnp.broadcast_to(want, (LEAVES, LANES)).astype(I32)
-    place_col = columns(place, LEAVES)
-    rows = []
-    for part in range(LEAVES // LANES):
-        inside = place_col == fiota((1, LANES), 1) + part * LANES
-        moved = 2.0 * jnp.sum(jnp.where(inside, p_col, 0.0), axis=0, keepdims=True)
-        rows.append(jnp.concatenate([moved, moved + 1.0], axis=1))
-    pixel_ref[...] = jnp.concatenate(rows + rows, axis=0).astype(I32)
+    for first in range(0, LEAVES, LANES):
+        rows = slice(first, first + LANES)
+        hit = place == fiota((LANES, LEAVES), 0) + first
+        want = jnp.sum(jnp.where(hit, ret, 0.0), axis=1, keepdims=True)
+        want_ref[rows, :] = jnp.broadcast_to(want, (LANES, LANES)).astype(I32)
+        block = 2.0 * jnp.sum(jnp.where(hit, parent, 0.0), axis=1, keepdims=True)
+        block_ref[rows, :] = jnp.broadcast_to(block, (LANES, LANES))
+    block_ref[LEAVES:, :] = jnp.full((GROUP, LANES), -8.0, F32)
     below = jnp.where(p_col < fiota((1, LANES), 1) * LANES, 1.0, 0.0)
     start_ref[...] = jnp.broadcast_to(jnp.sum(below, axis=0, keepdims=True), (8, LANES)).astype(I32)
 
@@ -271,7 +338,7 @@
         order_kernel,
         out_shape=[
             jax.ShapeDtypeStruct((LEAVES, LANES), I32),
-            jax.ShapeDtypeStruct((8, TILE), I32),
+            jax.ShapeDtypeStruct((LEAVES + GROUP, LANES), F32),
             jax.ShapeDtypeStruct((8, LANES), I32),
         ],
         in_specs=[VMEM, VMEM],
@@ -330,10 +397,10 @@
         scratch_shapes=[pltpu.VMEM((3, 4 * LANES, 2 * LANES), BF16)],
         compiler_params=pltpu.CompilerParams(vmem_limit_bytes=24 * 2**20),
         cost_estimate=pl.CostEstimate(flops=6 * 10**9, bytes_accessed=8 * 2**20, transcendentals=0),
-    )(coarse, coarse, coarse, head, foot, weight)
-
-
-def field_kernel(start_ref, conv_ref, back_ref, held_ref, want_ref, pixel_ref, we_ref, wp_ref, out_ref, pix_ref, acc_ref):
+    )(*[kept(coarse)] * 3, head, foot, weight)
+
+
+def field_kernel(start_ref, conv_ref, back_ref, held_ref, want_ref, block_ref, we_ref, wp_ref, out_ref, pix_ref):
     step = pl.program_id(0)
 
     @pl.when(step == 0)
@@ -341,32 +408,41 @@
         leaf = (gathered(want_ref[...], back_ref) + held_ref[...].astype(F32)).astype(BF16)
         expanded = jax.nn.gelu(dot(leaf, we_ref[...])).astype(BF16)
         pixels = dot(expanded, wp_ref[...]).astype(BF16)
-        for part in range(LEAVES // LANES):
-            leaves = slice(part * LANES, (part + 1) * LANES)
-            for c in range(2):
-                for r in range(2):
-                    block = pixels[leaves, (2 * r + c) * LANES : (2 * r + c + 1) * LANES]
-                    pix_ref[part, c * LANES : (c + 1) * LANES, r * LANES : (r + 1) * LANES] = block
-
+        for c in range(2):
+            for r in range(2):
+                lanes = slice(r * LANES, (r + 1) * LANES)
+                pix_ref[c, :LEAVES, lanes] = pixels[:, (2 * r + c) * LANES : (2 * r + c + 1) * LANES]
+            pix_ref[c, LEAVES:, :] = jnp.zeros((GROUP, D), BF16)
+
+    def added(index, first):
+        rows = pl.ds(pl.multiple_of(first, ALIGN), GROUP)
+        spots = block_ref[rows, :].T[0:1, :] - (index * TILE).astype(F32)
+        spots = jnp.concatenate([spots, spots + 1.0], axis=1).astype(I32)
+        hot = jnp.where(iota((TILE, 2 * GROUP), 0) == spots, 1.0, 0.0).astype(BF16)
+        return dot(hot, jnp.concatenate([pix_ref[0, rows, :], pix_ref[1, rows, :]], axis=0))
+
+    def held_rows(pair):
+        return jnp.concatenate([conv_ref[0, 2 * pair], conv_ref[0, 2 * pair + 1]], axis=1).astype(F32)
+
+    def store(pair, total):
+        out_ref[0, 2 * pair] = total[:, :LANES].astype(BF16)
+        out_ref[0, 2 * pair + 1] = total[:, LANES:].astype(BF16)
+
+    pairs = []
     for pair in range(STRIP // 2):
         index = step * (STRIP // 2) + pair
-        acc_ref[:, :LANES] = conv_ref[0, 2 * pair].astype(F32)
-        acc_ref[:, LANES:] = conv_ref[0, 2 * pair + 1].astype(F32)
-
-        def add(part, _):
-            target = pixel_ref[pl.ds(part, 1), :] - index * TILE
-            hot = jnp.where(iota((TILE, TILE), 0) == target, 1.0, 0.0).astype(BF16)
-            acc_ref[...] += dot(hot, pix_ref[part])
-            return 0
-
-        low = start_ref[index] // LANES
-        high = (start_ref[index + 1] + LANES - 1) // LANES
-        lax.fori_loop(low, high, add, 0)
-        out_ref[0, 2 * pair] = acc_ref[:, :LANES].astype(BF16)
-        out_ref[0, 2 * pair + 1] = acc_ref[:, LANES:].astype(BF16)
-
-
-def call_field(starts, conv, back, held, want, pixel, w_expand, w_pixels):
+        first = start_ref[index] // ALIGN * ALIGN
+        pairs.append((pair, index, first, start_ref[index + 1]))
+        store(pair, held_rows(pair) + added(index, first))
+    for pair, index, first, end in pairs:
+
+        @pl.when(end > first + GROUP)
+        def _():
+            more = lambda part, total: total + added(index, first + part * GROUP)
+            store(pair, lax.fori_loop(0, (end - first + GROUP - 1) // GROUP, more, held_rows(pair)))
+
+
+def call_field(starts, conv, back, held, want, block, w_expand, w_pixels):
     rows, cols, channels = conv.shape[1:]
     whole = lambda *shape: pl.BlockSpec(shape, lambda i, s: (0,) * len(shape))
     strip = pl.BlockSpec((1, STRIP, cols, channels), lambda i, s: (0, i, 0, 0))
@@ -380,17 +456,17 @@
                 whole(BACK, D),
                 whole(LEAVES, D),
                 whole(LEAVES, LANES),
-                whole(8, TILE),
+                whole(LEAVES + GROUP, LANES),
                 whole(D, D),
                 whole(D, 4 * LANES),
             ],
             out_specs=strip,
-            scratch_shapes=[pltpu.VMEM((LEAVES // LANES, TILE, TILE), BF16), pltpu.VMEM((TILE, TILE), F32)],
+            scratch_shapes=[pltpu.VMEM((2, LEAVES + GROUP, D), BF16)],
         ),
         out_shape=jax.ShapeDtypeStruct(conv.shape, BF16),
         compiler_params=pltpu.CompilerParams(vmem_limit_bytes=32 * 2**20),
         cost_estimate=pl.CostEstimate(flops=2 * 10**9, bytes_accessed=10 * 2**20, transcendentals=2**17),
-    )(starts, conv, back, held, want, pixel, w_expand, w_pixels)
+    )(starts, kept(conv), back, held, want, block, w_expand, w_pixels)
 
 
 def exchange(rows, capacity):
@@ -426,32 +502,39 @@
     sent, ret = pl.pallas_call(
         send_kernel,
         out_shape=[jax.ShapeDtypeStruct((SLOTS, WIDE), BF16), jax.ShapeDtypeStruct((8, LEAVES), I32)],
-        in_specs=[VMEM] * 3,
+        in_specs=[pl.BlockSpec(memory_space=pltpu.HBM)] * 3,
         out_specs=[VMEM] * 2,
+        scratch_shapes=[
+            pltpu.VMEM((LEAVES, D), BF16),
+            pltpu.VMEM((1, LEAVES), I32),
+            pltpu.VMEM((1, LEAVES), I32),
+            pltpu.SemaphoreType.DMA((3,)),
+        ],
         compiler_params=pltpu.CompilerParams(vmem_limit_bytes=24 * 2**20),
         cost_estimate=pl.CostEstimate(flops=10**9, bytes_accessed=2**20, transcendentals=0),
-    )(leaves, window_a.reshape(1, LEAVES), window_b.reshape(1, LEAVES))
+    )(*map(kept, (leaves, window_a.reshape(1, LEAVES), window_b.reshape(1, LEAVES))))
     rows_a = exchange(sent, CAP)
+    want, block, starts = call_order(ret, parent.reshape(1, LEAVES))
+    rows_a, want, head, foot = lax.optimization_barrier((rows_a, want, head, foot))
     (sent_b,) = call_layer(
-        layer_a_kernel, 0, [jax.ShapeDtypeStruct((SLOTS, WIDE), BF16)], rows_a, weights
+        layer_a_kernel, [jax.ShapeDtypeStruct((SLOTS, WIDE), BF16)], rows_a, weights
     )
     rows_b = exchange(sent_b, CAP)
+    conv = call_conv(coarse, head, foot, conv_weight)
+    rows_b, conv = lax.optimization_barrier((rows_b, conv))
     home, y, slot, rounds = call_layer(
         layer_b_kernel,
-        1,
         [
             jax.ShapeDtypeStruct((BACK, D), BF16),
             jax.ShapeDtypeStruct((SLOTS, D), BF16),
             jax.ShapeDtypeStruct((8, SLOTS), I32),
-            jax.ShapeDtypeStruct((8, LANES), I32),
+            jax.ShapeDtypeStruct((1,), I32),
         ],
         rows_b,
         weights,
     )
     back = exchange(home, RET)
-    conv = call_conv(coarse, head, foot, conv_weight)
-    want, pixel, starts = call_order(ret, parent.reshape(1, LEAVES))
-    total = rounds[0, 0]
+    total = rounds.reshape(())
 
     def more(state):
         return state[0] < total
@@ -475,7 +558,7 @@
         return turn + 1, held
 
     _, held = lax.while_loop(more, again, (jnp.asarray(1, I32), jnp.zeros((LEAVES, D), BF16)))
-    return call_field(starts[0], conv, back, held, want, pixel, w_expand, w_pixels)
+    return call_field(starts[0], conv, back, held, want, block, w_expand, w_pixels)
 
 
 def solution(mesh):

time: 131 us -> 114 us (0.87)
  blocking collectives: 27.7 us -> 0 us
  starting transfers between devices: 14.6 us -> 26.9 us
  waiting for transfers between devices: 22.5 us -> 33.6 us
  local copies, waits for them, and re-layouts: 12.3 us -> 2.87 us
  Pallas kernels: 52.9 us -> 49.5 us
    all_to_all x1 -> x0, blocking collectives: 27.7 us -> none  [exchange(): lax.all_to_all(blocks, ('tile', 'intra'), split_axis=0, concat_axis=0, ti...]
    all_to_all x2 -> x3, waiting for transfers between devices: 15.1 us -> 29.6 us  [exchange(): lax.all_to_all(blocks, ('tile', 'intra'), split_axis=0, concat_axis=0, ti...]
    all_to_all x2 -> x3, starting transfers between devices: 9.06 us -> 21.4 us  [exchange(): lax.all_to_all(blocks, ('tile', 'intra'), split_axis=0, concat_axis=0, ti...]
    unnamed x42 -> x10, local copies, waits for them, and re-layouts: 10.8 us -> 1.96 us
    pallas_call x2, Pallas kernels: 31.8 us -> 26.8 us  [call_layer(): pl.pallas_call(kernel, out_shape=out_shape, in_specs=[VMEM] + [pl.BlockSp...]
    ppermute x1, waiting for transfers between devices: 7.37 us -> 4.02 us  [shards(): lax.ppermute(coarse[:, :1], 'intra', [(i + 1, i) for i in range(count - 1)])]
    pallas_call x1, Pallas kernels: 1.32 us -> 2.92 us  [shards(): pl.pallas_call(send_kernel, out_shape=[jax.ShapeDtypeStruct((SLOTS, WIDE)...]
    pallas_call x1, Pallas kernels: 8.14 us -> 9.59 us  [call_conv(): pl.pallas_call(functools.partial(conv_kernel, count), grid=(count,), out_...]
  transfers between devices with their start and end apart: 4 -> 5, of which waited for: 2 -> 4; matrix products, arithmetic and copies ran while one was open for 1% -> 1% of each run, Pallas kernels for 7% -> 9%
where the time goes in v1:
time: 114 us
  Pallas kernels  49.5 us (43%)
  waiting for transfers between devices  33.6 us (29%)
  starting transfers between devices  26.9 us (24%)
  local copies, waits for them, and re-layouts  2.87 us (3%)
    all_to_all x3, waiting for transfers between devices, exchange(): lax.all_to_all(blocks, ('tile', 'intra'), split_axis=0, concat_axis=0, ti...  29.6 us
    pallas_call x2, Pallas kernels, call_layer(): pl.pallas_call(kernel, out_shape=out_shape, in_specs=[VMEM] + [pl.BlockSp...  26.8 us
    all_to_all x3, starting transfers between devices, exchange(): lax.all_to_all(blocks, ('tile', 'intra'), split_axis=0, concat_axis=0, ti...  21.4 us
    pallas_call x1, Pallas kernels, call_field(): pl.pallas_call(field_kernel, grid_spec=pltpu.PrefetchScalarGridSpec(num_s...  9.69 us
    pallas_call x1, Pallas kernels, call_conv(): pl.pallas_call(functools.partial(conv_kernel, count), grid=(count,), out_...  9.59 us
    ppermute x1, waiting for transfers between devices, shards(): lax.ppermute(coarse[:, :1], 'intra', [(i + 1, i) for i in range(count - 1)])  4.02 us
    ppermute x1, starting transfers between devices, shards(): lax.ppermute(coarse[:, :1], 'intra', [(i + 1, i) for i in range(count - 1)])  2.98 us
    pallas_call x1, Pallas kernels, shards(): pl.pallas_call(send_kernel, out_shape=[jax.ShapeDtypeStruct((SLOTS, WIDE)...  2.92 us
  transfers between devices with their start and end apart: 5, of which 4 were waited for; matrix products, arithmetic and copies ran while one was open for 1% of the time, Pallas kernels for 9%

profile of v1, /device:TPU:1, one launch (start us, length us, event | category | flops | bytes accessed | tf_op | source)
XLA Modules:
  0.0 113.8 jit_solution(13501431802813721363)
XLA Ops:
  0.0 2.9 %shard_map.154 = (bf16[1024,384]{1,0:T(8,128)(2,1)}, s32[8,512]{1,0:T(8,128)S(1)}) custom-call(bf16[512,256]{1,0:T(8,128)(2,1)} %leaves_hbm.1, s32[1,512]{1,0:T(1,128)} %bitcast.27, s32[1,512]{1,0:T(1,128)} %bitcast.28), custom_call_target="tpu_custom_call" | custom-call | flops 1000000000 | bytes 1048576 | tf_op jit(solution)/shard_map/pallas_call | solution.py:502
  2.9 11.5 %all-to-all-start.1 = ((bf16[128,8,384]{2,1,0:T(8,128)(2,1)}), bf16[128,8,384]{2,1,0:T(8,128)(2,1)S(1)}, u32[]{:S(2)}, u32[]{:S(2)}) async-start(bf16[128,8,384]{2,1,0:T(8,128)(2,1)} %bitcast.7), calls=%async_computation.1 | async-start | bytes 1572864 | tf_op jit(solution)/shard_map/all_to_all | solution.py:475
  14.4 0.9 fusion
  15.3 3.0 %collective-permute-start.1 = (bf16[1,1,256,128]{3,2,1,0:T(8,128)(2,1)S(1)}, bf16[1,1,256,128]{3,2,1,0:T(8,128)(2,1)S(1)}, u32[]{:S(2)}, u32[]{:S(2)}) collective-permute-start(bf16[1,1,256,128]{3,2,1,0:T(8,128)(2,1)S(1)} %get-tuple-element.81), channel_id=1, source_target_pairs={{1,0},{2,1},{3,2},{4,3},{5,4},{6,5},{7,6},{9,8},{10,9},{11,10},{12... | collective-permute-start | bytes 196616 | tf_op jit(solution)/shard_map/ppermute | solution.py:501
  18.3 2.6 %collective-permute-start = (bf16[1,1,256,128]{3,2,1,0:T(8,128)(2,1)S(1)}, bf16[1,1,256,128]{3,2,1,0:T(8,128)(2,1)S(1)}, u32[]{:S(2)}, u32[]{:S(2)}) collective-permute-start(bf16[1,1,256,128]{3,2,1,0:T(8,128)(2,1)S(1)} %get-tuple-element.82), channel_id=1, source_target_pairs={{0,1},{1,2},{2,3},{3,4},{4,5},{5,6},{6,7},{8,9},{9,10},{10,11},{11... | collective-permute-start | bytes 196616 | tf_op jit(solution)/shard_map/ppermute | solution.py:500
  20.9 0.0 copy-done.4
  20.9 0.6 shard_map.155
  21.5 4.0 %collective-permute-done.1.foot_ref = bf16[1,1,256,128]{3,2,1,0:T(8,128)(2,1)S(1)} collective-permute-done((bf16[1,1,256,128]{3,2,1,0:T(8,128)(2,1)S(1)}, bf16[1,1,256,128]{3,2,1,0:T(8,128)(2,1)S(1)}, u32[]{:S(2)}, u32[]{:S(2)}) %collective-permute-start.1) | collective-permute-done | bytes 65568 | tf_op jit(solution)/shard_map/ppermute | solution.py:501
  25.5 0.0 collective-permute-done.head_ref
  25.5 5.4 %all-to-all-done.1 = bf16[128,8,384]{2,1,0:T(8,128)(2,1)S(1)} async-done(((bf16[128,8,384]{2,1,0:T(8,128)(2,1)}), bf16[128,8,384]{2,1,0:T(8,128)(2,1)S(1)}, u32[]{:S(2)}, u32[]{:S(2)}) %all-to-all-start.1) | async-done | bytes 786464 | tf_op jit(solution)/shard_map/all_to_all | solution.py:475
  30.8 16.8 %shard_map.156 = bf16[1024,384]{1,0:T(8,128)(2,1)} custom-call(bf16[1024,384]{1,0:T(8,128)(2,1)S(1)} %bitcast.22, bf16[2,256,256]{2,1,0:T(8,128)(2,1)} %refs_0_.3, bf16[2,256,256]{2,1,0:T(8,128)(2,1)} %refs_1_.3, bf16[2,256,256]{2,1,0:T(8,128)(2,1)} %refs_2_.3, bf16[2,256,256]{2,1,0:T(8,128)(2,1)} %refs_3_.3, bf16[2,256,1024]{2,1,0:T(8,128)(2,1)} %refs_4_.3, ...), custom_call_target="tpu_custom_call" | custom-call | flops 6000000000 | bytes 4194304 | tf_op jit(solution)/shard_map/pallas_call | solution.py:274
  47.7 5.0 %all-to-all-start.2 = ((bf16[128,8,384]{2,1,0:T(8,128)(2,1)}), bf16[128,8,384]{2,1,0:T(8,128)(2,1)S(1)}, u32[]{:S(2)}, u32[]{:S(2)}) async-start(bf16[128,8,384]{2,1,0:T(8,128)(2,1)} %bitcast.9), calls=%async_computation.2 | async-start | bytes 1572864 | tf_op jit(solution)/shard_map/all_to_all | solution.py:475
  52.7 0.0 copy-done.3
  52.7 9.6 %shard_map.157.conv_ref = bf16[1,64,256,128]{3,2,1,0:T(8,128)(2,1)S(1)} custom-call(bf16[1,64,256,128]{3,2,1,0:T(8,128)(2,1)} %below_ref.1, bf16[1,64,256,128]{3,2,1,0:T(8,128)(2,1)} %below_ref.1, bf16[1,64,256,128]{3,2,1,0:T(8,128)(2,1)} %below_ref.1, bf16[1,1,256,128]{3,2,1,0:T(8,128)(2,1)S(1)} %collective-permute-done.head_ref, ...), custom_call_target="tpu_custom_call" | custom-call | flops 6000000000 | bytes 8388608 | tf_op jit(solution)/shard_map/pallas_call | solution.py:384
  62.3 1.9 %copy-done = bf16[1,64,256,128]{3,2,1,0:T(8,128)(2,1)} copy-done((bf16[1,64,256,128]{3,2,1,0:T(8,128)(2,1)}, bf16[1,64,256,128]{3,2,1,0:T(8,128)(2,1)S(1)}, u32[]{:S(2)}) %copy-start) | copy-done | bytes 4194328
  64.2 5.0 %all-to-all-done.2 = bf16[128,8,384]{2,1,0:T(8,128)(2,1)S(1)} async-done(((bf16[128,8,384]{2,1,0:T(8,128)(2,1)}), bf16[128,8,384]{2,1,0:T(8,128)(2,1)S(1)}, u32[]{:S(2)}, u32[]{:S(2)}) %all-to-all-start.2) | async-done | bytes 786464 | tf_op jit(solution)/shard_map/all_to_all | solution.py:475
  69.2 9.9 %shard_map.158 = (bf16[2048,256]{1,0:T(8,128)(2,1)}, bf16[1024,256]{1,0:T(8,128)(2,1)S(1)}, s32[8,1024]{1,0:T(8,128)S(1)}, s32[1]{0:T(128)}) custom-call(bf16[1024,384]{1,0:T(8,128)(2,1)S(1)} %bitcast.23, bf16[2,256,256]{2,1,0:T(8,128)(2,1)} %refs_0_.3, bf16[2,256,256]{2,1,0:T(8,128)(2,1)} %refs_1_.3, bf16[2,256,256]{2,1,0:T(8,128)(2,1)} %refs_2_.3, ...), custom_call_target="tpu_custom_call" | custom-call | flops 6000000000 | bytes 4194304 | tf_op jit(solution)/shard_map/pallas_call | solution.py:274
  79.2 0.0 copy-start.1
  79.2 0.0 copy-start.2
  79.2 0.7 while.10
  79.9 4.9 %all-to-all-start.3 = ((bf16[128,16,256]{2,1,0:T(8,128)(2,1)}), bf16[128,16,256]{2,1,0:T(8,128)(2,1)S(1)}, u32[]{:S(2)}, u32[]{:S(2)}) async-start(bf16[128,16,256]{2,1,0:T(8,128)(2,1)} %bitcast.11), calls=%async_computation.3 | async-start | bytes 2097152 | tf_op jit(solution)/shard_map/all_to_all | solution.py:475
  84.8 19.2 %all-to-all-done.3 = bf16[128,16,256]{2,1,0:T(8,128)(2,1)S(1)} async-done(((bf16[128,16,256]{2,1,0:T(8,128)(2,1)}), bf16[128,16,256]{2,1,0:T(8,128)(2,1)S(1)}, u32[]{:S(2)}, u32[]{:S(2)}) %all-to-all-start.3) | async-done | bytes 1048608 | tf_op jit(solution)/shard_map/all_to_all | solution.py:475
  104.1 0.0 copy-done.2
  104.1 9.7 %shard_map.159 = bf16[1,64,256,128]{3,2,1,0:T(8,128)(2,1)} custom-call(s32[128]{0:T(128)S(1)} %slice_bitcast_fusion.start_ref, bf16[1,64,256,128]{3,2,1,0:T(8,128)(2,1)} %copy-done, bf16[2048,256]{1,0:T(8,128)(2,1)S(1)} %bitcast.21, bf16[512,256]{1,0:T(8,128)(2,1)S(1)} %get-tuple-element.67.held_ref, s32[512,128]{1,0:T(8,128)S(1)} %get-tuple-element.150, ...), custom_call_target="tpu_custom_call" | custom-call | flops 2000000000 | bytes 10485760 | tf_op jit(solution)/shard_map/pallas_call | solution.py:449
  (6 shorter events, 0.0 us)
Async XLA Ops:
  0.0 20.9 %copy-start.4 = (s32[512]{0:T(512)S(1)}, s32[512]{0:T(512)}, u32[]{:S(2)}) copy-start(s32[512]{0:T(512)} %param.21) | copy-start | bytes 6148
  2.9 27.9 %all-to-all-start.1 = ((bf16[128,8,384]{2,1,0:T(8,128)(2,1)}), bf16[128,8,384]{2,1,0:T(8,128)(2,1)S(1)}, u32[]{:S(2)}, u32[]{:S(2)}) async-start(bf16[128,8,384]{2,1,0:T(8,128)(2,1)} %bitcast.7), calls=%async_computation.1 | async-start | bytes 1572864 | tf_op jit(solution)/shard_map/all_to_all | solution.py:475
  15.3 10.2 %collective-permute-start.1 = (bf16[1,1,256,128]{3,2,1,0:T(8,128)(2,1)S(1)}, bf16[1,1,256,128]{3,2,1,0:T(8,128)(2,1)S(1)}, u32[]{:S(2)}, u32[]{:S(2)}) collective-permute-start(bf16[1,1,256,128]{3,2,1,0:T(8,128)(2,1)S(1)} %get-tuple-element.81), channel_id=1, source_target_pairs={{1,0},{2,1},{3,2},{4,3},{5,4},{6,5},{7,6},{9,8},{10,9},{11,10},{12... | collective-permute-start | bytes 196616 | tf_op jit(solution)/shard_map/ppermute | solution.py:501
  18.3 7.2 %collective-permute-start = (bf16[1,1,256,128]{3,2,1,0:T(8,128)(2,1)S(1)}, bf16[1,1,256,128]{3,2,1,0:T(8,128)(2,1)S(1)}, u32[]{:S(2)}, u32[]{:S(2)}) collective-permute-start(bf16[1,1,256,128]{3,2,1,0:T(8,128)(2,1)S(1)} %get-tuple-element.82), channel_id=1, source_target_pairs={{0,1},{1,2},{2,3},{3,4},{4,5},{5,6},{6,7},{8,9},{9,10},{10,11},{11... | collective-permute-start | bytes 196616 | tf_op jit(solution)/shard_map/ppermute | solution.py:500
  30.8 21.8 %copy-start.3 = (bf16[3,3,128,128]{3,2,1,0:T(8,128)(2,1)S(1)}, bf16[3,3,128,128]{3,2,1,0:T(8,128)(2,1)}, u32[]{:S(2)}) copy-start(bf16[3,3,128,128]{3,2,1,0:T(8,128)(2,1)} %weight_ref.1) | copy-start | bytes 884740
  47.7 21.5 %all-to-all-start.2 = ((bf16[128,8,384]{2,1,0:T(8,128)(2,1)}), bf16[128,8,384]{2,1,0:T(8,128)(2,1)S(1)}, u32[]{:S(2)}, u32[]{:S(2)}) async-start(bf16[128,8,384]{2,1,0:T(8,128)(2,1)} %bitcast.9), calls=%async_computation.2 | async-start | bytes 1572864 | tf_op jit(solution)/shard_map/all_to_all | solution.py:475
  62.3 1.9 %copy-start = (bf16[1,64,256,128]{3,2,1,0:T(8,128)(2,1)}, bf16[1,64,256,128]{3,2,1,0:T(8,128)(2,1)S(1)}, u32[]{:S(2)}) copy-start(bf16[1,64,256,128]{3,2,1,0:T(8,128)(2,1)S(1)} %shard_map.157.conv_ref) | copy-start | bytes 12582916
  79.2 24.9 %copy-start.1 = (bf16[256,512]{1,0:T(8,128)(2,1)S(1)}, bf16[256,512]{1,0:T(8,128)(2,1)}, u32[]{:S(2)}) copy-start(bf16[256,512]{1,0:T(8,128)(2,1)} %wp_ref.1) | copy-start | bytes 786436
  79.2 24.9 %copy-start.2 = (bf16[256,256]{1,0:T(8,128)(2,1)S(1)}, bf16[256,256]{1,0:T(8,128)(2,1)}, u32[]{:S(2)}) copy-start(bf16[256,256]{1,0:T(8,128)(2,1)} %we_ref.1) | copy-start | bytes 393220
  79.9 24.1 %all-to-all-start.3 = ((bf16[128,16,256]{2,1,0:T(8,128)(2,1)}), bf16[128,16,256]{2,1,0:T(8,128)(2,1)S(1)}, u32[]{:S(2)}, u32[]{:S(2)}) async-start(bf16[128,16,256]{2,1,0:T(8,128)(2,1)} %bitcast.11), calls=%async_computation.3 | async-start | bytes 2097152 | tf_op jit(solution)/shard_map/all_to_all | solution.py:475

commit v2 on v1

--- a/solution.py
+++ b/solution.py
@@ -13,6 +13,7 @@
 EPSILON = 1e-06
 NEGATIVE = -1e30
 LOG2E = math.log2(math.e)
+GELU = math.sqrt(2.0 / math.pi)
 D = 256
 LANES = 128
 WIDE = D + LANES
@@ -25,6 +26,8 @@
 FEW = 640
 GROUP = 64
 ALIGN = 16
+SPAN = 1024
+BAND = 16
 TILE = 256
 FF = 1024
 F32 = jnp.float32
@@ -98,10 +101,10 @@
     lane = iota((LEAVES, LANES), 1)
     extra = jnp.where(lane == 0, b_col + 1.0, jnp.where(lane == 1, rounds, 0.0)).astype(BF16)
     moves[2].wait()
-    for first in range(0, SLOTS, TILE):
-        hot = onehot_rows(first, TILE, slot)
-        out_ref[first : first + TILE, :D] = dot(hot, leaves_ref[...]).astype(BF16)
-        out_ref[first : first + TILE, D:] = dot(hot, extra).astype(BF16)
+    for first in range(0, SLOTS, SPAN):
+        hot = onehot_rows(first, SPAN, slot)
+        out_ref[first : first + SPAN, :D] = dot(hot, leaves_ref[...]).astype(BF16)
+        out_ref[first : first + SPAN, D:] = dot(hot, extra).astype(BF16)
 
 
 def tags_of(x_ref):
@@ -141,51 +144,77 @@
     return moves
 
 
-def layer(layer_index, count, tile, x_ref, tag_row, weights, y_ref, q_ref, k_ref, v_ref):
+def gelu_twice(x):
+    inner = x * (x * x * (0.044715 * GELU) + GELU)
+    return x + x * jnp.tanh(inner)
+
+
+def layer(layer_index, count, tile, x_ref, live, weights, y_ref, q_ref, k_ref, v_ref, live_ref):
     wq, wk, wv, wo, wu, wd, gain_one, gain_two = weights
     one = gain_one[layer_index : layer_index + 1, :]
     two = gain_two[layer_index : layer_index + 1, :]
-    head_of = iota((tile, D), 1) // HEAD_DIM
+    low = iota((tile, LANES), 1) < HEAD_DIM
+    zero = jnp.asarray(0, BF16)
+    live_ref[:count, :] = live.astype(BF16)
+    first = dot(rms(x_ref[:ALIGN, :D].astype(F32), one), wk[...])[0:1, :].astype(BF16)
 
     def project(step, _):
         rows = pl.ds(pl.multiple_of(step * tile, tile), tile)
         normed = rms(x_ref[rows, :D].astype(F32), one)
-        q_ref[rows, :] = dot(normed, wq[...]).astype(BF16) * jnp.asarray(HEAD_DIM**-0.5, BF16)
-        k_ref[rows, :] = dot(normed, wk[...]).astype(BF16)
+        flag = live_ref[rows, :]
+        q_ref[rows, :] = (dot(normed, wq[...]) * (HEAD_DIM**-0.5 * LOG2E)).astype(BF16)
+        key = dot(normed, wk[...]).astype(BF16)
+        k_ref[rows, :] = jnp.where(jnp.concatenate([flag, flag], axis=1) > 0, key, first)
         value = dot(normed, wv[...]).astype(BF16)
-        for head in range(HEADS):
-            v_ref[head, rows, :] = jnp.where(head_of == head, value, jnp.asarray(1, BF16))
+        for pair in range(HEADS // 2):
+            part = value[:, pair * LANES : (pair + 1) * LANES]
+            lanes = slice(pair * LANES, (pair + 1) * LANES)
+            v_ref[2 * pair, rows, lanes] = jnp.where(low, part, flag)
+            v_ref[2 * pair + 1, rows, lanes] = jnp.where(low, flag, part)
+            other = slice((1 - pair) * LANES, (2 - pair) * LANES)
+            v_ref[2 * pair, rows, other] = flag
+            v_ref[2 * pair + 1, rows, other] = flag
         return 0
 
     lax.fori_loop(0, count // tile, project, 0)
-    live = tag_row > 0.0
 
     def attend(step, _):
         rows = pl.ds(pl.multiple_of(step * tile, tile), tile)
-        query = q_ref[rows, :]
-        top = jnp.zeros((tile, D), F32)
-        total = jnp.zeros((tile, D), F32)
+
+        def scored(head):
+            lanes = slice(head // 2 * LANES, (head // 2 + 1) * LANES)
+            query = q_ref[rows, lanes]
+            own = jnp.where(low, query, zero) if head % 2 == 0 else jnp.where(low, zero, query)
+            return dot_nt(own, k_ref[:count, lanes])
+
+        def mixed(head, scores):
+            peak = jnp.max(scores, axis=-1, keepdims=True)
+            lanes = slice(head // 2 * LANES, (head // 2 + 1) * LANES)
+            return dot(jnp.exp2(scores - peak).astype(BF16), v_ref[head, :count, :])[:, lanes]
+
+        ahead = scored(0)
+        outs = []
         for head in range(HEADS):
-            own = jnp.where(head_of == head, query, jnp.asarray(0, BF16))
-            scores = dot_nt(own, k_ref[:count, :])
-            scores = jnp.where(live, scores, NEGATIVE)
-            peak = jnp.max(scores, axis=-1, keepdims=True)
-            probs = jnp.exp2((scores - peak) * LOG2E).astype(BF16)
-            mixed = dot(probs, v_ref[head, :count, :])
-            top = jnp.where(head_of == head, mixed, top)
-            total = jnp.where(head_of == (head + 1) % HEADS, mixed, total)
-        total = pltpu.roll(total, D - HEAD_DIM, 1)
-        att = (top / total).astype(BF16)
+            scores = ahead
+            if head + 1 < HEADS:
+                ahead = scored(head + 1)
+            outs.append(mixed(head, scores))
+        parts = []
+        for pair in range(HEADS // 2):
+            even, odd = outs[2 * pair : 2 * pair + 2]
+            total = pltpu.roll(jnp.where(low, odd, even), HEAD_DIM, 1)
+            parts.append(jnp.where(low, even, odd) / total)
+        att = jnp.concatenate(parts, axis=1).astype(BF16)
         hidden = x_ref[rows, :D].astype(F32) + dot(att, wo[...])
-        up = jax.nn.gelu(dot(rms(hidden, two), wu[...])).astype(BF16)
-        y_ref[rows, :] = (hidden + dot(up, wd[...])).astype(BF16)
+        up = gelu_twice(dot(rms(hidden, two), wu[...])).astype(BF16)
+        y_ref[rows, :] = (hidden + 0.5 * dot(up, wd[...])).astype(BF16)
         return 0
 
     lax.fori_loop(0, count // tile, attend, 0)
 
 
 def layer_a_kernel(x_ref, *refs):
-    sources, out_ref, weights, sems, (y_ref, q_ref, k_ref, v_ref) = refs[:8], refs[8], refs[9:17], refs[17], refs[18:]
+    sources, out_ref, weights, sems, (y_ref, *rest) = refs[:8], refs[8], refs[9:17], refs[17], refs[18:]
     moves = fetch(0, sources, weights, sems)
     tag_row, tag_col, rounds = tags_of(x_ref)
     slot = (tag_row - 1.0) * CAP + ranks_of(tag_row, tag_col)
@@ -195,25 +224,34 @@
     extra = jnp.where(lane == 0, home.astype(F32), 0.0).astype(BF16)
     for move in moves:
         move.wait()
-    layer(0, SLOTS, TILE, x_ref, tag_row, weights, y_ref, q_ref, k_ref, v_ref)
-    for first in range(0, SLOTS, TILE):
-        hot = onehot_rows(first, TILE, slot)
-        out_ref[first : first + TILE, :D] = dot(hot, y_ref[...]).astype(BF16)
-        tail = jnp.where(lane[:TILE] == 1, rounds, dot(hot, extra))
-        out_ref[first : first + TILE, D:] = tail.astype(BF16)
-
-
-def finish_b(count, tile, x_ref, tag_row, tag_col, weights, refs):
-    out_ref, y_ref, slot_ref, q_ref, k_ref, v_ref = refs
-    layer(1, count, tile, x_ref, tag_row, weights, y_ref, q_ref, k_ref, v_ref)
+    live = jnp.where(tag_col > 0.0, 1.0, 0.0)
+    layer(0, SLOTS, 2 * TILE, x_ref, live, weights, y_ref, *rest)
+    for first in range(0, SLOTS, SPAN):
+        hot = onehot_rows(first, SPAN, slot)
+        out_ref[first : first + SPAN, :D] = dot(hot, y_ref[...]).astype(BF16)
+        tail = jnp.where(lane[:SPAN] == 1, rounds, dot(hot, extra))
+        out_ref[first : first + SPAN, D:] = tail.astype(BF16)
+
+
+def finish_b(count, tile, place, x_ref, packed_ref, weights, moves, refs):
+    out_ref, y_ref, slot_ref, *rest = refs
+    packed_ref[:count, :] = dot(onehot_rows(0, count, place), x_ref[...]).astype(BF16)
+    tag_row, tag_col, _ = tags_of(packed_ref.at[:count, :])
     rank = ranks_of(tag_row, tag_col)
     turn = jnp.floor(rank * (1.0 / RET))
     slot = (tag_row - 1.0) * RET + (rank - turn * RET) + turn * BACK
     slot = jnp.where(tag_row > 0.0, slot, -1.0).astype(I32)
     slot_ref[:, :count] = jnp.broadcast_to(slot, (8, count))
-    for first in range(0, BACK, TILE):
-        hot = onehot_rows(first, TILE, slot)
-        out_ref[first : first + TILE, :] = dot(hot, y_ref[:count, :]).astype(BF16)
+    if count < SLOTS:
+        slot_ref[:, count:] = jnp.full((8, SLOTS - count), -1, I32)
+        y_ref[count:, :] = jnp.zeros((SLOTS - count, D), BF16)
+    live = jnp.where(iota((count, LANES), 0) == 0, 1.0, jnp.where(tag_col > 0.0, 1.0, 0.0))
+    for move in moves:
+        move.wait()
+    layer(1, count, tile, packed_ref, live, weights, y_ref, *rest)
+    for first in range(0, BACK, SPAN):
+        hot = onehot_rows(first, SPAN, slot)
+        out_ref[first : first + SPAN, :] = dot(hot, y_ref[:count, :]).astype(BF16)
 
 
 def before(flags):
@@ -231,46 +269,34 @@
 
 def layer_b_kernel(x_ref, *refs):
     sources, (out_ref, y_ref, slot_ref, rounds_ref) = refs[:8], refs[8:12]
-    weights, sems, (q_ref, k_ref, v_ref, packed_ref) = refs[12:20], refs[20], refs[21:]
+    weights, sems, (packed_ref, *rest) = refs[12:20], refs[20], refs[21:]
     moves = fetch(1, sources, weights, sems)
-    tag_row, tag_col, rounds = tags_of(x_ref)
+    tag_row, _, rounds = tags_of(x_ref)
     rounds_ref[0] = rounds.astype(I32)
-    rest = (out_ref, y_ref, slot_ref, q_ref, k_ref, v_ref)
     live = jnp.where(tag_row > 0.0, 1.0, 0.0)
     total = jnp.sum(live)
+    place = jnp.where(tag_row > 0.0, before(live), -1.0).astype(I32)
+    outs = (out_ref, y_ref, slot_ref, *rest)
 
     @pl.when(total <= FEW)
     def _():
-        place = jnp.where(tag_row > 0.0, before(live), -1.0).astype(I32)
-        for first in range(0, FEW, LANES):
-            hot = onehot_rows(first, LANES, place)
-            packed_ref[first : first + LANES, :] = dot(hot, x_ref[...]).astype(BF16)
-        few_row, few_col, _ = tags_of(packed_ref)
-        slot_ref[:, FEW:] = jnp.full((8, SLOTS - FEW), -1, I32)
-        y_ref[FEW:, :] = jnp.zeros((SLOTS - FEW, D), BF16)
-        for move in moves:
-            move.wait()
-        finish_b(FEW, FEW // 2, packed_ref, few_row, few_col, weights, rest)
+        finish_b(FEW, FEW // 2, place, x_ref, packed_ref, weights, moves, outs)
 
     @pl.when(total > FEW)
     def _():
-        for move in moves:
-            move.wait()
-        finish_b(SLOTS, TILE, x_ref, tag_row, tag_col, weights, rest)
+        finish_b(SLOTS, TILE, place, x_ref, packed_ref, weights, moves, outs)
 
 
 def call_layer(kernel, out_shape, x, weights):
     kernel_weights = [pltpu.VMEM(weight.shape[1:], BF16) for weight in weights[:6]]
     kernel_weights += [pltpu.VMEM(gain.shape, F32) for gain in weights[6:]]
     scratch = [
+        pltpu.VMEM((SLOTS, D) if len(out_shape) == 1 else (SLOTS, WIDE), BF16),
         pltpu.VMEM((SLOTS, D), BF16),
         pltpu.VMEM((SLOTS, D), BF16),
         pltpu.VMEM((HEADS, SLOTS, D), BF16),
+        pltpu.VMEM((SLOTS, LANES), BF16),
     ]
-    if len(out_shape) == 1:
-        scratch = [pltpu.VMEM((SLOTS, D), BF16)] + scratch
-    else:
-        scratch = scratch + [pltpu.VMEM((FEW, WIDE), BF16)]
     return pl.pallas_call(
         kernel,
         out_shape=out_shape,
@@ -400,14 +426,20 @@
     )(*[kept(coarse)] * 3, head, foot, weight)
 
 
-def field_kernel(start_ref, conv_ref, back_ref, held_ref, want_ref, block_ref, we_ref, wp_ref, out_ref, pix_ref):
+def field_kernel(start_ref, conv_hbm, back_ref, held_ref, want_ref, block_ref, we_ref, wp_ref, out_ref, pix_ref, conv_ref, sems):
     step = pl.program_id(0)
+
+    def move(part):
+        rows = pl.ds(part * BAND, BAND)
+        return pltpu.make_async_copy(conv_hbm.at[0, rows], conv_ref.at[rows], sems.at[part])
 
     @pl.when(step == 0)
     def _():
+        for part in range(conv_ref.shape[0] // BAND):
+            move(part).start()
         leaf = (gathered(want_ref[...], back_ref) + held_ref[...].astype(F32)).astype(BF16)
-        expanded = jax.nn.gelu(dot(leaf, we_ref[...])).astype(BF16)
-        pixels = dot(expanded, wp_ref[...]).astype(BF16)
+        expanded = gelu_twice(dot(leaf, we_ref[...])).astype(BF16)
+        pixels = (0.5 * dot(expanded, wp_ref[...])).astype(BF16)
         for c in range(2):
             for r in range(2):
                 lanes = slice(r * LANES, (r + 1) * LANES)
@@ -422,37 +454,42 @@
         return dot(hot, jnp.concatenate([pix_ref[0, rows, :], pix_ref[1, rows, :]], axis=0))
 
     def held_rows(pair):
-        return jnp.concatenate([conv_ref[0, 2 * pair], conv_ref[0, 2 * pair + 1]], axis=1).astype(F32)
+        row = step * BAND + 2 * pair
+        return jnp.concatenate([conv_ref[row], conv_ref[row + 1]], axis=1).astype(F32)
 
     def store(pair, total):
         out_ref[0, 2 * pair] = total[:, :LANES].astype(BF16)
         out_ref[0, 2 * pair + 1] = total[:, LANES:].astype(BF16)
 
+    move(step).wait()
+    crowded = False
     pairs = []
-    for pair in range(STRIP // 2):
-        index = step * (STRIP // 2) + pair
-        first = start_ref[index] // ALIGN * ALIGN
-        pairs.append((pair, index, first, start_ref[index + 1]))
+    for pair in range(BAND // 2):
+        index = step * (BAND // 2) + pair
+        first = start_ref[0, index] // ALIGN * ALIGN
+        end = start_ref[0, index + 1]
+        crowded = (end > first + GROUP) | crowded
+        pairs.append((pair, index, first, end))
         store(pair, held_rows(pair) + added(index, first))
-    for pair, index, first, end in pairs:
-
-        @pl.when(end > first + GROUP)
-        def _():
-            more = lambda part, total: total + added(index, first + part * GROUP)
+
+    @pl.when(crowded)
+    def _():
+        for pair, index, first, end in pairs:
+            more = lambda part, total, index=index, first=first: total + added(index, first + part * GROUP)
             store(pair, lax.fori_loop(0, (end - first + GROUP - 1) // GROUP, more, held_rows(pair)))
 
 
 def call_field(starts, conv, back, held, want, block, w_expand, w_pixels):
     rows, cols, channels = conv.shape[1:]
     whole = lambda *shape: pl.BlockSpec(shape, lambda i, s: (0,) * len(shape))
-    strip = pl.BlockSpec((1, STRIP, cols, channels), lambda i, s: (0, i, 0, 0))
+    strip = pl.BlockSpec((1, BAND, cols, channels), lambda i, s: (0, i, 0, 0))
     return pl.pallas_call(
         field_kernel,
         grid_spec=pltpu.PrefetchScalarGridSpec(
             num_scalar_prefetch=1,
-            grid=(rows // STRIP,),
+            grid=(rows // BAND,),
             in_specs=[
-                strip,
+                pl.BlockSpec(memory_space=pltpu.HBM),
                 whole(BACK, D),
                 whole(LEAVES, D),
                 whole(LEAVES, LANES),
@@ -461,7 +498,11 @@
                 whole(D, 4 * LANES),
             ],
             out_specs=strip,
-            scratch_shapes=[pltpu.VMEM((2, LEAVES + GROUP, D), BF16)],
+            scratch_shapes=[
+                pltpu.VMEM((2, LEAVES + GROUP, D), BF16),
+                pltpu.VMEM(conv.shape[1:], BF16),
+                pltpu.SemaphoreType.DMA((rows // BAND,)),
+            ],
         ),
         out_shape=jax.ShapeDtypeStruct(conv.shape, BF16),
         compiler_params=pltpu.CompilerParams(vmem_limit_bytes=32 * 2**20),
@@ -558,7 +599,7 @@
         return turn + 1, held
 
     _, held = lax.while_loop(more, again, (jnp.asarray(1, I32), jnp.zeros((LEAVES, D), BF16)))
-    return call_field(starts[0], conv, back, held, want, block, w_expand, w_pixels)
+    return call_field(starts, conv, back, held, want, block, w_expand, w_pixels)
 
 
 def solution(mesh):

time: 114 us -> 108 us (0.947)
  blocking collectives: 0 us -> 23.9 us
  waiting for transfers between devices: 33.6 us -> 13.7 us
  Pallas kernels: 49.5 us -> 43.2 us
  starting transfers between devices: 26.9 us -> 22 us
    all_to_all x0 -> x1, blocking collectives: none -> 23.9 us  [exchange(): lax.all_to_all(blocks, ('tile', 'intra'), split_axis=0, concat_axis=0, ti...]
    all_to_all x3 -> x2, waiting for transfers between devices: 29.6 us -> 10.3 us  [exchange(): lax.all_to_all(blocks, ('tile', 'intra'), split_axis=0, concat_axis=0, ti...]
    all_to_all x3 -> x2, starting transfers between devices: 21.4 us -> 16.5 us  [exchange(): lax.all_to_all(blocks, ('tile', 'intra'), split_axis=0, concat_axis=0, ti...]
    pallas_call x2, Pallas kernels: 26.8 us -> 22.5 us  [call_layer(): pl.pallas_call(kernel, out_shape=out_shape, in_specs=[VMEM] + [pl.BlockSp...]
    pallas_call x1, Pallas kernels: 9.69 us -> 6.9 us  [call_field(): pl.pallas_call(field_kernel, grid_spec=pltpu.PrefetchScalarGridSpec(num_s...]
  transfers between devices with their start and end apart: 5 -> 4, of which waited for: 4 -> 3; matrix products, arithmetic and copies ran while one was open for 1% -> 1% of each run, Pallas kernels for 9% -> 10%
where the time goes in v2:
time: 108 us; the launch traced here: 107 us
  Pallas kernels  43.2 us (40%)
  blocking collectives  23.9 us (22%)
  starting transfers between devices  22 us (20%)
  waiting for transfers between devices  13.7 us (13%)
  local copies, waits for them, and re-layouts  3.57 us (3%)
    all_to_all x1, blocking collectives, exchange(): lax.all_to_all(blocks, ('tile', 'intra'), split_axis=0, concat_axis=0, ti...  23.9 us
    pallas_call x2, Pallas kernels, call_layer(): pl.pallas_call(kernel, out_shape=out_shape, in_specs=[VMEM] + [pl.BlockSp...  22.5 us
    all_to_all x2, starting transfers between devices, exchange(): lax.all_to_all(blocks, ('tile', 'intra'), split_axis=0, concat_axis=0, ti...  16.5 us
    all_to_all x2, waiting for transfers between devices, exchange(): lax.all_to_all(blocks, ('tile', 'intra'), split_axis=0, concat_axis=0, ti...  10.3 us
    pallas_call x1, Pallas kernels, call_conv(): pl.pallas_call(functools.partial(conv_kernel, count), grid=(count,), out_...  9.59 us
    pallas_call x1, Pallas kernels, call_field(): pl.pallas_call(field_kernel, grid_spec=pltpu.PrefetchScalarGridSpec(num_s...  6.9 us
    ppermute x1, waiting for transfers between devices, shards(): lax.ppermute(coarse[:, :1], 'intra', [(i + 1, i) for i in range(count - 1)])  3.35 us
    ppermute x1, starting transfers between devices, shards(): lax.ppermute(coarse[:, :1], 'intra', [(i + 1, i) for i in range(count - 1)])  2.98 us
  transfers between devices with their start and end apart: 4, of which 3 were waited for; matrix products, arithmetic and copies ran while one was open for 1% of the time, Pallas kernels for 10%

profile of v2, /device:TPU:1, one launch (start us, length us, event | category | flops | bytes accessed | tf_op | source)
XLA Modules:
  0.0 107.3 jit_solution(10191408159152610963)
XLA Ops:
  0.0 2.9 %shard_map.154 = (bf16[1024,384]{1,0:T(8,128)(2,1)}, s32[8,512]{1,0:T(8,128)S(1)}) custom-call(bf16[512,256]{1,0:T(8,128)(2,1)} %leaves_hbm.1, s32[1,512]{1,0:T(1,128)} %bitcast.26, s32[1,512]{1,0:T(1,128)} %bitcast.27), custom_call_target="tpu_custom_call" | custom-call | flops 1000000000 | bytes 1048576 | tf_op jit(solution)/shard_map/pallas_call | solution.py:543
  2.9 11.5 %all-to-all-start.1 = ((bf16[128,8,384]{2,1,0:T(8,128)(2,1)}), bf16[128,8,384]{2,1,0:T(8,128)(2,1)S(1)}, u32[]{:S(2)}, u32[]{:S(2)}) async-start(bf16[128,8,384]{2,1,0:T(8,128)(2,1)} %bitcast.6), calls=%async_computation.1 | async-start | bytes 1572864 | tf_op jit(solution)/shard_map/all_to_all | solution.py:516
  14.4 0.9 fusion
  15.3 3.0 %collective-permute-start.1 = (bf16[1,1,256,128]{3,2,1,0:T(8,128)(2,1)S(1)}, bf16[1,1,256,128]{3,2,1,0:T(8,128)(2,1)S(1)}, u32[]{:S(2)}, u32[]{:S(2)}) collective-permute-start(bf16[1,1,256,128]{3,2,1,0:T(8,128)(2,1)S(1)} %get-tuple-element.81), channel_id=1, source_target_pairs={{1,0},{2,1},{3,2},{4,3},{5,4},{6,5},{7,6},{9,8},{10,9},{11,10},{12... | collective-permute-start | bytes 196616 | tf_op jit(solution)/shard_map/ppermute | solution.py:542
  18.3 2.6 %collective-permute-start = (bf16[1,1,256,128]{3,2,1,0:T(8,128)(2,1)S(1)}, bf16[1,1,256,128]{3,2,1,0:T(8,128)(2,1)S(1)}, u32[]{:S(2)}, u32[]{:S(2)}) collective-permute-start(bf16[1,1,256,128]{3,2,1,0:T(8,128)(2,1)S(1)} %get-tuple-element.82), channel_id=1, source_target_pairs={{0,1},{1,2},{2,3},{3,4},{4,5},{5,6},{6,7},{8,9},{9,10},{10,11},{11... | collective-permute-start | bytes 196616 | tf_op jit(solution)/shard_map/ppermute | solution.py:541
  20.9 0.0 copy-done.4
  20.9 1.2 %shard_map.155 = (s32[512,128]{1,0:T(8,128)}, f32[576,128]{1,0:T(8,128)S(1)}, s32[8,128]{1,0:T(8,128)S(1)}) custom-call(s32[8,512]{1,0:T(8,128)S(1)} %get-tuple-element.53.ret_ref, s32[1,512]{1,0:T(1,128)S(1)} %bitcast.23), custom_call_target="tpu_custom_call" | custom-call | flops 1000000000 | bytes 1048576 | tf_op jit(solution)/shard_map/pallas_call | solution.py:363
  22.1 3.4 %collective-permute-done.1.foot_ref = bf16[1,1,256,128]{3,2,1,0:T(8,128)(2,1)S(1)} collective-permute-done((bf16[1,1,256,128]{3,2,1,0:T(8,128)(2,1)S(1)}, bf16[1,1,256,128]{3,2,1,0:T(8,128)(2,1)S(1)}, u32[]{:S(2)}, u32[]{:S(2)}) %collective-permute-start.1) | collective-permute-done | bytes 65568 | tf_op jit(solution)/shard_map/ppermute | solution.py:542
  25.5 0.0 collective-permute-done.head_ref
  25.5 5.4 %all-to-all-done.1 = bf16[128,8,384]{2,1,0:T(8,128)(2,1)S(1)} async-done(((bf16[128,8,384]{2,1,0:T(8,128)(2,1)}), bf16[128,8,384]{2,1,0:T(8,128)(2,1)S(1)}, u32[]{:S(2)}, u32[]{:S(2)}) %all-to-all-start.1) | async-done | bytes 786464 | tf_op jit(solution)/shard_map/all_to_all | solution.py:516
  30.8 13.2 %shard_map.156 = bf16[1024,384]{1,0:T(8,128)(2,1)} custom-call(bf16[1024,384]{1,0:T(8,128)(2,1)S(1)} %bitcast.21, bf16[2,256,256]{2,1,0:T(8,128)(2,1)} %refs_0_.3, bf16[2,256,256]{2,1,0:T(8,128)(2,1)} %refs_1_.3, bf16[2,256,256]{2,1,0:T(8,128)(2,1)} %refs_2_.3, bf16[2,256,256]{2,1,0:T(8,128)(2,1)} %refs_3_.3, bf16[2,256,1024]{2,1,0:T(8,128)(2,1)} %refs_4_.3, ...), custom_call_target="tpu_custom_call" | custom-call | flops 6000000000 | bytes 4194304 | tf_op jit(solution)/shard_map/pallas_call | solution.py:300
  44.0 5.0 %all-to-all-start.2 = ((bf16[128,8,384]{2,1,0:T(8,128)(2,1)}), bf16[128,8,384]{2,1,0:T(8,128)(2,1)S(1)}, u32[]{:S(2)}, u32[]{:S(2)}) async-start(bf16[128,8,384]{2,1,0:T(8,128)(2,1)} %bitcast.8), calls=%async_computation.2 | async-start | bytes 1572864 | tf_op jit(solution)/shard_map/all_to_all | solution.py:516
  49.0 0.0 copy-done.3
  49.0 9.6 %shard_map.157.conv_hbm = bf16[1,64,256,128]{3,2,1,0:T(8,128)(2,1)S(1)} custom-call(bf16[1,64,256,128]{3,2,1,0:T(8,128)(2,1)} %below_ref.1, bf16[1,64,256,128]{3,2,1,0:T(8,128)(2,1)} %below_ref.1, bf16[1,64,256,128]{3,2,1,0:T(8,128)(2,1)} %below_ref.1, bf16[1,1,256,128]{3,2,1,0:T(8,128)(2,1)S(1)} %collective-permute-done.head_ref, ...), custom_call_target="tpu_custom_call" | custom-call | flops 6000000000 | bytes 8388608 | tf_op jit(solution)/shard_map/pallas_call | solution.py:410
  58.6 0.0 copy-start
  58.6 1.9 %copy-done = bf16[1,64,256,128]{3,2,1,0:T(8,128)(2,1)} copy-done((bf16[1,64,256,128]{3,2,1,0:T(8,128)(2,1)}, bf16[1,64,256,128]{3,2,1,0:T(8,128)(2,1)S(1)}, u32[]{:S(2)}) %copy-start) | copy-done | bytes 4194328
  60.6 5.0 %all-to-all-done.2 = bf16[128,8,384]{2,1,0:T(8,128)(2,1)S(1)} async-done(((bf16[128,8,384]{2,1,0:T(8,128)(2,1)}), bf16[128,8,384]{2,1,0:T(8,128)(2,1)S(1)}, u32[]{:S(2)}, u32[]{:S(2)}) %all-to-all-start.2) | async-done | bytes 786464 | tf_op jit(solution)/shard_map/all_to_all | solution.py:516
  65.5 9.4 %shard_map.158 = (bf16[2048,256]{1,0:T(8,128)(2,1)S(1)}, bf16[1024,256]{1,0:T(8,128)(2,1)S(1)}, s32[8,1024]{1,0:T(8,128)S(1)}, s32[1]{0:T(128)}) custom-call(bf16[1024,384]{1,0:T(8,128)(2,1)S(1)} %bitcast.22, bf16[2,256,256]{2,1,0:T(8,128)(2,1)} %refs_0_.3, bf16[2,256,256]{2,1,0:T(8,128)(2,1)} %refs_1_.3, bf16[2,256,256]{2,1,0:T(8,128)(2,1)} %refs_2_.3, ...), custom_call_target="tpu_custom_call" | custom-call | flops 6000000000 | bytes 4194304 | tf_op jit(solution)/shard_map/pallas_call | solution.py:300
  74.9 0.7 broadcast_in_dim.3
  75.7 0.6 while.10
  76.3 23.9 %all_to_all.21 = bf16[128,16,256]{2,1,0:T(8,128)(2,1)S(1)} all-to-all(bf16[128,16,256]{2,1,0:T(8,128)(2,1)S(1)} %bitcast.20), channel_id=1, replica_groups=mesh['tile'=16,'intra'=8] {'tile','intra'}, dimensions={0} | all-to-all | bytes 2097152 | tf_op jit(solution)/shard_map/all_to_all | solution.py:516
  100.2 0.0 copy-done.1
  100.2 0.0 copy-done.2
  100.2 6.9 %shard_map.159 = bf16[1,64,256,128]{3,2,1,0:T(8,128)(2,1)} custom-call(s32[8,128]{1,0:T(8,128)S(1)} %get-tuple-element.54.start_ref, bf16[1,64,256,128]{3,2,1,0:T(8,128)(2,1)} %copy-done, bf16[2048,256]{1,0:T(8,128)(2,1)S(1)} %bitcast.19, bf16[512,256]{1,0:T(8,128)(2,1)} %get-tuple-element.67.held_ref, s32[512,128]{1,0:T(8,128)} %get-tuple-element.149, ...), custom_call_target="tpu_custom_call" | custom-call | flops 2000000000 | bytes 10485760 | tf_op jit(solution)/shard_map/pallas_call | solution.py:486
  (4 shorter events, 0.0 us)
Async XLA Ops:
  0.0 20.9 %copy-start.4 = (s32[512]{0:T(512)S(1)}, s32[512]{0:T(512)}, u32[]{:S(2)}) copy-start(s32[512]{0:T(512)} %param.21) | copy-start | bytes 6148
  2.9 27.9 %all-to-all-start.1 = ((bf16[128,8,384]{2,1,0:T(8,128)(2,1)}), bf16[128,8,384]{2,1,0:T(8,128)(2,1)S(1)}, u32[]{:S(2)}, u32[]{:S(2)}) async-start(bf16[128,8,384]{2,1,0:T(8,128)(2,1)} %bitcast.6), calls=%async_computation.1 | async-start | bytes 1572864 | tf_op jit(solution)/shard_map/all_to_all | solution.py:516
  15.3 10.2 %collective-permute-start.1 = (bf16[1,1,256,128]{3,2,1,0:T(8,128)(2,1)S(1)}, bf16[1,1,256,128]{3,2,1,0:T(8,128)(2,1)S(1)}, u32[]{:S(2)}, u32[]{:S(2)}) collective-permute-start(bf16[1,1,256,128]{3,2,1,0:T(8,128)(2,1)S(1)} %get-tuple-element.81), channel_id=1, source_target_pairs={{1,0},{2,1},{3,2},{4,3},{5,4},{6,5},{7,6},{9,8},{10,9},{11,10},{12... | collective-permute-start | bytes 196616 | tf_op jit(solution)/shard_map/ppermute | solution.py:542
  18.3 7.2 %collective-permute-start = (bf16[1,1,256,128]{3,2,1,0:T(8,128)(2,1)S(1)}, bf16[1,1,256,128]{3,2,1,0:T(8,128)(2,1)S(1)}, u32[]{:S(2)}, u32[]{:S(2)}) collective-permute-start(bf16[1,1,256,128]{3,2,1,0:T(8,128)(2,1)S(1)} %get-tuple-element.82), channel_id=1, source_target_pairs={{0,1},{1,2},{2,3},{3,4},{4,5},{5,6},{6,7},{8,9},{9,10},{10,11},{11... | collective-permute-start | bytes 196616 | tf_op jit(solution)/shard_map/ppermute | solution.py:541
  30.8 18.1 %copy-start.3 = (bf16[3,3,128,128]{3,2,1,0:T(8,128)(2,1)S(1)}, bf16[3,3,128,128]{3,2,1,0:T(8,128)(2,1)}, u32[]{:S(2)}) copy-start(bf16[3,3,128,128]{3,2,1,0:T(8,128)(2,1)} %weight_ref.1) | copy-start | bytes 884740
  44.0 21.5 %all-to-all-start.2 = ((bf16[128,8,384]{2,1,0:T(8,128)(2,1)}), bf16[128,8,384]{2,1,0:T(8,128)(2,1)S(1)}, u32[]{:S(2)}, u32[]{:S(2)}) async-start(bf16[128,8,384]{2,1,0:T(8,128)(2,1)} %bitcast.8), calls=%async_computation.2 | async-start | bytes 1572864 | tf_op jit(solution)/shard_map/all_to_all | solution.py:516
  58.6 2.0 %copy-start = (bf16[1,64,256,128]{3,2,1,0:T(8,128)(2,1)}, bf16[1,64,256,128]{3,2,1,0:T(8,128)(2,1)S(1)}, u32[]{:S(2)}) copy-start(bf16[1,64,256,128]{3,2,1,0:T(8,128)(2,1)S(1)} %shard_map.157.conv_hbm) | copy-start | bytes 12582916
  75.7 24.5 %copy-start.1 = (bf16[256,512]{1,0:T(8,128)(2,1)S(1)}, bf16[256,512]{1,0:T(8,128)(2,1)}, u32[]{:S(2)}) copy-start(bf16[256,512]{1,0:T(8,128)(2,1)} %wp_ref.1) | copy-start | bytes 786436
  75.7 24.5 %copy-start.2 = (bf16[256,256]{1,0:T(8,128)(2,1)S(1)}, bf16[256,256]{1,0:T(8,128)(2,1)}, u32[]{:S(2)}) copy-start(bf16[256,256]{1,0:T(8,128)(2,1)} %we_ref.1) | copy-start | bytes 393220

commit v3 on v2

--- a/solution.py
+++ b/solution.py
@@ -24,6 +24,7 @@
 RET = 16
 BACK = DEVICES * RET
 FEW = 640
+LIKELY = 544
 GROUP = 64
 ALIGN = 16
 SPAN = 1024
@@ -99,20 +100,32 @@
     ret_ref[...] = jnp.broadcast_to(ret, (8, LEAVES)).astype(I32)
     rounds = jnp.max(turn) + 1.0
     lane = iota((LEAVES, LANES), 1)
-    extra = jnp.where(lane == 0, b_col + 1.0, jnp.where(lane == 1, rounds, 0.0)).astype(BF16)
+    turn_col = columns(slot.astype(F32), LEAVES) - a_col * CAP
+    held = jnp.where(turn_col == lane.astype(F32), b_col + 1.0, 0.0).astype(BF16)
+    tags = dot(onehot_rows(0, DEVICES, a_row.astype(I32)), held)
+    tags = jnp.where(iota((DEVICES, LANES), 1) == CAP, rounds, tags).astype(BF16)
+    in_a = jnp.where(a_col == lane.astype(F32), 1.0, 0.0).astype(BF16)
+    counts = dot(onehot_rows(0, DEVICES, b_row.astype(I32)), in_a).astype(BF16)
+    line = iota((SLOTS, LANES), 0)
+    spread = jnp.where(line // CAP == iota((SLOTS, LANES), 1), 1.0, 0.0).astype(BF16)
+    extra = jnp.where(line % CAP == 0, dot(spread, tags), jnp.where(line % CAP == 1, dot(spread, counts), 0.0))
+    out_ref[:, D:] = extra.astype(BF16)
     moves[2].wait()
     for first in range(0, SLOTS, SPAN):
         hot = onehot_rows(first, SPAN, slot)
         out_ref[first : first + SPAN, :D] = dot(hot, leaves_ref[...]).astype(BF16)
-        out_ref[first : first + SPAN, D:] = dot(hot, extra).astype(BF16)
-
-
-def tags_of(x_ref):
-    tags = x_ref[:, D:]
-    picks = jnp.where(iota((8, LANES), 0) == iota((8, LANES), 1), 1.0, 0.0).astype(BF16)
-    rows = dot_nt(picks, tags)
-    spread = jnp.where(iota((LANES, LANES), 0) == 0, 1.0, 0.0).astype(BF16)
-    return rows[0:1, :], dot(tags, spread), jnp.max(rows[1:2, :])
+
+
+def message_rows(x_ref, which):
+    pick = iota((DEVICES, SLOTS), 0) * CAP + which == iota((DEVICES, SLOTS), 1)
+    return dot(jnp.where(pick, 1.0, 0.0).astype(BF16), x_ref[:, D:])
+
+
+def interleave(by_turn):
+    spread = jnp.where(iota((DEVICES, SLOTS), 1) // CAP == iota((DEVICES, SLOTS), 0), 1.0, 0.0).astype(BF16)
+    wide = dot(by_turn.astype(BF16), spread)
+    own = iota((CAP, SLOTS), 1) % CAP == iota((CAP, SLOTS), 0)
+    return jnp.sum(jnp.where(own, wide, 0.0), axis=0, keepdims=True)
 
 
 def ranks_of(tag_row, tag_col):
@@ -149,7 +162,7 @@
     return x + x * jnp.tanh(inner)
 
 
-def layer(layer_index, count, tile, x_ref, live, weights, y_ref, q_ref, k_ref, v_ref, live_ref):
+def layer(layer_index, count, tile, asked, x_ref, live, weights, y_ref, q_ref, k_ref, v_ref, live_ref):
     wq, wk, wv, wo, wu, wd, gain_one, gain_two = weights
     one = gain_one[layer_index : layer_index + 1, :]
     two = gain_two[layer_index : layer_index + 1, :]
@@ -178,8 +191,11 @@
 
     lax.fori_loop(0, count // tile, project, 0)
 
+    tile = asked[1]
+    low = iota((tile, LANES), 1) < HEAD_DIM
+
     def attend(step, _):
-        rows = pl.ds(pl.multiple_of(step * tile, tile), tile)
+        rows = pl.ds(pl.multiple_of(step * tile, ALIGN), tile)
 
         def scored(head):
             lanes = slice(head // 2 * LANES, (head // 2 + 1) * LANES)
@@ -210,48 +226,23 @@
         y_ref[rows, :] = (hidden + 0.5 * dot(up, wd[...])).astype(BF16)
         return 0
 
-    lax.fori_loop(0, count // tile, attend, 0)
+    lax.fori_loop(0, asked[0] // tile, attend, 0)
 
 
 def layer_a_kernel(x_ref, *refs):
     sources, out_ref, weights, sems, (y_ref, *rest) = refs[:8], refs[8], refs[9:17], refs[17], refs[18:]
     moves = fetch(0, sources, weights, sems)
-    tag_row, tag_col, rounds = tags_of(x_ref)
+    tags = message_rows(x_ref, 0)
+    picks = jnp.where(iota((CAP, LANES), 0) == iota((CAP, LANES), 1), 1.0, 0.0).astype(BF16)
+    tag_row = interleave(dot_nt(picks, tags.astype(BF16)))
+    tag_col = columns(tag_row, SLOTS)
     slot = (tag_row - 1.0) * CAP + ranks_of(tag_row, tag_col)
     slot = jnp.where(tag_row > 0.0, slot, -1.0).astype(I32)
-    lane = iota((SLOTS, LANES), 1)
-    home = iota((SLOTS, LANES), 0) // CAP + 1
-    extra = jnp.where(lane == 0, home.astype(F32), 0.0).astype(BF16)
     for move in moves:
         move.wait()
     live = jnp.where(tag_col > 0.0, 1.0, 0.0)
-    layer(0, SLOTS, 2 * TILE, x_ref, live, weights, y_ref, *rest)
-    for first in range(0, SLOTS, SPAN):
-        hot = onehot_rows(first, SPAN, slot)
-        out_ref[first : first + SPAN, :D] = dot(hot, y_ref[...]).astype(BF16)
-        tail = jnp.where(lane[:SPAN] == 1, rounds, dot(hot, extra))
-        out_ref[first : first + SPAN, D:] = tail.astype(BF16)
-
-
-def finish_b(count, tile, place, x_ref, packed_ref, weights, moves, refs):
-    out_ref, y_ref, slot_ref, *rest = refs
-    packed_ref[:count, :] = dot(onehot_rows(0, count, place), x_ref[...]).astype(BF16)
-    tag_row, tag_col, _ = tags_of(packed_ref.at[:count, :])
-    rank = ranks_of(tag_row, tag_col)
-    turn = jnp.floor(rank * (1.0 / RET))
-    slot = (tag_row - 1.0) * RET + (rank - turn * RET) + turn * BACK
-    slot = jnp.where(tag_row > 0.0, slot, -1.0).astype(I32)
-    slot_ref[:, :count] = jnp.broadcast_to(slot, (8, count))
-    if count < SLOTS:
-        slot_ref[:, count:] = jnp.full((8, SLOTS - count), -1, I32)
-        y_ref[count:, :] = jnp.zeros((SLOTS - count, D), BF16)
-    live = jnp.where(iota((count, LANES), 0) == 0, 1.0, jnp.where(tag_col > 0.0, 1.0, 0.0))
-    for move in moves:
-        move.wait()
-    layer(1, count, tile, packed_ref, live, weights, y_ref, *rest)
-    for first in range(0, BACK, SPAN):
-        hot = onehot_rows(first, SPAN, slot)
-        out_ref[first : first + SPAN, :] = dot(hot, y_ref[:count, :]).astype(BF16)
+    layer(0, SLOTS, 2 * TILE, (SLOTS, 2 * TILE), x_ref, live, weights, y_ref, *rest)
+    out_ref[...] = dot(onehot_rows(0, SLOTS, slot), y_ref[...]).astype(BF16)
 
 
 def before(flags):
@@ -267,45 +258,100 @@
     return jnp.concatenate(rows, axis=1)
 
 
-def layer_b_kernel(x_ref, *refs):
-    sources, (out_ref, y_ref, slot_ref, rounds_ref) = refs[:8], refs[8:12]
-    weights, sems, (packed_ref, *rest) = refs[12:20], refs[20], refs[21:]
+def plan_kernel(x_ref, place_ref, slot_ref, live_ref, total_ref, rounds_ref):
+    tags = message_rows(x_ref, 0)
+    rounds_ref[0] = jnp.max(jnp.where(iota((DEVICES, LANES), 1) == CAP, tags, 0.0)).astype(I32)
+    counts = message_rows(x_ref, 1)
+    lower = jnp.where(iota((DEVICES, DEVICES), 0) >= iota((DEVICES, DEVICES), 1), 1.0, 0.0).astype(BF16)
+    running = dot(lower, counts.astype(BF16))
+    homes = []
+    for turn in range(CAP):
+        home = jnp.sum(jnp.where(running <= turn, 1.0, 0.0), axis=0, keepdims=True)
+        homes.append(jnp.where(home < DEVICES, home + 1.0, 0.0))
+    tag = interleave(jnp.concatenate(homes, axis=0))
+    live = jnp.where(tag > 0.0, 1.0, 0.0)
+    total_ref[0] = jnp.sum(live).astype(I32)
+    place = jnp.where(tag > 0.0, before(live), -1.0).astype(I32)
+    place_ref[...] = jnp.broadcast_to(place, (8, SLOTS))
+    tag_col = dot(onehot_rows(0, SLOTS, place), columns(tag, SLOTS).astype(BF16))
+    tag_row = tag_col.T[0:1, :]
+    rank = ranks_of(tag_row, tag_col)
+    turn = jnp.floor(rank * (1.0 / RET))
+    slot = (tag_row - 1.0) * RET + (rank - turn * RET) + turn * BACK
+    slot = jnp.where(tag_row > 0.0, slot, -1.0).astype(I32)
+    slot_ref[...] = jnp.broadcast_to(slot, (8, SLOTS))
+    flag = jnp.where(iota((SLOTS, LANES), 0) == 0, 1.0, jnp.where(tag_col > 0.0, 1.0, 0.0))
+    live_ref[...] = flag.astype(BF16)
+
+
+def call_plan(rows):
+    smem = pl.BlockSpec(memory_space=pltpu.SMEM)
+    return pl.pallas_call(
+        plan_kernel,
+        out_shape=[
+            jax.ShapeDtypeStruct((8, SLOTS), I32),
+            jax.ShapeDtypeStruct((8, SLOTS), I32),
+            jax.ShapeDtypeStruct((SLOTS, LANES), BF16),
+            jax.ShapeDtypeStruct((1,), I32),
+            jax.ShapeDtypeStruct((1,), I32),
+        ],
+        in_specs=[VMEM],
+        out_specs=[VMEM, VMEM, VMEM, smem, smem],
+        compiler_params=pltpu.CompilerParams(vmem_limit_bytes=24 * 2**20),
+        cost_estimate=pl.CostEstimate(flops=2 * 10**9, bytes_accessed=2**20, transcendentals=0),
+    )(rows)
+
+
+def finish_b(count, tile, asked, x_ref, place_ref, slot_ref, flag_ref, packed_ref, weights, moves, refs):
+    out_ref, y_ref, *rest = refs
+    packed_ref[:count, :] = dot(onehot_rows(0, count, place_ref[0:1, :]), x_ref[...]).astype(BF16)
+    if count < SLOTS:
+        y_ref[asked[0] :, :] = jnp.zeros((SLOTS - asked[0], D), BF16)
+    for move in moves:
+        move.wait()
+    layer(1, count, tile, asked, packed_ref, flag_ref[:count, :], weights, y_ref, *rest)
+    for first in range(0, BACK, SPAN):
+        hot = onehot_rows(first, SPAN, slot_ref[0:1, :count])
+        out_ref[first : first + SPAN, :] = dot(hot, y_ref[:count, :]).astype(BF16)
+
+
+def layer_b_kernel(x_ref, place_ref, slot_ref, flag_ref, total_ref, *refs):
+    sources, (out_ref, y_ref, held_ref) = refs[:8], refs[8:11]
+    weights, sems, (packed_ref, *rest) = refs[11:19], refs[19], refs[20:]
     moves = fetch(1, sources, weights, sems)
-    tag_row, _, rounds = tags_of(x_ref)
-    rounds_ref[0] = rounds.astype(I32)
-    live = jnp.where(tag_row > 0.0, 1.0, 0.0)
-    total = jnp.sum(live)
-    place = jnp.where(tag_row > 0.0, before(live), -1.0).astype(I32)
-    outs = (out_ref, y_ref, slot_ref, *rest)
-
-    @pl.when(total <= FEW)
+    held_ref[...] = jnp.zeros(held_ref.shape, BF16)
+    given = (x_ref, place_ref, slot_ref, flag_ref, packed_ref, weights, moves, (out_ref, y_ref, *rest))
+
+    @pl.when(total_ref[0] <= LIKELY)
     def _():
-        finish_b(FEW, FEW // 2, place, x_ref, packed_ref, weights, moves, outs)
-
-    @pl.when(total > FEW)
+        finish_b(FEW, FEW // 2, (LIKELY, LIKELY // 2), *given)
+
+    @pl.when(total_ref[0] > LIKELY)
     def _():
-        finish_b(SLOTS, TILE, place, x_ref, packed_ref, weights, moves, outs)
-
-
-def call_layer(kernel, out_shape, x, weights):
+        finish_b(SLOTS, TILE, (SLOTS, TILE), *given)
+
+
+def call_layer(kernel, out_shape, rows, plan, weights):
     kernel_weights = [pltpu.VMEM(weight.shape[1:], BF16) for weight in weights[:6]]
     kernel_weights += [pltpu.VMEM(gain.shape, F32) for gain in weights[6:]]
     scratch = [
-        pltpu.VMEM((SLOTS, D) if len(out_shape) == 1 else (SLOTS, WIDE), BF16),
+        pltpu.VMEM((SLOTS, D), BF16),
         pltpu.VMEM((SLOTS, D), BF16),
         pltpu.VMEM((SLOTS, D), BF16),
         pltpu.VMEM((HEADS, SLOTS, D), BF16),
         pltpu.VMEM((SLOTS, LANES), BF16),
     ]
+    smem = pl.BlockSpec(memory_space=pltpu.SMEM)
     return pl.pallas_call(
         kernel,
         out_shape=out_shape,
-        in_specs=[VMEM] + [pl.BlockSpec(memory_space=pltpu.HBM)] * 8,
-        out_specs=[pl.BlockSpec(memory_space=pltpu.SMEM if shape.shape == (1,) else pltpu.VMEM) for shape in out_shape],
+        in_specs=[VMEM] + [smem if part.shape == (1,) else VMEM for part in plan]
+        + [pl.BlockSpec(memory_space=pltpu.HBM)] * 8,
+        out_specs=[VMEM] * len(out_shape),
         scratch_shapes=kernel_weights + [pltpu.SemaphoreType.DMA((8,))] + scratch,
         compiler_params=pltpu.CompilerParams(vmem_limit_bytes=24 * 2**20),
         cost_estimate=pl.CostEstimate(flops=6 * 10**9, bytes_accessed=4 * 2**20, transcendentals=5 * 2**20),
-    )(x, *map(kept, weights))
+    )(rows, *plan, *map(kept, weights))
 
 
 def resend_kernel(turn_ref, y_ref, slot_ref, out_ref):
@@ -335,7 +381,7 @@
     out_ref[...] = (held_ref[...].astype(F32) + rows).astype(BF16)
 
 
-def order_kernel(ret_ref, parent_ref, want_ref, block_ref, start_ref):
+def order_kernel(ret_ref, parent_ref, want_ref, again_ref, block_ref, start_ref):
     parent = parent_ref[...].astype(F32)
     ret = ret_ref[0:1, :].astype(F32)
     p_col = columns(parent, LEAVES)
@@ -352,6 +398,7 @@
         hit = place == fiota((LANES, LEAVES), 0) + first
         want = jnp.sum(jnp.where(hit, ret, 0.0), axis=1, keepdims=True)
         want_ref[rows, :] = jnp.broadcast_to(want, (LANES, LANES)).astype(I32)
+        again_ref[rows, :] = want_ref[rows, :]
         block = 2.0 * jnp.sum(jnp.where(hit, parent, 0.0), axis=1, keepdims=True)
         block_ref[rows, :] = jnp.broadcast_to(block, (LANES, LANES))
     block_ref[LEAVES:, :] = jnp.full((GROUP, LANES), -8.0, F32)
@@ -364,11 +411,12 @@
         order_kernel,
         out_shape=[
             jax.ShapeDtypeStruct((LEAVES, LANES), I32),
+            jax.ShapeDtypeStruct((LEAVES, LANES), I32),
             jax.ShapeDtypeStruct((LEAVES + GROUP, LANES), F32),
             jax.ShapeDtypeStruct((8, LANES), I32),
         ],
         in_specs=[VMEM, VMEM],
-        out_specs=[VMEM, VMEM, VMEM],
+        out_specs=[VMEM] * 4,
         compiler_params=pltpu.CompilerParams(vmem_limit_bytes=24 * 2**20),
         cost_estimate=pl.CostEstimate(flops=10**9, bytes_accessed=2**20, transcendentals=0),
     )(ret, parent)
@@ -426,7 +474,7 @@
     )(*[kept(coarse)] * 3, head, foot, weight)
 
 
-def field_kernel(start_ref, conv_hbm, back_ref, held_ref, want_ref, block_ref, we_ref, wp_ref, out_ref, pix_ref, conv_ref, sems):
+def field_kernel(start_ref, conv_hbm, held_hbm, rounds_ref, back_ref, want_ref, block_ref, we_ref, wp_ref, out_ref, pix_ref, conv_ref, held_ref, sems, held_sem):
     step = pl.program_id(0)
 
     def move(part):
@@ -437,6 +485,14 @@
     def _():
         for part in range(conv_ref.shape[0] // BAND):
             move(part).start()
+        held_ref[...] = jnp.zeros(held_ref.shape, BF16)
+
+        @pl.when(rounds_ref[0] > 1)
+        def _():
+            load = pltpu.make_async_copy(held_hbm, held_ref, held_sem.at[0])
+            load.start()
+            load.wait()
+
         leaf = (gathered(want_ref[...], back_ref) + held_ref[...].astype(F32)).astype(BF16)
         expanded = gelu_twice(dot(leaf, we_ref[...])).astype(BF16)
         pixels = (0.5 * dot(expanded, wp_ref[...])).astype(BF16)
@@ -479,9 +535,8 @@
             store(pair, lax.fori_loop(0, (end - first + GROUP - 1) // GROUP, more, held_rows(pair)))
 
 
-def call_field(starts, conv, back, held, want, block, w_expand, w_pixels):
+def call_field(starts, conv, held, rounds, back, want, block, w_expand, w_pixels):
     rows, cols, channels = conv.shape[1:]
-    whole = lambda *shape: pl.BlockSpec(shape, lambda i, s: (0,) * len(shape))
     strip = pl.BlockSpec((1, BAND, cols, channels), lambda i, s: (0, i, 0, 0))
     return pl.pallas_call(
         field_kernel,
@@ -490,24 +545,23 @@
             grid=(rows // BAND,),
             in_specs=[
                 pl.BlockSpec(memory_space=pltpu.HBM),
-                whole(BACK, D),
-                whole(LEAVES, D),
-                whole(LEAVES, LANES),
-                whole(LEAVES + GROUP, LANES),
-                whole(D, D),
-                whole(D, 4 * LANES),
-            ],
+                pl.BlockSpec(memory_space=pltpu.HBM),
+                pl.BlockSpec(memory_space=pltpu.SMEM),
+            ]
+            + [VMEM] * 5,
             out_specs=strip,
             scratch_shapes=[
                 pltpu.VMEM((2, LEAVES + GROUP, D), BF16),
                 pltpu.VMEM(conv.shape[1:], BF16),
+                pltpu.VMEM((LEAVES, D), BF16),
                 pltpu.SemaphoreType.DMA((rows // BAND,)),
+                pltpu.SemaphoreType.DMA((1,)),
             ],
         ),
         out_shape=jax.ShapeDtypeStruct(conv.shape, BF16),
         compiler_params=pltpu.CompilerParams(vmem_limit_bytes=32 * 2**20),
         cost_estimate=pl.CostEstimate(flops=2 * 10**9, bytes_accessed=10 * 2**20, transcendentals=2**17),
-    )(starts, kept(conv), back, held, want, block, w_expand, w_pixels)
+    )(starts, kept(conv), kept(held), rounds, back, want, block, w_expand, w_pixels)
 
 
 def exchange(rows, capacity):
@@ -555,23 +609,20 @@
         cost_estimate=pl.CostEstimate(flops=10**9, bytes_accessed=2**20, transcendentals=0),
     )(*map(kept, (leaves, window_a.reshape(1, LEAVES), window_b.reshape(1, LEAVES))))
     rows_a = exchange(sent, CAP)
-    want, block, starts = call_order(ret, parent.reshape(1, LEAVES))
+    want, again_want, block, starts = call_order(ret, parent.reshape(1, LEAVES))
     rows_a, want, head, foot = lax.optimization_barrier((rows_a, want, head, foot))
-    (sent_b,) = call_layer(
-        layer_a_kernel, [jax.ShapeDtypeStruct((SLOTS, WIDE), BF16)], rows_a, weights
-    )
+    (sent_b,) = call_layer(layer_a_kernel, [jax.ShapeDtypeStruct((SLOTS, D), BF16)], rows_a, (), weights)
     rows_b = exchange(sent_b, CAP)
-    conv = call_conv(coarse, head, foot, conv_weight)
-    rows_b, conv = lax.optimization_barrier((rows_b, conv))
-    home, y, slot, rounds = call_layer(
+    place, slot, flag, live, rounds = call_plan(rows_a)
+    home, y, held = call_layer(
         layer_b_kernel,
         [
             jax.ShapeDtypeStruct((BACK, D), BF16),
             jax.ShapeDtypeStruct((SLOTS, D), BF16),
-            jax.ShapeDtypeStruct((8, SLOTS), I32),
-            jax.ShapeDtypeStruct((1,), I32),
+            jax.ShapeDtypeStruct((LEAVES, D), BF16),
         ],
         rows_b,
+        (place, slot, flag, live),
         weights,
     )
     back = exchange(home, RET)
@@ -595,11 +646,13 @@
             out_shape=jax.ShapeDtypeStruct((LEAVES, D), BF16),
             in_specs=[smem, VMEM, VMEM, VMEM],
             out_specs=VMEM,
-        )(index, exchange(part, RET), want, held)
+        )(index, exchange(part, RET), again_want, held)
         return turn + 1, held
 
-    _, held = lax.while_loop(more, again, (jnp.asarray(1, I32), jnp.zeros((LEAVES, D), BF16)))
-    return call_field(starts, conv, back, held, want, block, w_expand, w_pixels)
+    _, held = lax.while_loop(more, again, (jnp.asarray(1, I32), held))
+    head, held = lax.optimization_barrier((head, held))
+    conv = call_conv(coarse, head, foot, conv_weight)
+    return call_field(starts, conv, held, rounds, back, want, block, w_expand, w_pixels)
 
 
 def solution(mesh):

time: 108 us -> 103 us (0.954)
  blocking collectives: 23.9 us -> 0 us
  waiting for transfers between devices: 13.7 us -> 28.4 us
  starting transfers between devices: 22 us -> 26.6 us
    all_to_all x1 -> x0, blocking collectives: 23.9 us -> none  [exchange(): lax.all_to_all(blocks, ('tile', 'intra'), split_axis=0, concat_axis=0, ti...]
    all_to_all x2 -> x3, waiting for transfers between devices: 10.3 us -> 24.3 us  [exchange(): lax.all_to_all(blocks, ('tile', 'intra'), split_axis=0, concat_axis=0, ti...]
    all_to_all x2 -> x3, starting transfers between devices: 16.5 us -> 21 us  [exchange(): lax.all_to_all(blocks, ('tile', 'intra'), split_axis=0, concat_axis=0, ti...]
    pallas_call x2 -> x3, Pallas kernels: 22.5 us -> 24.2 us  [the longest x2 21.9 us: call_layer(): pl.pallas_call(kernel, out_shape=out_shape, in_specs=[VMEM] + [smem if pa...]
  transfers between devices with their start and end apart: 4 -> 5, of which waited for: 3 -> 4; matrix products, arithmetic and copies ran while one was open for 1% -> 1% of each run, Pallas kernels for 10% -> 12%
where the time goes in v3:
time: 103 us
  Pallas kernels  44 us (43%)
  waiting for transfers between devices  28.4 us (28%)
  starting transfers between devices  26.6 us (26%)
  local copies, waits for them, and re-layouts  2.84 us (3%)
    all_to_all x3, waiting for transfers between devices, exchange(): lax.all_to_all(blocks, ('tile', 'intra'), split_axis=0, concat_axis=0, ti...  24.3 us
    pallas_call x2, Pallas kernels, call_layer(): pl.pallas_call(kernel, out_shape=out_shape, in_specs=[VMEM] + [smem if pa...  21.9 us
    all_to_all x3, starting transfers between devices, exchange(): lax.all_to_all(blocks, ('tile', 'intra'), split_axis=0, concat_axis=0, ti...  21 us
    pallas_call x1, Pallas kernels, call_conv(): pl.pallas_call(functools.partial(conv_kernel, count), grid=(count,), out_...  9.62 us
    pallas_call x1, Pallas kernels, call_field(): pl.pallas_call(field_kernel, grid_spec=pltpu.PrefetchScalarGridSpec(num_s...  6.5 us
    ppermute x1, waiting for transfers between devices, shards(): lax.ppermute(coarse[:, :1], 'intra', [(i + 1, i) for i in range(count - 1)])  4.02 us
    pallas_call x1, Pallas kernels, shards(): pl.pallas_call(send_kernel, out_shape=[jax.ShapeDtypeStruct((SLOTS, WIDE)...  3.03 us
    ppermute x1, starting transfers between devices, shards(): lax.ppermute(coarse[:, :1], 'intra', [(i + 1, i) for i in range(count - 1)])  2.98 us
  transfers between devices with their start and end apart: 5, of which 4 were waited for; matrix products, arithmetic and copies ran while one was open for 1% of the time, Pallas kernels for 12%

profile of v3, /device:TPU:1, one launch (start us, length us, event | category | flops | bytes accessed | tf_op | source)
XLA Modules:
  0.0 102.8 jit_solution(14611521715081805518)
XLA Ops:
  0.0 3.0 %shard_map.154 = (bf16[1024,384]{1,0:T(8,128)(2,1)}, s32[8,512]{1,0:T(8,128)S(1)}) custom-call(bf16[512,256]{1,0:T(8,128)(2,1)} %leaves_hbm.1, s32[1,512]{1,0:T(1,128)} %bitcast.26, s32[1,512]{1,0:T(1,128)} %bitcast.27), custom_call_target="tpu_custom_call" | custom-call | flops 1000000000 | bytes 1048576 | tf_op jit(solution)/shard_map/pallas_call | solution.py:597
  3.0 11.5 %all-to-all-start.1 = ((bf16[128,8,384]{2,1,0:T(8,128)(2,1)}), bf16[128,8,384]{2,1,0:T(8,128)(2,1)S(1)}, u32[]{:S(2)}, u32[]{:S(2)}) async-start(bf16[128,8,384]{2,1,0:T(8,128)(2,1)} %bitcast.6), calls=%async_computation.1 | async-start | bytes 1572864 | tf_op jit(solution)/shard_map/all_to_all | solution.py:570
  14.5 0.9 fusion
  15.4 3.0 %collective-permute-start.1 = (bf16[1,1,256,128]{3,2,1,0:T(8,128)(2,1)S(1)}, bf16[1,1,256,128]{3,2,1,0:T(8,128)(2,1)S(1)}, u32[]{:S(2)}, u32[]{:S(2)}) collective-permute-start(bf16[1,1,256,128]{3,2,1,0:T(8,128)(2,1)S(1)} %get-tuple-element.91), channel_id=1, source_target_pairs={{1,0},{2,1},{3,2},{4,3},{5,4},{6,5},{7,6},{9,8},{10,9},{11,10},{12... | collective-permute-start | bytes 196616 | tf_op jit(solution)/shard_map/ppermute | solution.py:596
  18.4 2.6 %collective-permute-start = (bf16[1,1,256,128]{3,2,1,0:T(8,128)(2,1)S(1)}, bf16[1,1,256,128]{3,2,1,0:T(8,128)(2,1)S(1)}, u32[]{:S(2)}, u32[]{:S(2)}) collective-permute-start(bf16[1,1,256,128]{3,2,1,0:T(8,128)(2,1)S(1)} %get-tuple-element.92), channel_id=1, source_target_pairs={{0,1},{1,2},{2,3},{3,4},{4,5},{5,6},{6,7},{8,9},{9,10},{10,11},{11... | collective-permute-start | bytes 196616 | tf_op jit(solution)/shard_map/ppermute | solution.py:595
  21.0 0.0 copy-done.4
  21.0 0.6 shard_map.155
  21.5 4.0 %collective-permute-done.1.foot_ref = bf16[1,1,256,128]{3,2,1,0:T(8,128)(2,1)S(1)} collective-permute-done((bf16[1,1,256,128]{3,2,1,0:T(8,128)(2,1)S(1)}, bf16[1,1,256,128]{3,2,1,0:T(8,128)(2,1)S(1)}, u32[]{:S(2)}, u32[]{:S(2)}) %collective-permute-start.1) | collective-permute-done | bytes 65568 | tf_op jit(solution)/shard_map/ppermute | solution.py:596
  25.6 0.0 collective-permute-done.head_ref
  25.6 5.4 %all-to-all-done.1 = bf16[128,8,384]{2,1,0:T(8,128)(2,1)S(1)} async-done(((bf16[128,8,384]{2,1,0:T(8,128)(2,1)}), bf16[128,8,384]{2,1,0:T(8,128)(2,1)S(1)}, u32[]{:S(2)}, u32[]{:S(2)}) %all-to-all-start.1) | async-done | bytes 786464 | tf_op jit(solution)/shard_map/all_to_all | solution.py:570
  30.9 12.6 %shard_map.156 = bf16[1024,256]{1,0:T(8,128)(2,1)} custom-call(bf16[1024,384]{1,0:T(8,128)(2,1)S(1)} %bitcast.20, bf16[2,256,256]{2,1,0:T(8,128)(2,1)} %refs_0_.3, bf16[2,256,256]{2,1,0:T(8,128)(2,1)} %refs_1_.3, bf16[2,256,256]{2,1,0:T(8,128)(2,1)} %refs_2_.3, bf16[2,256,256]{2,1,0:T(8,128)(2,1)} %refs_3_.3, bf16[2,256,1024]{2,1,0:T(8,128)(2,1)} %refs_4_.3, ...), custom_call_target="tpu_custom_call" | custom-call | flops 6000000000 | bytes 4194304 | tf_op jit(solution)/shard_map/pallas_call | solution.py:345
  43.5 5.0 %all-to-all-start.2 = ((bf16[128,8,256]{2,1,0:T(8,128)(2,1)}), bf16[128,8,256]{2,1,0:T(8,128)(2,1)S(1)}, u32[]{:S(2)}, u32[]{:S(2)}) async-start(bf16[128,8,256]{2,1,0:T(8,128)(2,1)} %bitcast.8), calls=%async_computation.2 | async-start | bytes 1048576 | tf_op jit(solution)/shard_map/all_to_all | solution.py:570
  48.4 2.4 %shard_map.157 = (s32[8,1024]{1,0:T(8,128)S(1)}, s32[8,1024]{1,0:T(8,128)S(1)}, bf16[1024,128]{1,0:T(8,128)(2,1)S(1)}, s32[1]{0:T(128)}, s32[1]{0:T(128)}) custom-call(bf16[1024,384]{1,0:T(8,128)(2,1)S(1)} %bitcast.21), custom_call_target="tpu_custom_call" | custom-call | flops 2000000000 | bytes 1048576 | tf_op jit(solution)/shard_map/pallas_call | solution.py:289
  50.8 11.4 %all-to-all-done.2 = bf16[128,8,256]{2,1,0:T(8,128)(2,1)S(1)} async-done(((bf16[128,8,256]{2,1,0:T(8,128)(2,1)}), bf16[128,8,256]{2,1,0:T(8,128)(2,1)S(1)}, u32[]{:S(2)}, u32[]{:S(2)}) %all-to-all-start.2) | async-done | bytes 524320 | tf_op jit(solution)/shard_map/all_to_all | solution.py:570
  62.2 9.3 %shard_map.158 = (bf16[2048,256]{1,0:T(8,128)(2,1)}, bf16[1024,256]{1,0:T(8,128)(2,1)S(1)}, bf16[512,256]{1,0:T(8,128)(2,1)S(1)}) custom-call(bf16[1024,256]{1,0:T(8,128)(2,1)S(1)} %bitcast.22, s32[8,1024]{1,0:T(8,128)S(1)} %get-tuple-element.64.place_ref, s32[8,1024]{1,0:T(8,128)S(1)} %get-tuple-element.135.slot_ref, ...), custom_call_target="tpu_custom_call" | custom-call | flops 6000000000 | bytes 4194304 | tf_op jit(solution)/shard_map/pallas_call | solution.py:345
  71.5 0.0 copy-start.3
  71.5 0.7 while.10
  72.2 4.6 %all-to-all-start.3 = ((bf16[128,16,256]{2,1,0:T(8,128)(2,1)}), bf16[128,16,256]{2,1,0:T(8,128)(2,1)S(1)}, u32[]{:S(2)}, u32[]{:S(2)}) async-start(bf16[128,16,256]{2,1,0:T(8,128)(2,1)} %bitcast.11), calls=%async_computation.3 | async-start | bytes 2097152 | tf_op jit(solution)/shard_map/all_to_all | solution.py:570
  76.9 0.0 copy-start.1
  76.9 0.0 copy-start.2
  76.9 9.6 %shard_map.159.conv_hbm = bf16[1,64,256,128]{3,2,1,0:T(8,128)(2,1)S(1)} custom-call(bf16[1,64,256,128]{3,2,1,0:T(8,128)(2,1)} %below_ref.1, bf16[1,64,256,128]{3,2,1,0:T(8,128)(2,1)} %below_ref.1, bf16[1,64,256,128]{3,2,1,0:T(8,128)(2,1)} %below_ref.1, bf16[1,1,256,128]{3,2,1,0:T(8,128)(2,1)S(1)} %collective-permute-done.head_ref, ...), custom_call_target="tpu_custom_call" | custom-call | flops 6000000000 | bytes 8388608 | tf_op jit(solution)/shard_map/pallas_call | solution.py:458
  86.6 1.9 %copy-done = bf16[1,64,256,128]{3,2,1,0:T(8,128)(2,1)} copy-done((bf16[1,64,256,128]{3,2,1,0:T(8,128)(2,1)}, bf16[1,64,256,128]{3,2,1,0:T(8,128)(2,1)S(1)}, u32[]{:S(2)}) %copy-start) | copy-done | bytes 4194328
  88.5 7.6 %all-to-all-done.3 = bf16[128,16,256]{2,1,0:T(8,128)(2,1)S(1)} async-done(((bf16[128,16,256]{2,1,0:T(8,128)(2,1)}), bf16[128,16,256]{2,1,0:T(8,128)(2,1)S(1)}, u32[]{:S(2)}, u32[]{:S(2)}) %all-to-all-start.3) | async-done | bytes 1048608 | tf_op jit(solution)/shard_map/all_to_all | solution.py:570
  96.1 6.5 %shard_map.160 = bf16[1,64,256,128]{3,2,1,0:T(8,128)(2,1)} custom-call(s32[8,128]{1,0:T(8,128)S(1)} %get-tuple-element.59.start_ref, bf16[1,64,256,128]{3,2,1,0:T(8,128)(2,1)} %copy-done, bf16[512,256]{1,0:T(8,128)(2,1)} %copy-done.6, s32[1]{0:T(128)} %get-tuple-element.69.rounds_ref, bf16[2048,256]{1,0:T(8,128)(2,1)S(1)} %bitcast.19, ...), custom_call_target="tpu_custom_call" | custom-call | flops 2000000000 | bytes 10485760 | tf_op jit(solution)/shard_map/pallas_call | solution.py:541
  (7 shorter events, 0.0 us)
Async XLA Ops:
  0.0 21.0 %copy-start.4 = (s32[512]{0:T(512)S(1)}, s32[512]{0:T(512)}, u32[]{:S(2)}) copy-start(s32[512]{0:T(512)} %param.21) | copy-start | bytes 6148
  3.0 27.9 %all-to-all-start.1 = ((bf16[128,8,384]{2,1,0:T(8,128)(2,1)}), bf16[128,8,384]{2,1,0:T(8,128)(2,1)S(1)}, u32[]{:S(2)}, u32[]{:S(2)}) async-start(bf16[128,8,384]{2,1,0:T(8,128)(2,1)} %bitcast.6), calls=%async_computation.1 | async-start | bytes 1572864 | tf_op jit(solution)/shard_map/all_to_all | solution.py:570
  15.4 10.2 %collective-permute-start.1 = (bf16[1,1,256,128]{3,2,1,0:T(8,128)(2,1)S(1)}, bf16[1,1,256,128]{3,2,1,0:T(8,128)(2,1)S(1)}, u32[]{:S(2)}, u32[]{:S(2)}) collective-permute-start(bf16[1,1,256,128]{3,2,1,0:T(8,128)(2,1)S(1)} %get-tuple-element.91), channel_id=1, source_target_pairs={{1,0},{2,1},{3,2},{4,3},{5,4},{6,5},{7,6},{9,8},{10,9},{11,10},{12... | collective-permute-start | bytes 196616 | tf_op jit(solution)/shard_map/ppermute | solution.py:596
  18.4 7.2 %collective-permute-start = (bf16[1,1,256,128]{3,2,1,0:T(8,128)(2,1)S(1)}, bf16[1,1,256,128]{3,2,1,0:T(8,128)(2,1)S(1)}, u32[]{:S(2)}, u32[]{:S(2)}) collective-permute-start(bf16[1,1,256,128]{3,2,1,0:T(8,128)(2,1)S(1)} %get-tuple-element.92), channel_id=1, source_target_pairs={{0,1},{1,2},{2,3},{3,4},{4,5},{5,6},{6,7},{8,9},{9,10},{10,11},{11... | collective-permute-start | bytes 196616 | tf_op jit(solution)/shard_map/ppermute | solution.py:595
  43.5 18.7 %all-to-all-start.2 = ((bf16[128,8,256]{2,1,0:T(8,128)(2,1)}), bf16[128,8,256]{2,1,0:T(8,128)(2,1)S(1)}, u32[]{:S(2)}, u32[]{:S(2)}) async-start(bf16[128,8,256]{2,1,0:T(8,128)(2,1)} %bitcast.8), calls=%async_computation.2 | async-start | bytes 1048576 | tf_op jit(solution)/shard_map/all_to_all | solution.py:570
  71.5 5.4 %copy-start.3 = (bf16[3,3,128,128]{3,2,1,0:T(8,128)(2,1)S(1)}, bf16[3,3,128,128]{3,2,1,0:T(8,128)(2,1)}, u32[]{:S(2)}) copy-start(bf16[3,3,128,128]{3,2,1,0:T(8,128)(2,1)} %weight_ref.1) | copy-start | bytes 884740
  72.2 14.3 %copy-start.6 = (bf16[512,256]{1,0:T(8,128)(2,1)}, bf16[512,256]{1,0:T(8,128)(2,1)S(1)}, u32[]{:S(2)}) copy-start(bf16[512,256]{1,0:T(8,128)(2,1)S(1)} %get-tuple-element.75.held_hbm) | copy-start | bytes 786436
  72.2 23.9 %all-to-all-start.3 = ((bf16[128,16,256]{2,1,0:T(8,128)(2,1)}), bf16[128,16,256]{2,1,0:T(8,128)(2,1)S(1)}, u32[]{:S(2)}, u32[]{:S(2)}) async-start(bf16[128,16,256]{2,1,0:T(8,128)(2,1)} %bitcast.11), calls=%async_computation.3 | async-start | bytes 2097152 | tf_op jit(solution)/shard_map/all_to_all | solution.py:570
  76.9 19.2 %copy-start.1 = (bf16[256,512]{1,0:T(8,128)(2,1)S(1)}, bf16[256,512]{1,0:T(8,128)(2,1)}, u32[]{:S(2)}) copy-start(bf16[256,512]{1,0:T(8,128)(2,1)} %wp_ref.1) | copy-start | bytes 786436
  76.9 19.2 %copy-start.2 = (bf16[256,256]{1,0:T(8,128)(2,1)S(1)}, bf16[256,256]{1,0:T(8,128)(2,1)}, u32[]{:S(2)}) copy-start(bf16[256,256]{1,0:T(8,128)(2,1)} %we_ref.1) | copy-start | bytes 393220
  86.5 1.9 %copy-start = (bf16[1,64,256,128]{3,2,1,0:T(8,128)(2,1)}, bf16[1,64,256,128]{3,2,1,0:T(8,128)(2,1)S(1)}, u32[]{:S(2)}) copy-start(bf16[1,64,256,128]{3,2,1,0:T(8,128)(2,1)S(1)} %shard_map.159.conv_hbm) | copy-start | bytes 12582916

commit v4 on v3

--- a/solution.py
+++ b/solution.py
@@ -27,7 +27,7 @@
 LIKELY = 544
 GROUP = 64
 ALIGN = 16
-SPAN = 1024
+CHUNK = 512
 BAND = 16
 TILE = 256
 FF = 1024
@@ -67,7 +67,7 @@
     return jnp.where(want == targets, 1.0, 0.0).astype(BF16)
 
 
-def send_kernel(leaves_hbm, wa_hbm, wb_hbm, out_ref, ret_ref, leaves_ref, wa_ref, wb_ref, sems):
+def send_kernel(leaves_hbm, wa_hbm, wb_hbm, out_hbm, ret_ref, out_ref, leaves_ref, wa_ref, wb_ref, sems, left):
     moves = [
         pltpu.make_async_copy(source, target, sems.at[index])
         for index, (source, target) in enumerate(((wa_hbm, wa_ref), (wb_hbm, wb_ref), (leaves_hbm, leaves_ref)))
@@ -111,9 +111,7 @@
     extra = jnp.where(line % CAP == 0, dot(spread, tags), jnp.where(line % CAP == 1, dot(spread, counts), 0.0))
     out_ref[:, D:] = extra.astype(BF16)
     moves[2].wait()
-    for first in range(0, SLOTS, SPAN):
-        hot = onehot_rows(first, SPAN, slot)
-        out_ref[first : first + SPAN, :D] = dot(hot, leaves_ref[...]).astype(BF16)
+    scatter_out(slot, leaves_ref[...], out_ref, out_hbm, left)
 
 
 def message_rows(x_ref, which):
@@ -148,6 +146,17 @@
     return (values * lax.rsqrt(mean_sq + EPSILON) * gain).astype(BF16)
 
 
+def scatter_out(slot, rows, held_ref, out_hbm, sems):
+    moves = []
+    for part in range(held_ref.shape[0] // CHUNK):
+        lines = pl.ds(part * CHUNK, CHUNK)
+        held_ref[lines, :D] = dot(onehot_rows(part * CHUNK, CHUNK, slot), rows).astype(BF16)
+        moves.append(pltpu.make_async_copy(held_ref.at[lines], out_hbm.at[lines], sems.at[part]))
+        moves[-1].start()
+    for move in moves:
+        move.wait()
+
+
 def fetch(layer_index, sources, targets, sems):
     moves = []
     for index, (source, target) in enumerate(zip(sources, targets)):
@@ -162,7 +171,7 @@
     return x + x * jnp.tanh(inner)
 
 
-def layer(layer_index, count, tile, asked, x_ref, live, weights, y_ref, q_ref, k_ref, v_ref, live_ref):
+def layer(layer_index, count, tile, asked, unroll, x_ref, live, weights, y_ref, q_ref, k_ref, v_ref, live_ref):
     wq, wk, wv, wo, wu, wd, gain_one, gain_two = weights
     one = gain_one[layer_index : layer_index + 1, :]
     two = gain_two[layer_index : layer_index + 1, :]
@@ -195,7 +204,7 @@
     low = iota((tile, LANES), 1) < HEAD_DIM
 
     def attend(step, _):
-        rows = pl.ds(pl.multiple_of(step * tile, ALIGN), tile)
+        rows = slice(step * tile, (step + 1) * tile) if unroll else pl.ds(pl.multiple_of(step * tile, ALIGN), tile)
 
         def scored(head):
             lanes = slice(head // 2 * LANES, (head // 2 + 1) * LANES)
@@ -226,11 +235,16 @@
         y_ref[rows, :] = (hidden + 0.5 * dot(up, wd[...])).astype(BF16)
         return 0
 
-    lax.fori_loop(0, asked[0] // tile, attend, 0)
+    if unroll:
+        for step in range(asked[0] // tile):
+            attend(step, 0)
+    else:
+        lax.fori_loop(0, asked[0] // tile, attend, 0)
 
 
 def layer_a_kernel(x_ref, *refs):
-    sources, out_ref, weights, sems, (y_ref, *rest) = refs[:8], refs[8], refs[9:17], refs[17], refs[18:]
+    sources, out_hbm, weights = refs[:8], refs[8], refs[9:17]
+    sems, left, out_ref, y_ref, *rest = refs[17:]
     moves = fetch(0, sources, weights, sems)
     tags = message_rows(x_ref, 0)
     picks = jnp.where(iota((CAP, LANES), 0) == iota((CAP, LANES), 1), 1.0, 0.0).astype(BF16)
@@ -241,8 +255,8 @@
     for move in moves:
         move.wait()
     live = jnp.where(tag_col > 0.0, 1.0, 0.0)
-    layer(0, SLOTS, 2 * TILE, (SLOTS, 2 * TILE), x_ref, live, weights, y_ref, *rest)
-    out_ref[...] = dot(onehot_rows(0, SLOTS, slot), y_ref[...]).astype(BF16)
+    layer(0, SLOTS, 2 * TILE, (SLOTS, 2 * TILE), True, x_ref, live, weights, y_ref, *rest)
+    scatter_out(slot, y_ref[...], out_ref, out_hbm, left)
 
 
 def before(flags):
@@ -303,24 +317,21 @@
 
 
 def finish_b(count, tile, asked, x_ref, place_ref, slot_ref, flag_ref, packed_ref, weights, moves, refs):
-    out_ref, y_ref, *rest = refs
+    out_hbm, left, out_ref, y_ref, *rest = refs
     packed_ref[:count, :] = dot(onehot_rows(0, count, place_ref[0:1, :]), x_ref[...]).astype(BF16)
     if count < SLOTS:
         y_ref[asked[0] :, :] = jnp.zeros((SLOTS - asked[0], D), BF16)
     for move in moves:
         move.wait()
-    layer(1, count, tile, asked, packed_ref, flag_ref[:count, :], weights, y_ref, *rest)
-    for first in range(0, BACK, SPAN):
-        hot = onehot_rows(first, SPAN, slot_ref[0:1, :count])
-        out_ref[first : first + SPAN, :] = dot(hot, y_ref[:count, :]).astype(BF16)
+    layer(1, count, tile, asked, count < SLOTS, packed_ref, flag_ref[:count, :], weights, y_ref, *rest)
+    scatter_out(slot_ref[0:1, :count], y_ref[:count, :], out_ref, out_hbm, left)
 
 
 def layer_b_kernel(x_ref, place_ref, slot_ref, flag_ref, total_ref, *refs):
-    sources, (out_ref, y_ref, held_ref) = refs[:8], refs[8:11]
-    weights, sems, (packed_ref, *rest) = refs[11:19], refs[19], refs[20:]
+    sources, (out_hbm, y_ref) = refs[:8], refs[8:10]
+    weights, (sems, left, out_ref, packed_ref, *rest) = refs[10:18], refs[18:]
     moves = fetch(1, sources, weights, sems)
-    held_ref[...] = jnp.zeros(held_ref.shape, BF16)
-    given = (x_ref, place_ref, slot_ref, flag_ref, packed_ref, weights, moves, (out_ref, y_ref, *rest))
+    given = (x_ref, place_ref, slot_ref, flag_ref, packed_ref, weights, moves, (out_hbm, left, out_ref, y_ref, *rest))
 
     @pl.when(total_ref[0] <= LIKELY)
     def _():
@@ -347,8 +358,11 @@
         out_shape=out_shape,
         in_specs=[VMEM] + [smem if part.shape == (1,) else VMEM for part in plan]
         + [pl.BlockSpec(memory_space=pltpu.HBM)] * 8,
-        out_specs=[VMEM] * len(out_shape),
-        scratch_shapes=kernel_weights + [pltpu.SemaphoreType.DMA((8,))] + scratch,
+        out_specs=[pl.BlockSpec(memory_space=pltpu.HBM)] + [VMEM] * (len(out_shape) - 1),
+        scratch_shapes=kernel_weights
+        + [pltpu.SemaphoreType.DMA((8,)), pltpu.SemaphoreType.DMA((out_shape[0].shape[0] // CHUNK,))]
+        + [pltpu.VMEM(out_shape[0].shape, BF16)]
+        + scratch,
         compiler_params=pltpu.CompilerParams(vmem_limit_bytes=24 * 2**20),
         cost_estimate=pl.CostEstimate(flops=6 * 10**9, bytes_accessed=4 * 2**20, transcendentals=5 * 2**20),
     )(rows, *plan, *map(kept, weights))
@@ -356,9 +370,9 @@
 
 def resend_kernel(turn_ref, y_ref, slot_ref, out_ref):
     slot = slot_ref[0:1, :] - turn_ref[0] * BACK
-    for first in range(0, BACK, TILE):
-        hot = onehot_rows(first, TILE, slot)
-        out_ref[first : first + TILE, :] = dot(hot, y_ref[...]).astype(BF16)
+    for first in range(0, BACK, CHUNK):
+        hot = onehot_rows(first, CHUNK, slot)
+        out_ref[first : first + CHUNK, :] = dot(hot, y_ref[...]).astype(BF16)
 
 
 def gathered(want, back_ref):
@@ -381,7 +395,8 @@
     out_ref[...] = (held_ref[...].astype(F32) + rows).astype(BF16)
 
 
-def order_kernel(ret_ref, parent_ref, want_ref, again_ref, block_ref, start_ref):
+def order_kernel(ret_ref, parent_ref, want_ref, again_ref, block_ref, start_ref, held_ref):
+    held_ref[...] = jnp.zeros(held_ref.shape, BF16)
     parent = parent_ref[...].astype(F32)
     ret = ret_ref[0:1, :].astype(F32)
     p_col = columns(parent, LEAVES)
@@ -414,9 +429,10 @@
             jax.ShapeDtypeStruct((LEAVES, LANES), I32),
             jax.ShapeDtypeStruct((LEAVES + GROUP, LANES), F32),
             jax.ShapeDtypeStruct((8, LANES), I32),
+            jax.ShapeDtypeStruct((LEAVES, D), BF16),
         ],
         in_specs=[VMEM, VMEM],
-        out_specs=[VMEM] * 4,
+        out_specs=[VMEM] * 5,
         compiler_params=pltpu.CompilerParams(vmem_limit_bytes=24 * 2**20),
         cost_estimate=pl.CostEstimate(flops=10**9, bytes_accessed=2**20, transcendentals=0),
     )(ret, parent)
@@ -598,28 +614,29 @@
         send_kernel,
         out_shape=[jax.ShapeDtypeStruct((SLOTS, WIDE), BF16), jax.ShapeDtypeStruct((8, LEAVES), I32)],
         in_specs=[pl.BlockSpec(memory_space=pltpu.HBM)] * 3,
-        out_specs=[VMEM] * 2,
+        out_specs=[pl.BlockSpec(memory_space=pltpu.HBM), VMEM],
         scratch_shapes=[
+            pltpu.VMEM((SLOTS, WIDE), BF16),
             pltpu.VMEM((LEAVES, D), BF16),
             pltpu.VMEM((1, LEAVES), I32),
             pltpu.VMEM((1, LEAVES), I32),
             pltpu.SemaphoreType.DMA((3,)),
+            pltpu.SemaphoreType.DMA((SLOTS // CHUNK,)),
         ],
         compiler_params=pltpu.CompilerParams(vmem_limit_bytes=24 * 2**20),
         cost_estimate=pl.CostEstimate(flops=10**9, bytes_accessed=2**20, transcendentals=0),
     )(*map(kept, (leaves, window_a.reshape(1, LEAVES), window_b.reshape(1, LEAVES))))
     rows_a = exchange(sent, CAP)
-    want, again_want, block, starts = call_order(ret, parent.reshape(1, LEAVES))
+    want, again_want, block, starts, held = call_order(ret, parent.reshape(1, LEAVES))
     rows_a, want, head, foot = lax.optimization_barrier((rows_a, want, head, foot))
     (sent_b,) = call_layer(layer_a_kernel, [jax.ShapeDtypeStruct((SLOTS, D), BF16)], rows_a, (), weights)
     rows_b = exchange(sent_b, CAP)
     place, slot, flag, live, rounds = call_plan(rows_a)
-    home, y, held = call_layer(
+    home, y = call_layer(
         layer_b_kernel,
         [
             jax.ShapeDtypeStruct((BACK, D), BF16),
             jax.ShapeDtypeStruct((SLOTS, D), BF16),
-            jax.ShapeDtypeStruct((LEAVES, D), BF16),
         ],
         rows_b,
         (place, slot, flag, live),

time: 103 us -> 103 us (level)
  Pallas kernels: 44 us -> 42.7 us
    pallas_call x2, Pallas kernels: 21.9 us -> 20.6 us  [call_layer(): pl.pallas_call(kernel, out_shape=out_shape, in_specs=[VMEM] + [smem if pa...]
where the time goes in v4:
time: 103 us; the launch traced here: 102 us
  Pallas kernels  42.7 us (41%)
  waiting for transfers between devices  28.4 us (28%)
  starting transfers between devices  26.8 us (26%)
  local copies, waits for them, and re-layouts  2.84 us (3%)
    all_to_all x3, waiting for transfers between devices, exchange(): lax.all_to_all(blocks, ('tile', 'intra'), split_axis=0, concat_axis=0, ti...  24.3 us
    all_to_all x3, starting transfers between devices, exchange(): lax.all_to_all(blocks, ('tile', 'intra'), split_axis=0, concat_axis=0, ti...  21.2 us
    pallas_call x2, Pallas kernels, call_layer(): pl.pallas_call(kernel, out_shape=out_shape, in_specs=[VMEM] + [smem if pa...  20.6 us
    pallas_call x1, Pallas kernels, call_conv(): pl.pallas_call(functools.partial(conv_kernel, count), grid=(count,), out_...  9.62 us
    pallas_call x1, Pallas kernels, call_field(): pl.pallas_call(field_kernel, grid_spec=pltpu.PrefetchScalarGridSpec(num_s...  6.5 us
    ppermute x1, waiting for transfers between devices, shards(): lax.ppermute(coarse[:, :1], 'intra', [(i + 1, i) for i in range(count - 1)])  4.02 us
    pallas_call x1, Pallas kernels, shards(): pl.pallas_call(send_kernel, out_shape=[jax.ShapeDtypeStruct((SLOTS, WIDE)...  3.01 us
    ppermute x1, starting transfers between devices, shards(): lax.ppermute(coarse[:, :1], 'intra', [(i + 1, i) for i in range(count - 1)])  2.98 us
  transfers between devices with their start and end apart: 5, of which 4 were waited for; matrix products, arithmetic and copies ran while one was open for 1% of the time, Pallas kernels for 12%

profile of v4, /device:TPU:1, one launch (start us, length us, event | category | flops | bytes accessed | tf_op | source)
XLA Modules:
  0.0 101.9 jit_solution(16027940282632529962)
XLA Ops:
  0.0 3.0 %shard_map.154 = (bf16[1024,384]{1,0:T(8,128)(2,1)}, s32[8,512]{1,0:T(8,128)S(1)}) custom-call(bf16[512,256]{1,0:T(8,128)(2,1)} %leaves_hbm.1, s32[1,512]{1,0:T(1,128)} %bitcast.26, s32[1,512]{1,0:T(1,128)} %bitcast.27), custom_call_target="tpu_custom_call" | custom-call | flops 1000000000 | bytes 1048576 | tf_op jit(solution)/shard_map/pallas_call | solution.py:613
  3.0 11.5 %all-to-all-start.1 = ((bf16[128,8,384]{2,1,0:T(8,128)(2,1)}), bf16[128,8,384]{2,1,0:T(8,128)(2,1)S(1)}, u32[]{:S(2)}, u32[]{:S(2)}) async-start(bf16[128,8,384]{2,1,0:T(8,128)(2,1)} %bitcast.6), calls=%async_computation.1 | async-start | bytes 1572864 | tf_op jit(solution)/shard_map/all_to_all | solution.py:586
  14.5 0.9 fusion
  15.4 3.0 %collective-permute-start.1 = (bf16[1,1,256,128]{3,2,1,0:T(8,128)(2,1)S(1)}, bf16[1,1,256,128]{3,2,1,0:T(8,128)(2,1)S(1)}, u32[]{:S(2)}, u32[]{:S(2)}) collective-permute-start(bf16[1,1,256,128]{3,2,1,0:T(8,128)(2,1)S(1)} %get-tuple-element.91), channel_id=1, source_target_pairs={{1,0},{2,1},{3,2},{4,3},{5,4},{6,5},{7,6},{9,8},{10,9},{11,10},{12... | collective-permute-start | bytes 196616 | tf_op jit(solution)/shard_map/ppermute | solution.py:612
  18.4 2.6 %collective-permute-start = (bf16[1,1,256,128]{3,2,1,0:T(8,128)(2,1)S(1)}, bf16[1,1,256,128]{3,2,1,0:T(8,128)(2,1)S(1)}, u32[]{:S(2)}, u32[]{:S(2)}) collective-permute-start(bf16[1,1,256,128]{3,2,1,0:T(8,128)(2,1)S(1)} %get-tuple-element.92), channel_id=1, source_target_pairs={{0,1},{1,2},{2,3},{3,4},{4,5},{5,6},{6,7},{8,9},{9,10},{10,11},{11... | collective-permute-start | bytes 196616 | tf_op jit(solution)/shard_map/ppermute | solution.py:611
  21.0 0.6 shard_map.155
  21.6 4.0 %collective-permute-done.1.foot_ref = bf16[1,1,256,128]{3,2,1,0:T(8,128)(2,1)S(1)} collective-permute-done((bf16[1,1,256,128]{3,2,1,0:T(8,128)(2,1)S(1)}, bf16[1,1,256,128]{3,2,1,0:T(8,128)(2,1)S(1)}, u32[]{:S(2)}, u32[]{:S(2)}) %collective-permute-start.1) | collective-permute-done | bytes 65568 | tf_op jit(solution)/shard_map/ppermute | solution.py:612
  25.6 0.0 collective-permute-done.head_ref
  25.6 5.4 %all-to-all-done.1 = bf16[128,8,384]{2,1,0:T(8,128)(2,1)S(1)} async-done(((bf16[128,8,384]{2,1,0:T(8,128)(2,1)}), bf16[128,8,384]{2,1,0:T(8,128)(2,1)S(1)}, u32[]{:S(2)}, u32[]{:S(2)}) %all-to-all-start.1) | async-done | bytes 786464 | tf_op jit(solution)/shard_map/all_to_all | solution.py:586
  30.9 11.7 %shard_map.157 = bf16[1024,256]{1,0:T(8,128)(2,1)} custom-call(bf16[1024,384]{1,0:T(8,128)(2,1)S(1)} %bitcast.20, bf16[2,256,256]{2,1,0:T(8,128)(2,1)} %refs_0_.3, bf16[2,256,256]{2,1,0:T(8,128)(2,1)} %refs_1_.3, bf16[2,256,256]{2,1,0:T(8,128)(2,1)} %refs_2_.3, bf16[2,256,256]{2,1,0:T(8,128)(2,1)} %refs_3_.3, bf16[2,256,1024]{2,1,0:T(8,128)(2,1)} %refs_4_.3, ...), custom_call_target="tpu_custom_call" | custom-call | flops 6000000000 | bytes 4194304 | tf_op jit(solution)/shard_map/pallas_call | solution.py:356
  42.7 5.1 %all-to-all-start.2 = ((bf16[128,8,256]{2,1,0:T(8,128)(2,1)}), bf16[128,8,256]{2,1,0:T(8,128)(2,1)S(1)}, u32[]{:S(2)}, u32[]{:S(2)}) async-start(bf16[128,8,256]{2,1,0:T(8,128)(2,1)} %bitcast.9), calls=%async_computation.2 | async-start | bytes 1048576 | tf_op jit(solution)/shard_map/all_to_all | solution.py:586
  47.8 2.4 %shard_map.156 = (s32[8,1024]{1,0:T(8,128)S(1)}, s32[8,1024]{1,0:T(8,128)S(1)}, bf16[1024,128]{1,0:T(8,128)(2,1)S(1)}, s32[1]{0:T(128)}, s32[1]{0:T(128)}) custom-call(bf16[1024,384]{1,0:T(8,128)(2,1)S(1)} %bitcast.21), custom_call_target="tpu_custom_call" | custom-call | flops 2000000000 | bytes 1048576 | tf_op jit(solution)/shard_map/pallas_call | solution.py:303
  50.2 11.4 %all-to-all-done.2 = bf16[128,8,256]{2,1,0:T(8,128)(2,1)S(1)} async-done(((bf16[128,8,256]{2,1,0:T(8,128)(2,1)}), bf16[128,8,256]{2,1,0:T(8,128)(2,1)S(1)}, u32[]{:S(2)}, u32[]{:S(2)}) %all-to-all-start.2) | async-done | bytes 524320 | tf_op jit(solution)/shard_map/all_to_all | solution.py:586
  61.6 8.9 %shard_map.158 = (bf16[2048,256]{1,0:T(8,128)(2,1)}, bf16[1024,256]{1,0:T(8,128)(2,1)S(1)}) custom-call(bf16[1024,256]{1,0:T(8,128)(2,1)S(1)} %bitcast.22, s32[8,1024]{1,0:T(8,128)S(1)} %get-tuple-element.66.place_ref, s32[8,1024]{1,0:T(8,128)S(1)} %get-tuple-element.135.slot_ref, bf16[1024,128]{1,0:T(8,128)(2,1)S(1)} %get-tuple-element.68.flag_ref, ...), custom_call_target="tpu_custom_call" | custom-call | flops 6000000000 | bytes 4194304 | tf_op jit(solution)/shard_map/pallas_call | solution.py:356
  70.5 0.0 copy-start.3
  70.5 0.9 while.10
  71.4 4.6 %all-to-all-start.3 = ((bf16[128,16,256]{2,1,0:T(8,128)(2,1)}), bf16[128,16,256]{2,1,0:T(8,128)(2,1)S(1)}, u32[]{:S(2)}, u32[]{:S(2)}) async-start(bf16[128,16,256]{2,1,0:T(8,128)(2,1)} %bitcast.11), calls=%async_computation.3 | async-start | bytes 2097152 | tf_op jit(solution)/shard_map/all_to_all | solution.py:586
  76.0 0.0 copy-done.3
  76.0 0.0 copy-start.1
  76.0 0.0 copy-start.2
  76.0 9.6 %shard_map.159.conv_hbm = bf16[1,64,256,128]{3,2,1,0:T(8,128)(2,1)S(1)} custom-call(bf16[1,64,256,128]{3,2,1,0:T(8,128)(2,1)} %below_ref.1, bf16[1,64,256,128]{3,2,1,0:T(8,128)(2,1)} %below_ref.1, bf16[1,64,256,128]{3,2,1,0:T(8,128)(2,1)} %below_ref.1, bf16[1,1,256,128]{3,2,1,0:T(8,128)(2,1)S(1)} %collective-permute-done.head_ref, ...), custom_call_target="tpu_custom_call" | custom-call | flops 6000000000 | bytes 8388608 | tf_op jit(solution)/shard_map/pallas_call | solution.py:474
  85.7 1.9 %copy-done = bf16[1,64,256,128]{3,2,1,0:T(8,128)(2,1)} copy-done((bf16[1,64,256,128]{3,2,1,0:T(8,128)(2,1)}, bf16[1,64,256,128]{3,2,1,0:T(8,128)(2,1)S(1)}, u32[]{:S(2)}) %copy-start) | copy-done | bytes 4194328
  87.6 7.6 %all-to-all-done.3 = bf16[128,16,256]{2,1,0:T(8,128)(2,1)S(1)} async-done(((bf16[128,16,256]{2,1,0:T(8,128)(2,1)}), bf16[128,16,256]{2,1,0:T(8,128)(2,1)S(1)}, u32[]{:S(2)}, u32[]{:S(2)}) %all-to-all-start.3) | async-done | bytes 1048608 | tf_op jit(solution)/shard_map/all_to_all | solution.py:586
  95.2 6.5 %shard_map.160 = bf16[1,64,256,128]{3,2,1,0:T(8,128)(2,1)} custom-call(s32[8,128]{1,0:T(8,128)S(1)} %get-tuple-element.59.start_ref, bf16[1,64,256,128]{3,2,1,0:T(8,128)(2,1)} %copy-done, bf16[512,256]{1,0:T(8,128)(2,1)} %copy-done.6, s32[1]{0:T(128)} %get-tuple-element.65.rounds_ref, bf16[2048,256]{1,0:T(8,128)(2,1)S(1)} %bitcast.19, ...), custom_call_target="tpu_custom_call" | custom-call | flops 2000000000 | bytes 10485760 | tf_op jit(solution)/shard_map/pallas_call | solution.py:557
  (7 shorter events, 0.0 us)
Async XLA Ops:
  0.0 21.0 %copy-start.4 = (s32[512]{0:T(512)S(1)}, s32[512]{0:T(512)}, u32[]{:S(2)}) copy-start(s32[512]{0:T(512)} %param.21) | copy-start | bytes 6148
  3.0 27.9 %all-to-all-start.1 = ((bf16[128,8,384]{2,1,0:T(8,128)(2,1)}), bf16[128,8,384]{2,1,0:T(8,128)(2,1)S(1)}, u32[]{:S(2)}, u32[]{:S(2)}) async-start(bf16[128,8,384]{2,1,0:T(8,128)(2,1)} %bitcast.6), calls=%async_computation.1 | async-start | bytes 1572864 | tf_op jit(solution)/shard_map/all_to_all | solution.py:586
  15.4 10.2 %collective-permute-start.1 = (bf16[1,1,256,128]{3,2,1,0:T(8,128)(2,1)S(1)}, bf16[1,1,256,128]{3,2,1,0:T(8,128)(2,1)S(1)}, u32[]{:S(2)}, u32[]{:S(2)}) collective-permute-start(bf16[1,1,256,128]{3,2,1,0:T(8,128)(2,1)S(1)} %get-tuple-element.91), channel_id=1, source_target_pairs={{1,0},{2,1},{3,2},{4,3},{5,4},{6,5},{7,6},{9,8},{10,9},{11,10},{12... | collective-permute-start | bytes 196616 | tf_op jit(solution)/shard_map/ppermute | solution.py:612
  18.4 7.2 %collective-permute-start = (bf16[1,1,256,128]{3,2,1,0:T(8,128)(2,1)S(1)}, bf16[1,1,256,128]{3,2,1,0:T(8,128)(2,1)S(1)}, u32[]{:S(2)}, u32[]{:S(2)}) collective-permute-start(bf16[1,1,256,128]{3,2,1,0:T(8,128)(2,1)S(1)} %get-tuple-element.92), channel_id=1, source_target_pairs={{0,1},{1,2},{2,3},{3,4},{4,5},{5,6},{6,7},{8,9},{9,10},{10,11},{11... | collective-permute-start | bytes 196616 | tf_op jit(solution)/shard_map/ppermute | solution.py:611
  42.7 18.9 %all-to-all-start.2 = ((bf16[128,8,256]{2,1,0:T(8,128)(2,1)}), bf16[128,8,256]{2,1,0:T(8,128)(2,1)S(1)}, u32[]{:S(2)}, u32[]{:S(2)}) async-start(bf16[128,8,256]{2,1,0:T(8,128)(2,1)} %bitcast.9), calls=%async_computation.2 | async-start | bytes 1048576 | tf_op jit(solution)/shard_map/all_to_all | solution.py:586
  70.5 5.6 %copy-start.3 = (bf16[3,3,128,128]{3,2,1,0:T(8,128)(2,1)S(1)}, bf16[3,3,128,128]{3,2,1,0:T(8,128)(2,1)}, u32[]{:S(2)}) copy-start(bf16[3,3,128,128]{3,2,1,0:T(8,128)(2,1)} %weight_ref.1) | copy-start | bytes 884740
  71.4 14.3 %copy-start.6 = (bf16[512,256]{1,0:T(8,128)(2,1)}, bf16[512,256]{1,0:T(8,128)(2,1)S(1)}, u32[]{:S(2)}) copy-start(bf16[512,256]{1,0:T(8,128)(2,1)S(1)} %get-tuple-element.75.held_hbm) | copy-start | bytes 786436
  71.4 23.8 %all-to-all-start.3 = ((bf16[128,16,256]{2,1,0:T(8,128)(2,1)}), bf16[128,16,256]{2,1,0:T(8,128)(2,1)S(1)}, u32[]{:S(2)}, u32[]{:S(2)}) async-start(bf16[128,16,256]{2,1,0:T(8,128)(2,1)} %bitcast.11), calls=%async_computation.3 | async-start | bytes 2097152 | tf_op jit(solution)/shard_map/all_to_all | solution.py:586
  76.0 19.2 %copy-start.1 = (bf16[256,512]{1,0:T(8,128)(2,1)S(1)}, bf16[256,512]{1,0:T(8,128)(2,1)}, u32[]{:S(2)}) copy-start(bf16[256,512]{1,0:T(8,128)(2,1)} %wp_ref.1) | copy-start | bytes 786436
  76.0 19.2 %copy-start.2 = (bf16[256,256]{1,0:T(8,128)(2,1)S(1)}, bf16[256,256]{1,0:T(8,128)(2,1)}, u32[]{:S(2)}) copy-start(bf16[256,256]{1,0:T(8,128)(2,1)} %we_ref.1) | copy-start | bytes 393220
  85.7 1.9 %copy-start = (bf16[1,64,256,128]{3,2,1,0:T(8,128)(2,1)}, bf16[1,64,256,128]{3,2,1,0:T(8,128)(2,1)S(1)}, u32[]{:S(2)}) copy-start(bf16[1,64,256,128]{3,2,1,0:T(8,128)(2,1)S(1)} %shard_map.159.conv_hbm) | copy-start | bytes 12582916

commit v5 on v4

--- a/solution.py
+++ b/solution.py
@@ -181,7 +181,7 @@
     first = dot(rms(x_ref[:ALIGN, :D].astype(F32), one), wk[...])[0:1, :].astype(BF16)
 
     def project(step, _):
-        rows = pl.ds(pl.multiple_of(step * tile, tile), tile)
+        rows = pl.ds(step * tile if unroll and count == SLOTS else pl.multiple_of(step * tile, tile), tile)
         normed = rms(x_ref[rows, :D].astype(F32), one)
         flag = live_ref[rows, :]
         q_ref[rows, :] = (dot(normed, wq[...]) * (HEAD_DIM**-0.5 * LOG2E)).astype(BF16)
@@ -198,7 +198,11 @@
             v_ref[2 * pair + 1, rows, other] = flag
         return 0
 
-    lax.fori_loop(0, count // tile, project, 0)
+    if unroll and count == SLOTS:
+        for step in range(count // tile):
+            project(step, 0)
+    else:
+        lax.fori_loop(0, count // tile, project, 0)
 
     tile = asked[1]
     low = iota((tile, LANES), 1) < HEAD_DIM
@@ -335,7 +339,7 @@
 
     @pl.when(total_ref[0] <= LIKELY)
     def _():
-        finish_b(FEW, FEW // 2, (LIKELY, LIKELY // 2), *given)
+        finish_b(FEW, FEW // 2, (LIKELY, LIKELY), *given)
 
     @pl.when(total_ref[0] > LIKELY)
     def _():

time: 103 us -> 101 us (0.981)
  Pallas kernels: 42.7 us -> 41.6 us
    pallas_call x2, Pallas kernels: 20.6 us -> 19.6 us  [call_layer(): pl.pallas_call(kernel, out_shape=out_shape, in_specs=[VMEM] + [smem if pa...]
where the time goes in v5:
time: 101 us
  Pallas kernels  41.6 us (41%)
  waiting for transfers between devices  28.4 us (28%)
  starting transfers between devices  26.8 us (27%)
  local copies, waits for them, and re-layouts  2.84 us (3%)
    all_to_all x3, waiting for transfers between devices, exchange(): lax.all_to_all(blocks, ('tile', 'intra'), split_axis=0, concat_axis=0, ti...  24.3 us
    all_to_all x3, starting transfers between devices, exchange(): lax.all_to_all(blocks, ('tile', 'intra'), split_axis=0, concat_axis=0, ti...  21.2 us
    pallas_call x2, Pallas kernels, call_layer(): pl.pallas_call(kernel, out_shape=out_shape, in_specs=[VMEM] + [smem if pa...  19.6 us
    pallas_call x1, Pallas kernels, call_conv(): pl.pallas_call(functools.partial(conv_kernel, count), grid=(count,), out_...  9.62 us
    pallas_call x1, Pallas kernels, call_field(): pl.pallas_call(field_kernel, grid_spec=pltpu.PrefetchScalarGridSpec(num_s...  6.49 us
    ppermute x1, waiting for transfers between devices, shards(): lax.ppermute(coarse[:, :1], 'intra', [(i + 1, i) for i in range(count - 1)])  4.02 us
    pallas_call x1, Pallas kernels, shards(): pl.pallas_call(send_kernel, out_shape=[jax.ShapeDtypeStruct((SLOTS, WIDE)...  3.01 us
    ppermute x1, starting transfers between devices, shards(): lax.ppermute(coarse[:, :1], 'intra', [(i + 1, i) for i in range(count - 1)])  2.98 us
  transfers between devices with their start and end apart: 5, of which 4 were waited for; matrix products, arithmetic and copies ran while one was open for 1% of the time, Pallas kernels for 12%

profile of v5, /device:TPU:1, one launch (start us, length us, event | category | flops | bytes accessed | tf_op | source)
XLA Modules:
  0.0 100.9 jit_solution(10279028628299123923)
XLA Ops:
  0.0 3.0 %shard_map.154 = (bf16[1024,384]{1,0:T(8,128)(2,1)}, s32[8,512]{1,0:T(8,128)S(1)}) custom-call(bf16[512,256]{1,0:T(8,128)(2,1)} %leaves_hbm.1, s32[1,512]{1,0:T(1,128)} %bitcast.26, s32[1,512]{1,0:T(1,128)} %bitcast.27), custom_call_target="tpu_custom_call" | custom-call | flops 1000000000 | bytes 1048576 | tf_op jit(solution)/shard_map/pallas_call | solution.py:617
  3.0 11.5 %all-to-all-start.1 = ((bf16[128,8,384]{2,1,0:T(8,128)(2,1)}), bf16[128,8,384]{2,1,0:T(8,128)(2,1)S(1)}, u32[]{:S(2)}, u32[]{:S(2)}) async-start(bf16[128,8,384]{2,1,0:T(8,128)(2,1)} %bitcast.6), calls=%async_computation.1 | async-start | bytes 1572864 | tf_op jit(solution)/shard_map/all_to_all | solution.py:590
  14.5 0.9 fusion
  15.4 3.0 %collective-permute-start.1 = (bf16[1,1,256,128]{3,2,1,0:T(8,128)(2,1)S(1)}, bf16[1,1,256,128]{3,2,1,0:T(8,128)(2,1)S(1)}, u32[]{:S(2)}, u32[]{:S(2)}) collective-permute-start(bf16[1,1,256,128]{3,2,1,0:T(8,128)(2,1)S(1)} %get-tuple-element.91), channel_id=1, source_target_pairs={{1,0},{2,1},{3,2},{4,3},{5,4},{6,5},{7,6},{9,8},{10,9},{11,10},{12... | collective-permute-start | bytes 196616 | tf_op jit(solution)/shard_map/ppermute | solution.py:616
  18.4 2.6 %collective-permute-start = (bf16[1,1,256,128]{3,2,1,0:T(8,128)(2,1)S(1)}, bf16[1,1,256,128]{3,2,1,0:T(8,128)(2,1)S(1)}, u32[]{:S(2)}, u32[]{:S(2)}) collective-permute-start(bf16[1,1,256,128]{3,2,1,0:T(8,128)(2,1)S(1)} %get-tuple-element.92), channel_id=1, source_target_pairs={{0,1},{1,2},{2,3},{3,4},{4,5},{5,6},{6,7},{8,9},{9,10},{10,11},{11... | collective-permute-start | bytes 196616 | tf_op jit(solution)/shard_map/ppermute | solution.py:615
  21.0 0.6 shard_map.155
  21.6 4.0 %collective-permute-done.1.foot_ref = bf16[1,1,256,128]{3,2,1,0:T(8,128)(2,1)S(1)} collective-permute-done((bf16[1,1,256,128]{3,2,1,0:T(8,128)(2,1)S(1)}, bf16[1,1,256,128]{3,2,1,0:T(8,128)(2,1)S(1)}, u32[]{:S(2)}, u32[]{:S(2)}) %collective-permute-start.1) | collective-permute-done | bytes 65568 | tf_op jit(solution)/shard_map/ppermute | solution.py:616
  25.6 0.0 collective-permute-done.head_ref
  25.6 5.4 %all-to-all-done.1 = bf16[128,8,384]{2,1,0:T(8,128)(2,1)S(1)} async-done(((bf16[128,8,384]{2,1,0:T(8,128)(2,1)}), bf16[128,8,384]{2,1,0:T(8,128)(2,1)S(1)}, u32[]{:S(2)}, u32[]{:S(2)}) %all-to-all-start.1) | async-done | bytes 786464 | tf_op jit(solution)/shard_map/all_to_all | solution.py:590
  30.9 11.0 %shard_map.157 = bf16[1024,256]{1,0:T(8,128)(2,1)} custom-call(bf16[1024,384]{1,0:T(8,128)(2,1)S(1)} %bitcast.20, bf16[2,256,256]{2,1,0:T(8,128)(2,1)} %refs_0_.3, bf16[2,256,256]{2,1,0:T(8,128)(2,1)} %refs_1_.3, bf16[2,256,256]{2,1,0:T(8,128)(2,1)} %refs_2_.3, bf16[2,256,256]{2,1,0:T(8,128)(2,1)} %refs_3_.3, bf16[2,256,1024]{2,1,0:T(8,128)(2,1)} %refs_4_.3, ...), custom_call_target="tpu_custom_call" | custom-call | flops 6000000000 | bytes 4194304 | tf_op jit(solution)/shard_map/pallas_call | solution.py:360
  41.9 5.1 %all-to-all-start.2 = ((bf16[128,8,256]{2,1,0:T(8,128)(2,1)}), bf16[128,8,256]{2,1,0:T(8,128)(2,1)S(1)}, u32[]{:S(2)}, u32[]{:S(2)}) async-start(bf16[128,8,256]{2,1,0:T(8,128)(2,1)} %bitcast.9), calls=%async_computation.2 | async-start | bytes 1048576 | tf_op jit(solution)/shard_map/all_to_all | solution.py:590
  47.1 2.4 %shard_map.156 = (s32[8,1024]{1,0:T(8,128)S(1)}, s32[8,1024]{1,0:T(8,128)S(1)}, bf16[1024,128]{1,0:T(8,128)(2,1)S(1)}, s32[1]{0:T(128)}, s32[1]{0:T(128)}) custom-call(bf16[1024,384]{1,0:T(8,128)(2,1)S(1)} %bitcast.21), custom_call_target="tpu_custom_call" | custom-call | flops 2000000000 | bytes 1048576 | tf_op jit(solution)/shard_map/pallas_call | solution.py:307
  49.4 11.4 %all-to-all-done.2 = bf16[128,8,256]{2,1,0:T(8,128)(2,1)S(1)} async-done(((bf16[128,8,256]{2,1,0:T(8,128)(2,1)}), bf16[128,8,256]{2,1,0:T(8,128)(2,1)S(1)}, u32[]{:S(2)}, u32[]{:S(2)}) %all-to-all-start.2) | async-done | bytes 524320 | tf_op jit(solution)/shard_map/all_to_all | solution.py:590
  60.8 8.6 %shard_map.158 = (bf16[2048,256]{1,0:T(8,128)(2,1)}, bf16[1024,256]{1,0:T(8,128)(2,1)S(1)}) custom-call(bf16[1024,256]{1,0:T(8,128)(2,1)S(1)} %bitcast.22, s32[8,1024]{1,0:T(8,128)S(1)} %get-tuple-element.66.place_ref, s32[8,1024]{1,0:T(8,128)S(1)} %get-tuple-element.135.slot_ref, bf16[1024,128]{1,0:T(8,128)(2,1)S(1)} %get-tuple-element.68.flag_ref, ...), custom_call_target="tpu_custom_call" | custom-call | flops 6000000000 | bytes 4194304 | tf_op jit(solution)/shard_map/pallas_call | solution.py:360
  69.4 0.0 copy-start.3
  69.4 0.9 while.10
  70.3 4.6 %all-to-all-start.3 = ((bf16[128,16,256]{2,1,0:T(8,128)(2,1)}), bf16[128,16,256]{2,1,0:T(8,128)(2,1)S(1)}, u32[]{:S(2)}, u32[]{:S(2)}) async-start(bf16[128,16,256]{2,1,0:T(8,128)(2,1)} %bitcast.11), calls=%async_computation.3 | async-start | bytes 2097152 | tf_op jit(solution)/shard_map/all_to_all | solution.py:590
  75.0 0.0 copy-done.3
  75.0 0.0 copy-start.1
  75.0 0.0 copy-start.2
  75.0 9.6 %shard_map.159.conv_hbm = bf16[1,64,256,128]{3,2,1,0:T(8,128)(2,1)S(1)} custom-call(bf16[1,64,256,128]{3,2,1,0:T(8,128)(2,1)} %below_ref.1, bf16[1,64,256,128]{3,2,1,0:T(8,128)(2,1)} %below_ref.1, bf16[1,64,256,128]{3,2,1,0:T(8,128)(2,1)} %below_ref.1, bf16[1,1,256,128]{3,2,1,0:T(8,128)(2,1)S(1)} %collective-permute-done.head_ref, ...), custom_call_target="tpu_custom_call" | custom-call | flops 6000000000 | bytes 8388608 | tf_op jit(solution)/shard_map/pallas_call | solution.py:478
  84.6 1.9 %copy-done = bf16[1,64,256,128]{3,2,1,0:T(8,128)(2,1)} copy-done((bf16[1,64,256,128]{3,2,1,0:T(8,128)(2,1)}, bf16[1,64,256,128]{3,2,1,0:T(8,128)(2,1)S(1)}, u32[]{:S(2)}) %copy-start) | copy-done | bytes 4194328
  86.6 7.6 %all-to-all-done.3 = bf16[128,16,256]{2,1,0:T(8,128)(2,1)S(1)} async-done(((bf16[128,16,256]{2,1,0:T(8,128)(2,1)}), bf16[128,16,256]{2,1,0:T(8,128)(2,1)S(1)}, u32[]{:S(2)}, u32[]{:S(2)}) %all-to-all-start.3) | async-done | bytes 1048608 | tf_op jit(solution)/shard_map/all_to_all | solution.py:590
  94.2 6.5 %shard_map.160 = bf16[1,64,256,128]{3,2,1,0:T(8,128)(2,1)} custom-call(s32[8,128]{1,0:T(8,128)S(1)} %get-tuple-element.59.start_ref, bf16[1,64,256,128]{3,2,1,0:T(8,128)(2,1)} %copy-done, bf16[512,256]{1,0:T(8,128)(2,1)} %copy-done.6, s32[1]{0:T(128)} %get-tuple-element.65.rounds_ref, bf16[2048,256]{1,0:T(8,128)(2,1)S(1)} %bitcast.19, ...), custom_call_target="tpu_custom_call" | custom-call | flops 2000000000 | bytes 10485760 | tf_op jit(solution)/shard_map/pallas_call | solution.py:561
  (7 shorter events, 0.0 us)
Async XLA Ops:
  0.0 21.0 %copy-start.4 = (s32[512]{0:T(512)S(1)}, s32[512]{0:T(512)}, u32[]{:S(2)}) copy-start(s32[512]{0:T(512)} %param.21) | copy-start | bytes 6148
  3.0 27.9 %all-to-all-start.1 = ((bf16[128,8,384]{2,1,0:T(8,128)(2,1)}), bf16[128,8,384]{2,1,0:T(8,128)(2,1)S(1)}, u32[]{:S(2)}, u32[]{:S(2)}) async-start(bf16[128,8,384]{2,1,0:T(8,128)(2,1)} %bitcast.6), calls=%async_computation.1 | async-start | bytes 1572864 | tf_op jit(solution)/shard_map/all_to_all | solution.py:590
  15.4 10.2 %collective-permute-start.1 = (bf16[1,1,256,128]{3,2,1,0:T(8,128)(2,1)S(1)}, bf16[1,1,256,128]{3,2,1,0:T(8,128)(2,1)S(1)}, u32[]{:S(2)}, u32[]{:S(2)}) collective-permute-start(bf16[1,1,256,128]{3,2,1,0:T(8,128)(2,1)S(1)} %get-tuple-element.91), channel_id=1, source_target_pairs={{1,0},{2,1},{3,2},{4,3},{5,4},{6,5},{7,6},{9,8},{10,9},{11,10},{12... | collective-permute-start | bytes 196616 | tf_op jit(solution)/shard_map/ppermute | solution.py:616
  18.4 7.2 %collective-permute-start = (bf16[1,1,256,128]{3,2,1,0:T(8,128)(2,1)S(1)}, bf16[1,1,256,128]{3,2,1,0:T(8,128)(2,1)S(1)}, u32[]{:S(2)}, u32[]{:S(2)}) collective-permute-start(bf16[1,1,256,128]{3,2,1,0:T(8,128)(2,1)S(1)} %get-tuple-element.92), channel_id=1, source_target_pairs={{0,1},{1,2},{2,3},{3,4},{4,5},{5,6},{6,7},{8,9},{9,10},{10,11},{11... | collective-permute-start | bytes 196616 | tf_op jit(solution)/shard_map/ppermute | solution.py:615
  41.9 18.9 %all-to-all-start.2 = ((bf16[128,8,256]{2,1,0:T(8,128)(2,1)}), bf16[128,8,256]{2,1,0:T(8,128)(2,1)S(1)}, u32[]{:S(2)}, u32[]{:S(2)}) async-start(bf16[128,8,256]{2,1,0:T(8,128)(2,1)} %bitcast.9), calls=%async_computation.2 | async-start | bytes 1048576 | tf_op jit(solution)/shard_map/all_to_all | solution.py:590
  69.4 5.5 %copy-start.3 = (bf16[3,3,128,128]{3,2,1,0:T(8,128)(2,1)S(1)}, bf16[3,3,128,128]{3,2,1,0:T(8,128)(2,1)}, u32[]{:S(2)}) copy-start(bf16[3,3,128,128]{3,2,1,0:T(8,128)(2,1)} %weight_ref.1) | copy-start | bytes 884740
  70.3 14.3 %copy-start.6 = (bf16[512,256]{1,0:T(8,128)(2,1)}, bf16[512,256]{1,0:T(8,128)(2,1)S(1)}, u32[]{:S(2)}) copy-start(bf16[512,256]{1,0:T(8,128)(2,1)S(1)} %get-tuple-element.75.held_hbm) | copy-start | bytes 786436
  70.3 23.8 %all-to-all-start.3 = ((bf16[128,16,256]{2,1,0:T(8,128)(2,1)}), bf16[128,16,256]{2,1,0:T(8,128)(2,1)S(1)}, u32[]{:S(2)}, u32[]{:S(2)}) async-start(bf16[128,16,256]{2,1,0:T(8,128)(2,1)} %bitcast.11), calls=%async_computation.3 | async-start | bytes 2097152 | tf_op jit(solution)/shard_map/all_to_all | solution.py:590
  75.0 19.2 %copy-start.1 = (bf16[256,512]{1,0:T(8,128)(2,1)S(1)}, bf16[256,512]{1,0:T(8,128)(2,1)}, u32[]{:S(2)}) copy-start(bf16[256,512]{1,0:T(8,128)(2,1)} %wp_ref.1) | copy-start | bytes 786436
  75.0 19.2 %copy-start.2 = (bf16[256,256]{1,0:T(8,128)(2,1)S(1)}, bf16[256,256]{1,0:T(8,128)(2,1)}, u32[]{:S(2)}) copy-start(bf16[256,256]{1,0:T(8,128)(2,1)} %we_ref.1) | copy-start | bytes 393220
  84.6 1.9 %copy-start = (bf16[1,64,256,128]{3,2,1,0:T(8,128)(2,1)}, bf16[1,64,256,128]{3,2,1,0:T(8,128)(2,1)S(1)}, u32[]{:S(2)}) copy-start(bf16[1,64,256,128]{3,2,1,0:T(8,128)(2,1)S(1)} %shard_map.159.conv_hbm) | copy-start | bytes 12582916
